TPU v7x, 32 devices: a whole 2x2x4 slice. The times are simulated.
32 devices in a mesh: gx: 8 (over z, x), gy: 4 (over y, core).
Axes of the slice: x: 2, y: 2, z: 4, core: 2. Of those that a mesh axis runs over, the one named last changes fastest.
Arguments:
- adjoint_init: float32 [3, 128, 128, 128], P(None, 'gx', 'gy'), may hold values from -4 to 4
- adjoint_rhs: float32 [3, 128, 128, 128], P(None, 'gx', 'gy'), may hold values from -6 to 6
- jacobian: bfloat16 [7, 3, 3, 128, 128, 128], P(None, None, None, 'gx', 'gy'), may hold values from -1.796875 to 1.796875
- cell_diag: float32 [3, 128, 128, 128], P(None, 'gx', 'gy'), may hold values from 1.5 to 3
- perf_owner: int32 [8192, 1], P(('gx', 'gy')), may hold values from 0 to 3; in each aligned block of 256 rows (0 to 255, 256 to 511, ...) at most 64 rows name the same one
- perf_well: int32 [8192], P(('gx', 'gy')), may hold values from 0 to 31
- perf_block: int32 [8192], P(('gx', 'gy')), may hold values from 0 to 1023
- well_coupling: bfloat16 [4, 192, 8192], P(None, None, ('gx', 'gy')), may hold values from -0.4375 to 0.4375
- cell_coupling: bfloat16 [4, 192, 8192], P(None, None, ('gx', 'gy')), may hold values from -0.29882812 to 0.29882812
- well_rhs: float32 [4, 1024], P(None, ('gx', 'gy')), may hold values from -6 to 6
- well_inverse: float32 [4, 4, 1024], P(None, None, ('gx', 'gy')), may hold values from -1.5 to 1.5
Outputs:
- adjoint: float32 [3, 128, 128, 128], P(None, 'gx', 'gy')
- well_adjoint: float32 [4, 1024], P(None, ('gx', 'gy'))
Inputs may be any that keep to these rules, and one draw needn't show every extreme that they name: `perf_owner`: the owner is a gy index within the perforation's own gx row. Among the 256 perforations of one device no owner is named more than 64 times, and in some device one owner is named exactly 64 times.
All inputs are finite; a program needn't handle non-finite values.
Results may differ from a plain program's by a relative error of at most 0.0004.
Values may be sent and summed in bfloat16 or wider, within the bound.
No kernel may reach another device: no remote copies, remote signals or barrier semaphores. Data moves between devices by JAX's collectives and lax.ppermute only.
A program may use at most 128 MiB of HBM per device.

v0:
```python
import functools

import jax
import jax.numpy as jnp
from jax import lax
from jax.experimental import pallas as pl
from jax.experimental.pallas import tpu as pltpu
from jax.sharding import PartitionSpec as P

PHASES = 3
WELL_UNK = 4
BLOCK = 64
ITERS = 8
LANES = 128
F32 = jnp.float32
BF16 = jnp.bfloat16
VM = pl.BlockSpec(memory_space=pltpu.VMEM)
SM = pl.BlockSpec(memory_space=pltpu.SMEM)
PARAMS = pltpu.CompilerParams(vmem_limit_bytes=24 * 1024 * 1024)


def split_2(value):
    high = value.astype(BF16)
    return high, (value - high.astype(F32)).astype(BF16)


def edge_messages(flags, x_ref, jac_ref, col_ref, m1_ref, m2_ref, m3_ref, m4_ref):
    rows, cols = jac_ref.shape[3], jac_ref.shape[4]
    gx_odd, gy_odd = flags[0] == 1, flags[1] == 1
    x_first = [x_ref[r, 0:cols, :] for r in range(PHASES)]
    x_last = [x_ref[r, (rows - 1) * cols : rows * cols, :] for r in range(PHASES)]
    c_first = [x_ref[r, pl.ds(0, rows, stride=cols), :] for r in range(PHASES)]
    c_last = [x_ref[r, pl.ds(cols - 1, rows, stride=cols), :] for r in range(PHASES)]
    for t in range(PHASES):
        up = sum(jac_ref[1, r, t, 0].astype(F32) * x_first[r] for r in range(PHASES))
        down = sum(jac_ref[2, r, t, rows - 1].astype(F32) * x_last[r] for r in range(PHASES))
        left = sum(col_ref[0, r, t] * c_first[r] for r in range(PHASES))
        right = sum(col_ref[1, r, t] * c_last[r] for r in range(PHASES))
        m3_ref[t * cols : (t + 1) * cols, :] = jnp.where(gx_odd, up, down)
        m4_ref[t * cols : (t + 1) * cols, :] = jnp.where(gx_odd, down, up)
        m1_ref[t * rows : (t + 1) * rows, :] = jnp.where(gy_odd, left, right)
        m2_ref[t * rows : (t + 1) * rows, :] = jnp.where(gy_odd, right, left)


def well_partials(x_ref, pick_ref, well_ref, wc_ref, xs_ref, g_ref, write):
    cells = x_ref.shape[1]
    perfs = pick_ref.shape[0]
    for r in range(PHASES):
        high, low = split_2(x_ref[r])
        xs_ref[0:cells, r * LANES : (r + 1) * LANES] = high
        xs_ref[cells : 2 * cells, r * LANES : (r + 1) * LANES] = low
    g_ref[...] = jnp.dot(pick_ref[...], xs_ref[...], preferred_element_type=F32)
    width = well_ref.shape[0]
    chunk = 64
    totals = [[jnp.zeros((8, LANES), F32) for _ in range(width)] for _ in range(WELL_UNK)]
    for start in range(0, perfs, chunk):
        rows = slice(start, start + chunk)
        picked = [g_ref[rows, r * LANES : (r + 1) * LANES] for r in range(PHASES)]
        for u in range(WELL_UNK):
            lane_terms = sum(wc_ref[u, r, rows].astype(F32) * picked[r] for r in range(PHASES))
            term = jnp.sum(lane_terms, axis=1, keepdims=True)
            for h in range(width):
                spread = well_ref[h, rows, :] * term
                totals[u][h] = totals[u][h] + sum(spread[i : i + 8] for i in range(0, chunk, 8))
    for h in range(width):
        for u in range(WELL_UNK):
            write(h * WELL_UNK + u, jnp.sum(totals[u][h], axis=0, keepdims=True))


def expanded(eye, coupling_ref, u, half, out_ref):
    lane = lax.broadcasted_iota(jnp.int32, (eye.shape[0], LANES), 1)
    own_half = (lane // BLOCK) == half
    for r in range(PHASES):
        piece = coupling_ref[u, r * BLOCK : (r + 1) * BLOCK, :]
        doubled = jnp.concatenate([piece, piece], axis=0)
        turned = lax.dot_general(
            eye, doubled, (((1,), (1,)), ((), ())), preferred_element_type=F32
        )
        out_ref[u, r] = jnp.where(own_half, turned, 0.0).astype(BF16)


def first_kernel(
    flags, x_ref, jac_ref, diag_ref, block_row, block_col, well_col, wcoef, ccoef, wconst,
    inv_ref, col_ref, pick_ref, spread_ref, well_ref, wc_ref, cc_ref,
    m1_ref, m2_ref, m3_ref, m4_ref, xs_ref, g_ref,
):
    rows, cols = jac_ref.shape[3], jac_ref.shape[4]
    cells = rows * cols
    perfs = block_row.shape[1]
    inv_ref[...] = 1.0 / diag_ref[...]
    for r in range(PHASES):
        for t in range(PHASES):
            for i in range(rows):
                edge = jac_ref[3, r, t, i].astype(F32)
                col_ref[0, r, t, i : i + 1, :] = edge[0:1]
                edge = jac_ref[4, r, t, i].astype(F32)
                col_ref[1, r, t, i : i + 1, :] = edge[cols - 1 : cols]
    column = block_row[...] // 2
    cell = lax.broadcasted_iota(jnp.int32, (cells, perfs), 0)
    spread = (cell == column).astype(F32).astype(BF16)
    spread_ref[:, 0:perfs] = spread
    spread_ref[:, perfs : 2 * perfs] = spread
    block = block_col[...]
    cell = lax.broadcasted_iota(jnp.int32, (perfs, cells), 1)
    pick = (cell == block // 2).astype(F32).astype(BF16)
    pick_ref[:, 0:cells] = pick
    pick_ref[:, cells : 2 * cells] = pick
    lane = lax.broadcasted_iota(jnp.int32, (perfs, LANES), 1)
    for h in range(well_ref.shape[0]):
        well_ref[h] = (lane + h * LANES == well_col[...]).astype(F32)
    half = block % 2
    a = lax.broadcasted_iota(jnp.int32, (perfs, perfs), 0)
    b = lax.broadcasted_iota(jnp.int32, (perfs, perfs), 1)
    eye = (a == b).astype(F32).astype(BF16)
    for u in range(WELL_UNK):
        expanded(eye, wcoef, u, half, wc_ref)
        expanded(eye, ccoef, u, half, cc_ref)
    edge_messages(flags, x_ref, jac_ref, col_ref, m1_ref, m2_ref, m3_ref, m4_ref)
    base = PHASES * rows

    def write(row, value):
        m1_ref[base + row : base + row + 1, :] = value

    well_partials(x_ref, pick_ref, well_ref, wc_ref, xs_ref, g_ref, write)
    count = WELL_UNK * well_ref.shape[0]
    m1_ref[base + count :, :] = wconst[...]


def add_kernel(base, kept_ref, own_ref, got_ref, out_ref):
    out_ref[0:base, :] = kept_ref[...]
    out_ref[base:, :] = own_ref[base:, :] + got_ref[base:, :]


def inner_kernel(x_ref, jac_ref, rhs_ref, z_ref):
    rows, cols = jac_ref.shape[3], jac_ref.shape[4]
    lane = lax.broadcasted_iota(jnp.int32, (cols, LANES), 1)
    col = lax.broadcasted_iota(jnp.int32, (cols, LANES), 0)

    def row_body(i, carry):
        before, after = jnp.maximum(i - 1, 0), jnp.minimum(i + 1, rows - 1)
        has_before = (i > 0).astype(F32)
        has_after = (i < rows - 1).astype(F32)

        def load(row):
            start = pl.multiple_of(row * cols, cols)
            return [x_ref[r, pl.ds(start, cols), :] for r in range(PHASES)]

        here = load(i)

        def term(d, t, row, values):
            return sum(jac_ref[d, r, t, row].astype(F32) * values[r] for r in range(PHASES))

        start = pl.multiple_of(i * cols, cols)
        total = [term(0, t, i, here) for t in range(PHASES)]
        values = [v * has_after for v in load(after)]
        total = [total[t] + term(1, t, after, values) for t in range(PHASES)]
        values = [v * has_before for v in load(before)]
        total = [total[t] + term(2, t, before, values) for t in range(PHASES)]
        values = [jnp.where(col == 0, 0.0, v) for v in here]
        total = [
            total[t] + pltpu.roll(term(3, t, i, values), cols - 1, 0) for t in range(PHASES)
        ]
        values = [jnp.where(col == cols - 1, 0.0, v) for v in here]
        total = [total[t] + pltpu.roll(term(4, t, i, values), 1, 0) for t in range(PHASES)]
        values = [jnp.where(lane == 0, 0.0, v) for v in here]
        total = [
            total[t] + pltpu.roll(term(5, t, i, values), LANES - 1, 1) for t in range(PHASES)
        ]
        values = [jnp.where(lane == LANES - 1, 0.0, v) for v in here]
        total = [total[t] + pltpu.roll(term(6, t, i, values), 1, 1) for t in range(PHASES)]
        for t in range(PHASES):
            z_ref[t, pl.ds(start, cols), :] = rhs_ref[t, pl.ds(start, cols), :] - total[t]
        return carry

    lax.fori_loop(0, rows, row_body, 0)


def update_kernel(
    last, flags, z_ref, own, g1, g2, g3, g4, wconst, inv_ref, spread_ref, well_ref, cc_ref,
    *rest,
):
    if last:
        x_ref, adj_ref, rs_ref, c_ref = rest
    else:
        (jac_ref, col_ref, pick_ref, wc_ref, x_ref, m1_ref, m2_ref, m3_ref, m4_ref,
         rs_ref, c_ref, xs_ref, g_ref) = rest
    cells, perfs = spread_ref.shape[0], spread_ref.shape[1] // 2
    rows = (own.shape[0] - WELL_UNK * well_ref.shape[0]) // PHASES
    cols = cells // rows
    base = PHASES * rows
    width = well_ref.shape[0]
    unk = WELL_UNK * width
    terms = own[base : base + unk, :] + g2[base : base + unk, :]
    left = wconst[0:unk, :] - terms
    solved = []
    for h in range(width):
        value = 0.0
        for v in range(WELL_UNK):
            at = unk + (h * WELL_UNK + v) * WELL_UNK
            at_v = h * WELL_UNK + v
            value = value + wconst[at : at + WELL_UNK, :] * left[at_v : at_v + 1, :]
        solved.append(value)
    if last:
        for h in range(width):
            adj_ref[h] = solved[h]
    chunk = 64
    for start in range(0, perfs, chunk):
        part = slice(start, start + chunk)
        value = [0.0] * PHASES
        for u in range(WELL_UNK):
            chosen = sum(well_ref[h, part, :] * solved[h][u : u + 1, :] for h in range(width))
            factor = jnp.sum(chosen, axis=1, keepdims=True)
            for r in range(PHASES):
                value[r] = value[r] + cc_ref[u, r, part].astype(F32) * factor
        for r in range(PHASES):
            high, low = split_2(value[r])
            rs_ref[start : start + chunk, r * LANES : (r + 1) * LANES] = high
            rs_ref[perfs + start : perfs + start + chunk, r * LANES : (r + 1) * LANES] = low
    c_ref[...] = jnp.dot(spread_ref[...], rs_ref[...], preferred_element_type=F32)
    gx_odd, gy_odd = flags[0] == 1, flags[1] == 1
    gx_open, gy_open = flags[2].astype(F32), flags[3].astype(F32)
    for t in range(PHASES):
        x_ref[t] = (z_ref[t] - c_ref[:, t * LANES : (t + 1) * LANES]) * inv_ref[t]
    for t in range(PHASES):
        near, far = g3[t * cols : (t + 1) * cols, :], g4[t * cols : (t + 1) * cols, :] * gx_open
        first, final = slice(0, cols), slice((rows - 1) * cols, rows * cols)
        x_ref[t, first, :] = x_ref[t, first, :] - inv_ref[t, first, :] * jnp.where(gx_odd, near, far)
        x_ref[t, final, :] = x_ref[t, final, :] - inv_ref[t, final, :] * jnp.where(gx_odd, far, near)
        near, far = g1[t * rows : (t + 1) * rows, :], g2[t * rows : (t + 1) * rows, :] * gy_open
        first, final = pl.ds(0, rows, stride=cols), pl.ds(cols - 1, rows, stride=cols)
        x_ref[t, first, :] = x_ref[t, first, :] - inv_ref[t, first, :] * jnp.where(gy_odd, near, far)
        x_ref[t, final, :] = x_ref[t, final, :] - inv_ref[t, final, :] * jnp.where(gy_odd, far, near)
    if not last:
        edge_messages(flags, x_ref, jac_ref, col_ref, m1_ref, m2_ref, m3_ref, m4_ref)

        def write(row, value):
            m1_ref[base + row : base + row + 1, :] = value

        well_partials(x_ref, pick_ref, well_ref, wc_ref, xs_ref, g_ref, write)


def gx_swap(gx, gy, parity):
    pairs = []
    for i in range(gx):
        k = i ^ 1 if parity == 0 else ((i + 1) ^ 1) - 1
        for j in range(gy):
            pairs.append((i * gy + j, k * gy + j if 0 <= k < gx else i * gy + (j ^ 1)))
    return pairs


def gy_swap(gy, parity):
    if parity == 0:
        return [(j, j ^ 1) for j in range(gy)]
    return [(j, (((j + 1) ^ 1) - 1) % gy) for j in range(gy)]


def shape(*dims, dtype=F32):
    return jax.ShapeDtypeStruct(dims, dtype)


def body(
    adjoint_init, adjoint_rhs, jacobian, cell_diag, perf_owner, perf_well, perf_block,
    well_coupling, cell_coupling, well_rhs, well_inverse,
):
    gx, gy = lax.axis_size("gx"), lax.axis_size("gy")
    ix, iy = lax.axis_index("gx"), lax.axis_index("gy")
    phases, rows, cols, layers = adjoint_init.shape
    cells = rows * cols
    perfs = perf_well.shape[0]
    well_dev = well_rhs.shape[1]
    width = gy * well_dev // LANES
    unk = WELL_UNK * width
    base = PHASES * rows
    both = ("gx", "gy")
    flags = jnp.stack(
        [
            ix % 2,
            iy % 2,
            jnp.where(ix % 2 == 1, ix < gx - 1, ix > 0).astype(jnp.int32),
            jnp.where(iy % 2 == 1, iy < gy - 1, iy > 0).astype(jnp.int32),
        ]
    ).astype(jnp.int32)
    x = adjoint_init.reshape(phases, cells, layers)
    rhs = adjoint_rhs.reshape(phases, cells, layers)
    diag = cell_diag.reshape(phases, cells, layers)
    own_wells = jnp.concatenate([well_rhs, well_inverse.reshape(-1, well_dev)], axis=0)
    place = jnp.arange(gy * well_dev, dtype=jnp.int32) // well_dev == iy
    wide = jnp.where(place[None, :], jnp.tile(own_wells, (1, gy)), 0.0)
    wide = wide.reshape(5, WELL_UNK, width, LANES)
    wconst = jnp.transpose(wide, (2, 0, 1, 3))
    wconst = jnp.concatenate(
        [wconst[:, 0].reshape(unk, LANES), wconst[:, 1:].reshape(4 * unk, LANES)], axis=0
    )
    well_index = perf_owner[:, 0] * well_dev + perf_well

    full = base + unk
    first = pl.pallas_call(
        first_kernel,
        out_shape=(
            shape(phases, cells, layers),
            shape(2, 3, 3, rows, LANES),
            shape(perfs, 2 * cells, dtype=BF16),
            shape(cells, 2 * perfs, dtype=BF16),
            shape(width, perfs, LANES),
            shape(WELL_UNK, PHASES, perfs, LANES, dtype=BF16),
            shape(WELL_UNK, PHASES, perfs, LANES, dtype=BF16),
            shape(full + 5 * unk, LANES),
            shape(base, LANES),
            shape(PHASES * cols, LANES),
            shape(PHASES * cols, LANES),
        ),
        in_specs=[SM] + [VM] * 9,
        out_specs=(VM,) * 11,
        scratch_shapes=[
            pltpu.VMEM((2 * cells, PHASES * LANES), BF16),
            pltpu.VMEM((perfs, PHASES * LANES), F32),
        ],
        compiler_params=PARAMS,
        name="first",
    )
    inv, col_edges, pick, spread, well_hot, wc, cc, m1, m2_halo, m3, m4 = first(
        flags, x, jacobian, diag, perf_block.reshape(1, perfs), perf_block.reshape(perfs, 1),
        well_index.reshape(perfs, 1), well_coupling, cell_coupling, wconst,
    )

    def add(kept, own, got):
        return pl.pallas_call(
            functools.partial(add_kernel, base),
            out_shape=shape(*own.shape),
            in_specs=[VM] * 3,
            out_specs=VM,
            compiler_params=PARAMS,
            name="add",
        )(kept, own, got)

    inner = pl.pallas_call(
        inner_kernel,
        out_shape=shape(phases, cells, layers),
        in_specs=[VM] * 3,
        out_specs=VM,
        compiler_params=PARAMS,
        name="inner",
    )
    work = [
        pltpu.VMEM((2 * perfs, PHASES * LANES), BF16),
        pltpu.VMEM((cells, PHASES * LANES), F32),
    ]
    for sweep in range(ITERS):
        last = sweep == ITERS - 1
        g1 = lax.ppermute(m1, "gy", gy_swap(gy, 0))
        g3 = lax.ppermute(m3, both, gx_swap(gx, gy, 0))
        g4 = lax.ppermute(m4, both, gx_swap(gx, gy, 1))
        own = add(m2_halo, m1, g1)
        g2 = lax.ppermute(own, "gy", gy_swap(gy, 1))
        hop = 4
        while hop < gy:
            own = jnp.concatenate([own[:base], own[base:] + g2[base:]], axis=0)
            far = lax.ppermute(own[base:], "gy", [(j, (j + hop) % gy) for j in range(gy)])
            g2 = jnp.concatenate([g2[:base], far], axis=0)
            hop *= 2
        if sweep == 0:
            wconst = own[full:] + g2[full:]
            own, g1, g2 = own[:full], g1[:full], g2[:full]
        z = inner(x, jacobian, rhs)
        operands = (flags, z, own, g1, g2, g3, g4, wconst, inv, spread, well_hot, cc)
        if last:
            x, adj = pl.pallas_call(
                functools.partial(update_kernel, True),
                out_shape=(shape(phases, cells, layers), shape(width, WELL_UNK, LANES)),
                in_specs=[SM] + [VM] * 11,
                out_specs=(VM, VM),
                scratch_shapes=work,
                compiler_params=PARAMS,
                name="update_last",
            )(*operands)
        else:
            x, m1, m2_halo, m3, m4 = pl.pallas_call(
                functools.partial(update_kernel, False),
                out_shape=(
                    shape(phases, cells, layers),
                    shape(full, LANES),
                    shape(base, LANES),
                    shape(PHASES * cols, LANES),
                    shape(PHASES * cols, LANES),
                ),
                in_specs=[SM] + [VM] * 15,
                out_specs=(VM,) * 5,
                scratch_shapes=work
                + [
                    pltpu.VMEM((2 * cells, PHASES * LANES), BF16),
                    pltpu.VMEM((perfs, PHASES * LANES), F32),
                ],
                compiler_params=PARAMS,
                name="update",
            )(*operands, jacobian, col_edges, pick, wc)
    adj = jnp.transpose(adj, (1, 0, 2)).reshape(WELL_UNK, width * LANES)
    own_adj = lax.dynamic_slice_in_dim(adj, iy * well_dev, well_dev, axis=1)
    return x.reshape(adjoint_init.shape), own_adj


def solution(mesh):
    in_specs = (
        P(None, "gx", "gy", None),
        P(None, "gx", "gy", None),
        P(None, None, None, "gx", "gy", None),
        P(None, "gx", "gy", None),
        P(("gx", "gy"), None),
        P(("gx", "gy")),
        P(("gx", "gy")),
        P(None, None, ("gx", "gy")),
        P(None, None, ("gx", "gy")),
        P(None, ("gx", "gy")),
        P(None, None, ("gx", "gy")),
    )
    out_specs = (P(None, "gx", "gy", None), P(None, ("gx", "gy")))
    return jax.shard_map(body, mesh=mesh, in_specs=in_specs, out_specs=out_specs, check_vma=False)
```

profile of v0, /device:TPU:0, one launch (start us, length us, event | category | flops | bytes accessed | tf_op | source)
XLA Modules:
  0.0 89.5 jit_solution(12699882052329357718)
XLA Ops:
  4.0 3.3 %copy-done = bf16[7,3,3,16,32,128]{5,4,3,2,1,0:T(8,128)(2,1)S(1)} copy-done((bf16[7,3,3,16,32,128]{5,4,3,2,1,0:T(8,128)(2,1)S(1)}, bf16[7,3,3,16,32,128]{5,4,3,2,1,0:T(8,128)(2,1)}, u32[]{:S(2)}) %copy-start) | copy-done | bytes 8257560
  7.3 1.1 %copy-done.3 = f32[3,16,32,128]{3,2,1,0:T(8,128)S(1)} copy-done((f32[3,16,32,128]{3,2,1,0:T(8,128)S(1)}, f32[3,16,32,128]{3,2,1,0:T(8,128)}, u32[]{:S(2)}) %copy-start.3) | copy-done | bytes 786456
  8.5 1.1 %copy-done.5 = f32[3,16,32,128]{3,2,1,0:T(8,128)S(1)} copy-done((f32[3,16,32,128]{3,2,1,0:T(8,128)S(1)}, f32[3,16,32,128]{3,2,1,0:T(8,128)}, u32[]{:S(2)}) %copy-start.5) | copy-done | bytes 786456
  12.3 2.3 %first.1 = (f32[3,512,128]{2,1,0:T(8,128)S(1)}, f32[2,3,3,16,128]{4,3,2,1,0:T(8,128)S(1)}, bf16[256,1024]{1,0:T(8,128)(2,1)S(1)}, bf16[512,512]{1,0:T(8,128)(2,1...) custom-call(s32[4]{0:T(128)S(1)} %pad_add_fusion.flags, ...), custom_call_target="tpu_custom_call" | custom-call | tf_op jit(solution)/shard_map/first/pallas_call | solution.py:321
  16.0 2.6 %collective-permute-start.1 = (f32[72,128]{1,0:T(8,128)S(1)}, f32[72,128]{1,0:T(8,128)S(1)}, u32[]{:S(2)}, u32[]{:S(2)}) collective-permute-start(f32[72,128]{1,0:T(8,128)S(1)} %add.43), channel_id=1, source_target_pairs={{0,3},{1,2},{2,1},{3,0},{4,7},{5,6},{6,5},{7,4},{8,11},{9,10},{10,... | collective-permute-start | bytes 110600 | tf_op jit(solution)/shard_map/ppermute | solution.py:354
  18.6 1.5 %collective-permute-start.2 = (f32[96,128]{1,0:T(8,128)S(1)}, f32[96,128]{1,0:T(8,128)S(1)}, u32[]{:S(2)}, u32[]{:S(2)}) collective-permute-start(f32[96,128]{1,0:T(8,128)S(1)} %get-tuple-element.52), channel_id=1, source_target_pairs={{0,4},{1,5},{2,6},{3,7},{4,0},{5,1},{6,2},{7,3},{8,12},{9,13},{10,... | collective-permute-start | bytes 147464 | tf_op jit(solution)/shard_map/ppermute | solution.py:351
  20.3 2.2 %inner.8.z_ref = f32[3,512,128]{2,1,0:T(8,128)S(1)} custom-call(f32[3,512,128]{2,1,0:T(8,128)S(1)} %bitcast.29, bf16[7,3,3,16,32,128]{5,4,3,2,1,0:T(8,128)(2,1)S(1)} %copy-done, f32[3,512,128]{2,1,0:T(8,128)S(1)} %bitcast.20), custom_call_target="tpu_custom_call" | custom-call | tf_op jit(solution)/shard_map/inner/pallas_call | solution.py:364
  22.8 2.1 %update.7 = (f32[3,512,128]{2,1,0:T(8,128)S(1)}, f32[52,128]{1,0:T(8,128)S(1)}, f32[48,128]{1,0:T(8,128)S(1)}, f32[96,128]{1,0:T(8,128)S(1)}, f32[96,128]{1,0:T(8,128)S(1)}) custom-call(s32[4]{0:T(128)S(1)} %pad_add_fusion.flags, f32[3,512,128]{2,1,0:T(8,128)S(1)} %inner.8.z_ref, f32[52,128]{1,0:T(8,128)S(1)} %slice.30.own, f32[52,128]{1,0:T(8,128)S(1)} %slice.31.g1, ...), custom_call_target="tpu_custom_call" | custom-call | tf_op jit(solution)/shard_map/update/pallas_call | solution.py:377
  25.0 2.9 %collective-permute-start.6 = (f32[96,128]{1,0:T(8,128)S(1)}, f32[96,128]{1,0:T(8,128)S(1)}, u32[]{:S(2)}, u32[]{:S(2)}) collective-permute-start(f32[96,128]{1,0:T(8,128)S(1)} %get-tuple-element.64), channel_id=1, source_target_pairs={{0,4},{1,5},{2,6},{3,7},{4,0},{5,1},{6,2},{7,3},{8,12},{9,13},{10,... | collective-permute-start | bytes 147464 | tf_op jit(solution)/shard_map/ppermute | solution.py:351
  28.4 2.0 %inner.9.z_ref = f32[3,512,128]{2,1,0:T(8,128)S(1)} custom-call(f32[3,512,128]{2,1,0:T(8,128)S(1)} %get-tuple-element.61.x_ref, bf16[7,3,3,16,32,128]{5,4,3,2,1,0:T(8,128)(2,1)S(1)} %bitcast.19, f32[3,512,128]{2,1,0:T(8,128)S(1)} %bitcast.21), custom_call_target="tpu_custom_call" | custom-call | tf_op jit(solution)/shard_map/inner/pallas_call | solution.py:364
  30.4 1.0 %collective-permute-done.5.g2 = f32[52,128]{1,0:T(8,128)S(1)} collective-permute-done((f32[52,128]{1,0:T(8,128)S(1)}, f32[52,128]{1,0:T(8,128)S(1)}, u32[]{:S(2)}, u32[]{:S(2)}) %collective-permute-start.5) | collective-permute-done | bytes 26656 | tf_op jit(solution)/shard_map/ppermute | solution.py:354
  31.4 2.1 %update.8 = (f32[3,512,128]{2,1,0:T(8,128)S(1)}, f32[52,128]{1,0:T(8,128)S(1)}, f32[48,128]{1,0:T(8,128)S(1)}, f32[96,128]{1,0:T(8,128)S(1)}, f32[96,128]{1,0:T(8,128)S(1)}) custom-call(s32[4]{0:T(128)S(1)} %pad_add_fusion.flags, f32[3,512,128]{2,1,0:T(8,128)S(1)} %inner.9.z_ref, f32[52,128]{1,0:T(8,128)S(1)} %add.44.own, ...), custom_call_target="tpu_custom_call" | custom-call | tf_op jit(solution)/shard_map/update/pallas_call | solution.py:377
  33.9 2.9 %collective-permute-start.10 = (f32[96,128]{1,0:T(8,128)S(1)}, f32[96,128]{1,0:T(8,128)S(1)}, u32[]{:S(2)}, u32[]{:S(2)}) collective-permute-start(f32[96,128]{1,0:T(8,128)S(1)} %get-tuple-element.69), channel_id=1, source_target_pairs={{0,4},{1,5},{2,6},{3,7},{4,0},{5,1},{6,2},{7,3},{8,12},{9,13},{10,... | collective-permute-start | bytes 147464 | tf_op jit(solution)/shard_map/ppermute | solution.py:351
  37.4 2.1 %inner.10.z_ref = f32[3,512,128]{2,1,0:T(8,128)S(1)} custom-call(f32[3,512,128]{2,1,0:T(8,128)S(1)} %get-tuple-element.66.x_ref, bf16[7,3,3,16,32,128]{5,4,3,2,1,0:T(8,128)(2,1)S(1)} %bitcast.19, f32[3,512,128]{2,1,0:T(8,128)S(1)} %bitcast.22), custom_call_target="tpu_custom_call" | custom-call | tf_op jit(solution)/shard_map/inner/pallas_call | solution.py:364
  40.2 2.1 %update.9 = (f32[3,512,128]{2,1,0:T(8,128)S(1)}, f32[52,128]{1,0:T(8,128)S(1)}, f32[48,128]{1,0:T(8,128)S(1)}, f32[96,128]{1,0:T(8,128)S(1)}, f32[96,128]{1,0:T(8,128)S(1)}) custom-call(s32[4]{0:T(128)S(1)} %pad_add_fusion.flags, f32[3,512,128]{2,1,0:T(8,128)S(1)} %inner.10.z_ref, f32[52,128]{1,0:T(8,128)S(1)} %add.45.own, ...), custom_call_target="tpu_custom_call" | custom-call | tf_op jit(solution)/shard_map/update/pallas_call | solution.py:377
  42.7 2.9 %collective-permute-start.14 = (f32[96,128]{1,0:T(8,128)S(1)}, f32[96,128]{1,0:T(8,128)S(1)}, u32[]{:S(2)}, u32[]{:S(2)}) collective-permute-start(f32[96,128]{1,0:T(8,128)S(1)} %get-tuple-element.74), channel_id=1, source_target_pairs={{0,4},{1,5},{2,6},{3,7},{4,0},{5,1},{6,2},{7,3},{8,12},{9,13},{10,... | collective-permute-start | bytes 147464 | tf_op jit(solution)/shard_map/ppermute | solution.py:351
  46.3 2.1 %inner.11.z_ref = f32[3,512,128]{2,1,0:T(8,128)S(1)} custom-call(f32[3,512,128]{2,1,0:T(8,128)S(1)} %get-tuple-element.71.x_ref, bf16[7,3,3,16,32,128]{5,4,3,2,1,0:T(8,128)(2,1)S(1)} %bitcast.19, f32[3,512,128]{2,1,0:T(8,128)S(1)} %bitcast.23), custom_call_target="tpu_custom_call" | custom-call | tf_op jit(solution)/shard_map/inner/pallas_call | solution.py:364
  49.1 2.1 %update.10 = (f32[3,512,128]{2,1,0:T(8,128)S(1)}, f32[52,128]{1,0:T(8,128)S(1)}, f32[48,128]{1,0:T(8,128)S(1)}, f32[96,128]{1,0:T(8,128)S(1)}, f32[96,128]{1,0:T(8,128)S(1)}) custom-call(s32[4]{0:T(128)S(1)} %pad_add_fusion.flags, f32[3,512,128]{2,1,0:T(8,128)S(1)} %inner.11.z_ref, f32[52,128]{1,0:T(8,128)S(1)} %add.46.own, ...), custom_call_target="tpu_custom_call" | custom-call | tf_op jit(solution)/shard_map/update/pallas_call | solution.py:377
  51.6 2.7 %collective-permute-start.18 = (f32[96,128]{1,0:T(8,128)S(1)}, f32[96,128]{1,0:T(8,128)S(1)}, u32[]{:S(2)}, u32[]{:S(2)}) collective-permute-start(f32[96,128]{1,0:T(8,128)S(1)} %get-tuple-element.79), channel_id=1, source_target_pairs={{0,4},{1,5},{2,6},{3,7},{4,0},{5,1},{6,2},{7,3},{8,12},{9,13},{10,... | collective-permute-start | bytes 147464 | tf_op jit(solution)/shard_map/ppermute | solution.py:351
  55.0 2.1 %inner.12.z_ref = f32[3,512,128]{2,1,0:T(8,128)S(1)} custom-call(f32[3,512,128]{2,1,0:T(8,128)S(1)} %get-tuple-element.76.x_ref, bf16[7,3,3,16,32,128]{5,4,3,2,1,0:T(8,128)(2,1)S(1)} %bitcast.19, f32[3,512,128]{2,1,0:T(8,128)S(1)} %bitcast.24), custom_call_target="tpu_custom_call" | custom-call | tf_op jit(solution)/shard_map/inner/pallas_call | solution.py:364
  57.8 2.1 %update.11 = (f32[3,512,128]{2,1,0:T(8,128)S(1)}, f32[52,128]{1,0:T(8,128)S(1)}, f32[48,128]{1,0:T(8,128)S(1)}, f32[96,128]{1,0:T(8,128)S(1)}, f32[96,128]{1,0:T(8,128)S(1)}) custom-call(s32[4]{0:T(128)S(1)} %pad_add_fusion.flags, f32[3,512,128]{2,1,0:T(8,128)S(1)} %inner.12.z_ref, f32[52,128]{1,0:T(8,128)S(1)} %add.47.own, ...), custom_call_target="tpu_custom_call" | custom-call | tf_op jit(solution)/shard_map/update/pallas_call | solution.py:377
  60.3 1.9 %collective-permute-start.22 = (f32[96,128]{1,0:T(8,128)S(1)}, f32[96,128]{1,0:T(8,128)S(1)}, u32[]{:S(2)}, u32[]{:S(2)}) collective-permute-start(f32[96,128]{1,0:T(8,128)S(1)} %get-tuple-element.84), channel_id=1, source_target_pairs={{0,4},{1,5},{2,6},{3,7},{4,0},{5,1},{6,2},{7,3},{8,12},{9,13},{10,... | collective-permute-start | bytes 147464 | tf_op jit(solution)/shard_map/ppermute | solution.py:351
  62.8 2.1 %inner.13.z_ref = f32[3,512,128]{2,1,0:T(8,128)S(1)} custom-call(f32[3,512,128]{2,1,0:T(8,128)S(1)} %get-tuple-element.81.x_ref, bf16[7,3,3,16,32,128]{5,4,3,2,1,0:T(8,128)(2,1)S(1)} %bitcast.19, f32[3,512,128]{2,1,0:T(8,128)S(1)} %bitcast.25), custom_call_target="tpu_custom_call" | custom-call | tf_op jit(solution)/shard_map/inner/pallas_call | solution.py:364
  65.6 2.1 %update.12 = (f32[3,512,128]{2,1,0:T(8,128)S(1)}, f32[52,128]{1,0:T(8,128)S(1)}, f32[48,128]{1,0:T(8,128)S(1)}, f32[96,128]{1,0:T(8,128)S(1)}, f32[96,128]{1,0:T(8,128)S(1)}) custom-call(s32[4]{0:T(128)S(1)} %pad_add_fusion.flags, f32[3,512,128]{2,1,0:T(8,128)S(1)} %inner.13.z_ref, f32[52,128]{1,0:T(8,128)S(1)} %add.48.own, ...), custom_call_target="tpu_custom_call" | custom-call | tf_op jit(solution)/shard_map/update/pallas_call | solution.py:377
  68.1 2.7 %collective-permute-start.26 = (f32[96,128]{1,0:T(8,128)S(1)}, f32[96,128]{1,0:T(8,128)S(1)}, u32[]{:S(2)}, u32[]{:S(2)}) collective-permute-start(f32[96,128]{1,0:T(8,128)S(1)} %get-tuple-element.89), channel_id=1, source_target_pairs={{0,4},{1,5},{2,6},{3,7},{4,0},{5,1},{6,2},{7,3},{8,12},{9,13},{10,... | collective-permute-start | bytes 147464 | tf_op jit(solution)/shard_map/ppermute | solution.py:351
  71.5 2.1 %inner.14.z_ref = f32[3,512,128]{2,1,0:T(8,128)S(1)} custom-call(f32[3,512,128]{2,1,0:T(8,128)S(1)} %get-tuple-element.86.x_ref, bf16[7,3,3,16,32,128]{5,4,3,2,1,0:T(8,128)(2,1)S(1)} %bitcast.19, f32[3,512,128]{2,1,0:T(8,128)S(1)} %bitcast.26), custom_call_target="tpu_custom_call" | custom-call | tf_op jit(solution)/shard_map/inner/pallas_call | solution.py:364
  74.3 2.1 %update.13 = (f32[3,512,128]{2,1,0:T(8,128)S(1)}, f32[52,128]{1,0:T(8,128)S(1)}, f32[48,128]{1,0:T(8,128)S(1)}, f32[96,128]{1,0:T(8,128)S(1)}, f32[96,128]{1,0:T(8,128)S(1)}) custom-call(s32[4]{0:T(128)S(1)} %pad_add_fusion.flags, f32[3,512,128]{2,1,0:T(8,128)S(1)} %inner.14.z_ref, f32[52,128]{1,0:T(8,128)S(1)} %add.49.own, ...), custom_call_target="tpu_custom_call" | custom-call | tf_op jit(solution)/shard_map/update/pallas_call | solution.py:377
  77.6 1.9 %collective-permute-start.30 = (f32[96,128]{1,0:T(8,128)S(1)}, f32[96,128]{1,0:T(8,128)S(1)}, u32[]{:S(2)}, u32[]{:S(2)}) collective-permute-start(f32[96,128]{1,0:T(8,128)S(1)} %get-tuple-element.94), channel_id=1, source_target_pairs={{0,4},{1,5},{2,6},{3,7},{4,0},{5,1},{6,2},{7,3},{8,12},{9,13},{10,... | collective-permute-start | bytes 147464 | tf_op jit(solution)/shard_map/ppermute | solution.py:351
  80.2 3.3 %copy-done.1 = bf16[7,3,3,16,32,128]{5,4,3,2,1,0:T(8,128)(2,1)S(1)} copy-done((bf16[7,3,3,16,32,128]{5,4,3,2,1,0:T(8,128)(2,1)S(1)}, bf16[7,3,3,16,32,128]{5,4,3,2,1,0:T(8,128)(2,1)}, u32[]{:S(2)}) %copy-start.1) | copy-done | bytes 8257560
  83.5 1.1 %copy-done.7 = f32[3,512,128]{2,1,0:T(8,128)S(1)} copy-done((f32[3,512,128]{2,1,0:T(8,128)S(1)}, f32[3,512,128]{2,1,0:T(8,128)}, u32[]{:S(2)}) %copy-start.7) | copy-done | bytes 786456
  84.7 2.0 %inner.15.z_ref = f32[3,512,128]{2,1,0:T(8,128)S(1)} custom-call(f32[3,512,128]{2,1,0:T(8,128)S(1)} %copy-done.7, bf16[7,3,3,16,32,128]{5,4,3,2,1,0:T(8,128)(2,1)S(1)} %copy-done.1, f32[3,512,128]{2,1,0:T(8,128)S(1)} %bitcast.27), custom_call_target="tpu_custom_call" | custom-call | tf_op jit(solution)/shard_map/inner/pallas_call | solution.py:364
  86.7 2.2 %update_last.1 = (f32[3,512,128]{2,1,0:T(8,128)}, f32[1,4,128]{2,1,0:T(4,128)S(1)}) custom-call(s32[4]{0:T(128)S(1)} %pad_add_fusion.flags, f32[3,512,128]{2,1,0:T(8,128)S(1)} %inner.15.z_ref, f32[52,128]{1,0:T(8,128)S(1)} %add.50.own, f32[52,128]{1,0:T(8,128)S(1)} %collective-permute-done.28.got_ref.g1, f32[52,128]{1,0:T(8,128)S(1)} %collective-permute-done.29.g2, ...), custom_call_target="tpu_custom_call" | custom-call | tf_op jit(solution)/shard_map/update_last/pallas_call | solution.py:367
  (102 shorter events, 19.9 us)
Async XLA Ops:
  14.6 1.4 %collective-permute-start = (f32[72,128]{1,0:T(8,128)S(1)}, f32[72,128]{1,0:T(8,128)S(1)}, u32[]{:S(2)}, u32[]{:S(2)}) collective-permute-start(f32[72,128]{1,0:T(8,128)S(1)} %get-tuple-element.51.own_ref), channel_id=1, source_target_pairs={{0,1},{1,0},{2,3},{3,2},{4,5},{5,4},{6,7},{7,6},{8,9},{9,8},{10,11... | collective-permute-start | bytes 110600 | tf_op jit(solution)/shard_map/ppermute | solution.py:350
  16.0 6.5 %collective-permute-start.1 = (f32[72,128]{1,0:T(8,128)S(1)}, f32[72,128]{1,0:T(8,128)S(1)}, u32[]{:S(2)}, u32[]{:S(2)}) collective-permute-start(f32[72,128]{1,0:T(8,128)S(1)} %add.43), channel_id=1, source_target_pairs={{0,3},{1,2},{2,1},{3,0},{4,7},{5,6},{6,5},{7,4},{8,11},{9,10},{10,... | collective-permute-start | bytes 110600 | tf_op jit(solution)/shard_map/ppermute | solution.py:354
  18.6 4.1 %collective-permute-start.2 = (f32[96,128]{1,0:T(8,128)S(1)}, f32[96,128]{1,0:T(8,128)S(1)}, u32[]{:S(2)}, u32[]{:S(2)}) collective-permute-start(f32[96,128]{1,0:T(8,128)S(1)} %get-tuple-element.52), channel_id=1, source_target_pairs={{0,4},{1,5},{2,6},{3,7},{4,0},{5,1},{6,2},{7,3},{8,12},{9,13},{10,... | collective-permute-start | bytes 147464 | tf_op jit(solution)/shard_map/ppermute | solution.py:351
  20.2 2.6 %collective-permute-start.3 = (f32[96,128]{1,0:T(8,128)S(1)}, f32[96,128]{1,0:T(8,128)S(1)}, u32[]{:S(2)}, u32[]{:S(2)}) collective-permute-start(f32[96,128]{1,0:T(8,128)S(1)} %get-tuple-element.53), channel_id=1, source_target_pairs={{0,1},{1,0},{2,3},{3,2},{4,8},{5,9},{6,10},{7,11},{8,4},{9,5},{10,... | collective-permute-start | bytes 147464 | tf_op jit(solution)/shard_map/ppermute | solution.py:352
  24.9 3.2 %collective-permute-start.4 = (f32[52,128]{1,0:T(8,128)S(1)}, f32[52,128]{1,0:T(8,128)S(1)}, u32[]{:S(2)}, u32[]{:S(2)}) collective-permute-start(f32[52,128]{1,0:T(8,128)S(1)} %get-tuple-element.63.own_ref), channel_id=1, source_target_pairs={{0,1},{1,0},{2,3},{3,2},{4,5},{5,4},{6,7},{7,6},{8,9},{9,8},{10,11... | collective-permute-start | bytes 79880 | tf_op jit(solution)/shard_map/ppermute | solution.py:350
  25.0 5.3 %collective-permute-start.6 = (f32[96,128]{1,0:T(8,128)S(1)}, f32[96,128]{1,0:T(8,128)S(1)}, u32[]{:S(2)}, u32[]{:S(2)}) collective-permute-start(f32[96,128]{1,0:T(8,128)S(1)} %get-tuple-element.64), channel_id=1, source_target_pairs={{0,4},{1,5},{2,6},{3,7},{4,0},{5,1},{6,2},{7,3},{8,12},{9,13},{10,... | collective-permute-start | bytes 147464 | tf_op jit(solution)/shard_map/ppermute | solution.py:351
  27.9 2.5 %collective-permute-start.7 = (f32[96,128]{1,0:T(8,128)S(1)}, f32[96,128]{1,0:T(8,128)S(1)}, u32[]{:S(2)}, u32[]{:S(2)}) collective-permute-start(f32[96,128]{1,0:T(8,128)S(1)} %get-tuple-element.65), channel_id=1, source_target_pairs={{0,1},{1,0},{2,3},{3,2},{4,8},{5,9},{6,10},{7,11},{8,4},{9,5},{10,... | collective-permute-start | bytes 147464 | tf_op jit(solution)/shard_map/ppermute | solution.py:352
  28.1 3.3 %collective-permute-start.5 = (f32[52,128]{1,0:T(8,128)S(1)}, f32[52,128]{1,0:T(8,128)S(1)}, u32[]{:S(2)}, u32[]{:S(2)}) collective-permute-start(f32[52,128]{1,0:T(8,128)S(1)} %add.44.own), channel_id=1, source_target_pairs={{0,3},{1,2},{2,1},{3,0},{4,7},{5,6},{6,5},{7,4},{8,11},{9,10},{10,... | collective-permute-start | bytes 79880 | tf_op jit(solution)/shard_map/ppermute | solution.py:354
  33.5 3.4 %collective-permute-start.8 = (f32[52,128]{1,0:T(8,128)S(1)}, f32[52,128]{1,0:T(8,128)S(1)}, u32[]{:S(2)}, u32[]{:S(2)}) collective-permute-start(f32[52,128]{1,0:T(8,128)S(1)} %get-tuple-element.68.own_ref), channel_id=1, source_target_pairs={{0,1},{1,0},{2,3},{3,2},{4,5},{5,4},{6,7},{7,6},{8,9},{9,8},{10,11... | collective-permute-start | bytes 79880 | tf_op jit(solution)/shard_map/ppermute | solution.py:350
  33.9 5.7 %collective-permute-start.10 = (f32[96,128]{1,0:T(8,128)S(1)}, f32[96,128]{1,0:T(8,128)S(1)}, u32[]{:S(2)}, u32[]{:S(2)}) collective-permute-start(f32[96,128]{1,0:T(8,128)S(1)} %get-tuple-element.69), channel_id=1, source_target_pairs={{0,4},{1,5},{2,6},{3,7},{4,0},{5,1},{6,2},{7,3},{8,12},{9,13},{10,... | collective-permute-start | bytes 147464 | tf_op jit(solution)/shard_map/ppermute | solution.py:351
  36.8 2.7 %collective-permute-start.11 = (f32[96,128]{1,0:T(8,128)S(1)}, f32[96,128]{1,0:T(8,128)S(1)}, u32[]{:S(2)}, u32[]{:S(2)}) collective-permute-start(f32[96,128]{1,0:T(8,128)S(1)} %get-tuple-element.70), channel_id=1, source_target_pairs={{0,1},{1,0},{2,3},{3,2},{4,8},{5,9},{6,10},{7,11},{8,4},{9,5},{10,... | collective-permute-start | bytes 147464 | tf_op jit(solution)/shard_map/ppermute | solution.py:352
  36.9 3.4 %collective-permute-start.9 = (f32[52,128]{1,0:T(8,128)S(1)}, f32[52,128]{1,0:T(8,128)S(1)}, u32[]{:S(2)}, u32[]{:S(2)}) collective-permute-start(f32[52,128]{1,0:T(8,128)S(1)} %add.45.own), channel_id=1, source_target_pairs={{0,3},{1,2},{2,1},{3,0},{4,7},{5,6},{6,5},{7,4},{8,11},{9,10},{10,... | collective-permute-start | bytes 79880 | tf_op jit(solution)/shard_map/ppermute | solution.py:354
  42.3 3.5 %collective-permute-start.12 = (f32[52,128]{1,0:T(8,128)S(1)}, f32[52,128]{1,0:T(8,128)S(1)}, u32[]{:S(2)}, u32[]{:S(2)}) collective-permute-start(f32[52,128]{1,0:T(8,128)S(1)} %get-tuple-element.73.own_ref), channel_id=1, source_target_pairs={{0,1},{1,0},{2,3},{3,2},{4,5},{5,4},{6,7},{7,6},{8,9},{9,8},{10,11... | collective-permute-start | bytes 79880 | tf_op jit(solution)/shard_map/ppermute | solution.py:350
  42.7 5.7 %collective-permute-start.14 = (f32[96,128]{1,0:T(8,128)S(1)}, f32[96,128]{1,0:T(8,128)S(1)}, u32[]{:S(2)}, u32[]{:S(2)}) collective-permute-start(f32[96,128]{1,0:T(8,128)S(1)} %get-tuple-element.74), channel_id=1, source_target_pairs={{0,4},{1,5},{2,6},{3,7},{4,0},{5,1},{6,2},{7,3},{8,12},{9,13},{10,... | collective-permute-start | bytes 147464 | tf_op jit(solution)/shard_map/ppermute | solution.py:351
  45.6 2.8 %collective-permute-start.15 = (f32[96,128]{1,0:T(8,128)S(1)}, f32[96,128]{1,0:T(8,128)S(1)}, u32[]{:S(2)}, u32[]{:S(2)}) collective-permute-start(f32[96,128]{1,0:T(8,128)S(1)} %get-tuple-element.75), channel_id=1, source_target_pairs={{0,1},{1,0},{2,3},{3,2},{4,8},{5,9},{6,10},{7,11},{8,4},{9,5},{10,... | collective-permute-start | bytes 147464 | tf_op jit(solution)/shard_map/ppermute | solution.py:352
  45.8 3.3 %collective-permute-start.13 = (f32[52,128]{1,0:T(8,128)S(1)}, f32[52,128]{1,0:T(8,128)S(1)}, u32[]{:S(2)}, u32[]{:S(2)}) collective-permute-start(f32[52,128]{1,0:T(8,128)S(1)} %add.46.own), channel_id=1, source_target_pairs={{0,3},{1,2},{2,1},{3,0},{4,7},{5,6},{6,5},{7,4},{8,11},{9,10},{10,... | collective-permute-start | bytes 79880 | tf_op jit(solution)/shard_map/ppermute | solution.py:354
  51.2 3.2 %collective-permute-start.16 = (f32[52,128]{1,0:T(8,128)S(1)}, f32[52,128]{1,0:T(8,128)S(1)}, u32[]{:S(2)}, u32[]{:S(2)}) collective-permute-start(f32[52,128]{1,0:T(8,128)S(1)} %get-tuple-element.78.own_ref), channel_id=1, source_target_pairs={{0,1},{1,0},{2,3},{3,2},{4,5},{5,4},{6,7},{7,6},{8,9},{9,8},{10,11... | collective-permute-start | bytes 79880 | tf_op jit(solution)/shard_map/ppermute | solution.py:350
  51.6 5.5 %collective-permute-start.18 = (f32[96,128]{1,0:T(8,128)S(1)}, f32[96,128]{1,0:T(8,128)S(1)}, u32[]{:S(2)}, u32[]{:S(2)}) collective-permute-start(f32[96,128]{1,0:T(8,128)S(1)} %get-tuple-element.79), channel_id=1, source_target_pairs={{0,4},{1,5},{2,6},{3,7},{4,0},{5,1},{6,2},{7,3},{8,12},{9,13},{10,... | collective-permute-start | bytes 147464 | tf_op jit(solution)/shard_map/ppermute | solution.py:351
  54.3 2.8 %collective-permute-start.19 = (f32[96,128]{1,0:T(8,128)S(1)}, f32[96,128]{1,0:T(8,128)S(1)}, u32[]{:S(2)}, u32[]{:S(2)}) collective-permute-start(f32[96,128]{1,0:T(8,128)S(1)} %get-tuple-element.80), channel_id=1, source_target_pairs={{0,1},{1,0},{2,3},{3,2},{4,8},{5,9},{6,10},{7,11},{8,4},{9,5},{10,... | collective-permute-start | bytes 147464 | tf_op jit(solution)/shard_map/ppermute | solution.py:352
  54.4 3.4 %collective-permute-start.17 = (f32[52,128]{1,0:T(8,128)S(1)}, f32[52,128]{1,0:T(8,128)S(1)}, u32[]{:S(2)}, u32[]{:S(2)}) collective-permute-start(f32[52,128]{1,0:T(8,128)S(1)} %add.47.own), channel_id=1, source_target_pairs={{0,3},{1,2},{2,1},{3,0},{4,7},{5,6},{6,5},{7,4},{8,11},{9,10},{10,... | collective-permute-start | bytes 79880 | tf_op jit(solution)/shard_map/ppermute | solution.py:354
  59.9 2.4 %collective-permute-start.20 = (f32[52,128]{1,0:T(8,128)S(1)}, f32[52,128]{1,0:T(8,128)S(1)}, u32[]{:S(2)}, u32[]{:S(2)}) collective-permute-start(f32[52,128]{1,0:T(8,128)S(1)} %get-tuple-element.83.own_ref), channel_id=1, source_target_pairs={{0,1},{1,0},{2,3},{3,2},{4,5},{5,4},{6,7},{7,6},{8,9},{9,8},{10,11... | collective-permute-start | bytes 79880 | tf_op jit(solution)/shard_map/ppermute | solution.py:350
  60.3 4.6 %collective-permute-start.22 = (f32[96,128]{1,0:T(8,128)S(1)}, f32[96,128]{1,0:T(8,128)S(1)}, u32[]{:S(2)}, u32[]{:S(2)}) collective-permute-start(f32[96,128]{1,0:T(8,128)S(1)} %get-tuple-element.84), channel_id=1, source_target_pairs={{0,4},{1,5},{2,6},{3,7},{4,0},{5,1},{6,2},{7,3},{8,12},{9,13},{10,... | collective-permute-start | bytes 147464 | tf_op jit(solution)/shard_map/ppermute | solution.py:351
  62.1 2.8 %collective-permute-start.23 = (f32[96,128]{1,0:T(8,128)S(1)}, f32[96,128]{1,0:T(8,128)S(1)}, u32[]{:S(2)}, u32[]{:S(2)}) collective-permute-start(f32[96,128]{1,0:T(8,128)S(1)} %get-tuple-element.85), channel_id=1, source_target_pairs={{0,1},{1,0},{2,3},{3,2},{4,8},{5,9},{6,10},{7,11},{8,4},{9,5},{10,... | collective-permute-start | bytes 147464 | tf_op jit(solution)/shard_map/ppermute | solution.py:352
  62.2 3.4 %collective-permute-start.21 = (f32[52,128]{1,0:T(8,128)S(1)}, f32[52,128]{1,0:T(8,128)S(1)}, u32[]{:S(2)}, u32[]{:S(2)}) collective-permute-start(f32[52,128]{1,0:T(8,128)S(1)} %add.48.own), channel_id=1, source_target_pairs={{0,3},{1,2},{2,1},{3,0},{4,7},{5,6},{6,5},{7,4},{8,11},{9,10},{10,... | collective-permute-start | bytes 79880 | tf_op jit(solution)/shard_map/ppermute | solution.py:354
  67.7 3.2 %collective-permute-start.24 = (f32[52,128]{1,0:T(8,128)S(1)}, f32[52,128]{1,0:T(8,128)S(1)}, u32[]{:S(2)}, u32[]{:S(2)}) collective-permute-start(f32[52,128]{1,0:T(8,128)S(1)} %get-tuple-element.88.own_ref), channel_id=1, source_target_pairs={{0,1},{1,0},{2,3},{3,2},{4,5},{5,4},{6,7},{7,6},{8,9},{9,8},{10,11... | collective-permute-start | bytes 79880 | tf_op jit(solution)/shard_map/ppermute | solution.py:350
  68.1 5.5 %collective-permute-start.26 = (f32[96,128]{1,0:T(8,128)S(1)}, f32[96,128]{1,0:T(8,128)S(1)}, u32[]{:S(2)}, u32[]{:S(2)}) collective-permute-start(f32[96,128]{1,0:T(8,128)S(1)} %get-tuple-element.89), channel_id=1, source_target_pairs={{0,4},{1,5},{2,6},{3,7},{4,0},{5,1},{6,2},{7,3},{8,12},{9,13},{10,... | collective-permute-start | bytes 147464 | tf_op jit(solution)/shard_map/ppermute | solution.py:351
  70.8 2.8 %collective-permute-start.27 = (f32[96,128]{1,0:T(8,128)S(1)}, f32[96,128]{1,0:T(8,128)S(1)}, u32[]{:S(2)}, u32[]{:S(2)}) collective-permute-start(f32[96,128]{1,0:T(8,128)S(1)} %get-tuple-element.90), channel_id=1, source_target_pairs={{0,1},{1,0},{2,3},{3,2},{4,8},{5,9},{6,10},{7,11},{8,4},{9,5},{10,... | collective-permute-start | bytes 147464 | tf_op jit(solution)/shard_map/ppermute | solution.py:352
  70.9 3.4 %collective-permute-start.25 = (f32[52,128]{1,0:T(8,128)S(1)}, f32[52,128]{1,0:T(8,128)S(1)}, u32[]{:S(2)}, u32[]{:S(2)}) collective-permute-start(f32[52,128]{1,0:T(8,128)S(1)} %add.49.own), channel_id=1, source_target_pairs={{0,3},{1,2},{2,1},{3,0},{4,7},{5,6},{6,5},{7,4},{8,11},{9,10},{10,... | collective-permute-start | bytes 79880 | tf_op jit(solution)/shard_map/ppermute | solution.py:354
  77.2 2.4 %collective-permute-start.28 = (f32[52,128]{1,0:T(8,128)S(1)}, f32[52,128]{1,0:T(8,128)S(1)}, u32[]{:S(2)}, u32[]{:S(2)}) collective-permute-start(f32[52,128]{1,0:T(8,128)S(1)} %get-tuple-element.93.own_ref), channel_id=1, source_target_pairs={{0,1},{1,0},{2,3},{3,2},{4,5},{5,4},{6,7},{7,6},{8,9},{9,8},{10,11... | collective-permute-start | bytes 79880 | tf_op jit(solution)/shard_map/ppermute | solution.py:350
  77.6 9.1 %collective-permute-start.30 = (f32[96,128]{1,0:T(8,128)S(1)}, f32[96,128]{1,0:T(8,128)S(1)}, u32[]{:S(2)}, u32[]{:S(2)}) collective-permute-start(f32[96,128]{1,0:T(8,128)S(1)} %get-tuple-element.94), channel_id=1, source_target_pairs={{0,4},{1,5},{2,6},{3,7},{4,0},{5,1},{6,2},{7,3},{8,12},{9,13},{10,... | collective-permute-start | bytes 147464 | tf_op jit(solution)/shard_map/ppermute | solution.py:351
  79.4 7.2 %collective-permute-start.31 = (f32[96,128]{1,0:T(8,128)S(1)}, f32[96,128]{1,0:T(8,128)S(1)}, u32[]{:S(2)}, u32[]{:S(2)}) collective-permute-start(f32[96,128]{1,0:T(8,128)S(1)} %get-tuple-element.95), channel_id=1, source_target_pairs={{0,1},{1,0},{2,3},{3,2},{4,8},{5,9},{6,10},{7,11},{8,4},{9,5},{10,... | collective-permute-start | bytes 147464 | tf_op jit(solution)/shard_map/ppermute | solution.py:352
  79.6 7.1 %collective-permute-start.29 = (f32[52,128]{1,0:T(8,128)S(1)}, f32[52,128]{1,0:T(8,128)S(1)}, u32[]{:S(2)}, u32[]{:S(2)}) collective-permute-start(f32[52,128]{1,0:T(8,128)S(1)} %add.50.own), channel_id=1, source_target_pairs={{0,3},{1,2},{2,1},{3,0},{4,7},{5,6},{6,5},{7,4},{8,11},{9,10},{10,... | collective-permute-start | bytes 79880 | tf_op jit(solution)/shard_map/ppermute | solution.py:354
  (13 other events, 46.9 us)
where the time goes:
time: 90.1 us; the launch traced here: 89.5 us
  Pallas kernels  35.5 us (39%)
  starting transfers between devices  29.9 us (33%)
  local copies, waits for them, and re-layouts  15.4 us (17%)
  waiting for transfers between devices  5.59 us (6%)
  other arithmetic  2.18 us (2%)
  between operations  1.02 us (1%)
    ppermute x8, starting transfers between devices, body(): g3 = lax.ppermute(m3, both, gx_swap(gx, gy, 0))  19.4 us
    pallas_call x8, Pallas kernels, body(): z = inner(x, jacobian, rhs)  16.5 us
    pallas_call x7, Pallas kernels, body(): pl.pallas_call(functools.partial(update_kernel, False), out_shape=(shape(...  14.5 us
    unnamed x26, local copies, waits for them, and re-layouts  13.6 us
    ppermute x8, starting transfers between devices, body(): g2 = lax.ppermute(own, 'gy', gy_swap(gy, 1))  6.46 us
    ppermute x8, waiting for transfers between devices, body(): g2 = lax.ppermute(own, 'gy', gy_swap(gy, 1))  4.43 us
    ppermute x8, starting transfers between devices, body(): g1 = lax.ppermute(m1, 'gy', gy_swap(gy, 0))  3.12 us
    pallas_call x1, Pallas kernels, body(): first(flags, x, jacobian, diag, perf_block.reshape(1, perfs), perf_block....  2.32 us
  transfers between devices with their start and end apart: 32, of which 8 were waited for; matrix products, arithmetic and copies ran while one was open for 0% of the time, Pallas kernels for 18%

commit v1 on v0

v1 whole, which is shorter than its diff:
```python
import functools

import jax
import jax.numpy as jnp
from jax import lax
from jax.experimental import pallas as pl
from jax.experimental.pallas import tpu as pltpu
from jax.sharding import PartitionSpec as P

PHASES = 3
WELL_UNK = 4
BLOCK = 64
ITERS = 8
LANES = 128
F32 = jnp.float32
BF16 = jnp.bfloat16
VM = pl.BlockSpec(memory_space=pltpu.VMEM)
HB = pl.BlockSpec(memory_space=pltpu.MemorySpace.HBM)
SM = pl.BlockSpec(memory_space=pltpu.SMEM)
PARAMS = pltpu.CompilerParams(vmem_limit_bytes=16 * 1024 * 1024)


def split_2(value):
    high = value.astype(BF16)
    return high, (value - high.astype(F32)).astype(BF16)


def edge_messages(flags, x_ref, row_ref, col_ref, m1_ref, m2_ref, m3_ref, m4_ref):
    rows, cols = col_ref.shape[3], row_ref.shape[3]
    gx_odd, gy_odd = flags[0] == 1, flags[1] == 1
    x_first = [x_ref[r, 0:cols, :] for r in range(PHASES)]
    x_last = [x_ref[r, (rows - 1) * cols : rows * cols, :] for r in range(PHASES)]
    c_first = [x_ref[r, pl.ds(0, rows, stride=cols), :] for r in range(PHASES)]
    c_last = [x_ref[r, pl.ds(cols - 1, rows, stride=cols), :] for r in range(PHASES)]
    for t in range(PHASES):
        up = sum(row_ref[0, r, t] * x_first[r] for r in range(PHASES))
        down = sum(row_ref[1, r, t] * x_last[r] for r in range(PHASES))
        left = sum(col_ref[0, r, t] * c_first[r] for r in range(PHASES))
        right = sum(col_ref[1, r, t] * c_last[r] for r in range(PHASES))
        m3_ref[t * cols : (t + 1) * cols, :] = jnp.where(gx_odd, up, down)
        m4_ref[t * cols : (t + 1) * cols, :] = jnp.where(gx_odd, down, up)
        m1_ref[t * rows : (t + 1) * rows, :] = jnp.where(gy_odd, left, right)
        m2_ref[t * rows : (t + 1) * rows, :] = jnp.where(gy_odd, right, left)


def well_partials(x_ref, pick_ref, well_ref, wc_ref, xs_ref, g_ref, write):
    cells = x_ref.shape[1]
    perfs = pick_ref.shape[0]
    for r in range(PHASES):
        high, low = split_2(x_ref[r])
        xs_ref[0:cells, r * LANES : (r + 1) * LANES] = high
        xs_ref[cells : 2 * cells, r * LANES : (r + 1) * LANES] = low
    g_ref[...] = jnp.dot(pick_ref[...], xs_ref[...], preferred_element_type=F32)
    width = well_ref.shape[0]
    chunk = 64
    totals = [[jnp.zeros((8, LANES), F32) for _ in range(width)] for _ in range(WELL_UNK)]
    for start in range(0, perfs, chunk):
        rows = slice(start, start + chunk)
        picked = [g_ref[rows, r * LANES : (r + 1) * LANES] for r in range(PHASES)]
        for u in range(WELL_UNK):
            lane_terms = sum(wc_ref[u, r, rows].astype(F32) * picked[r] for r in range(PHASES))
            term = jnp.sum(lane_terms, axis=1, keepdims=True)
            for h in range(width):
                spread = well_ref[h, rows, :] * term
                totals[u][h] = totals[u][h] + sum(spread[i : i + 8] for i in range(0, chunk, 8))
    for h in range(width):
        for u in range(WELL_UNK):
            write(h * WELL_UNK + u, jnp.sum(totals[u][h], axis=0, keepdims=True))


def expanded(eye, coupling_ref, u, own_half, out_ref):
    for r in range(PHASES):
        piece = coupling_ref[u, r * BLOCK : (r + 1) * BLOCK, :]
        doubled = jnp.concatenate([piece, piece], axis=0)
        out_ref[u, r] = jnp.where(own_half, turned(eye, doubled), 0.0).astype(BF16)


def turned(eye, value):
    return lax.dot_general(eye, value, (((1,), (1,)), ((), ())), preferred_element_type=F32)


def hot(mask):
    return mask.astype(F32).astype(BF16)


def iota(dims, axis):
    return lax.broadcasted_iota(jnp.int32, dims, axis)


def first_kernel(
    flags, x_in, jac_in, rhs_in, diag_in, wcoef_in, ccoef_in,
    block_in, well_in, owner_in, rhs_well_in, inv_well_in,
    x_ref, jac_ref, rhs_ref, inv_ref, row_ref, col_ref, pick_ref, spread_ref, well_ref, wc_ref,
    cc_ref, m1_ref, m2_ref, m3_ref, m4_ref, wcoef, ccoef, xs_ref, g_ref,
    block_row, well_row, owner_row, rhs_well, inv_well, sems, small_sems,
):
    pairs = [
        (block_in, block_row), (well_in, well_row), (owner_in, owner_row),
        (rhs_well_in, rhs_well), (inv_well_in, inv_well),
    ]
    small = [pltpu.make_async_copy(a, b, small_sems.at[i]) for i, (a, b) in enumerate(pairs)]
    for copy in small:
        copy.start()
    pairs = [
        (wcoef_in, wcoef), (ccoef_in, ccoef), (x_in, x_ref),
        (jac_in, jac_ref), (diag_in, inv_ref), (rhs_in, rhs_ref),
    ]
    copies = [pltpu.make_async_copy(a, b, sems.at[i]) for i, (a, b) in enumerate(pairs)]
    for copy in copies:
        copy.start()
    rows, cols = jac_ref.shape[3], jac_ref.shape[4]
    cells = rows * cols
    perfs = block_row.shape[1]
    width = well_ref.shape[0]
    well_dev = rhs_well.shape[1]
    base, unk = PHASES * rows, WELL_UNK * width
    eye = hot(iota((perfs, perfs), 0) == iota((perfs, perfs), 1))
    for copy in small:
        copy.wait()
    block = block_row[...]
    spread = hot(iota((cells, perfs), 0) == block // 2)
    spread_ref[:, 0:perfs] = spread
    spread_ref[:, perfs : 2 * perfs] = spread
    pick = turned(eye, spread).astype(BF16)
    pick_ref[:, 0:cells] = pick
    pick_ref[:, cells : 2 * cells] = pick
    own_half = turned(eye, hot(iota((LANES, perfs), 0) // BLOCK == block % 2)) > 0.5
    for h in range(width):
        slot = iota((LANES, perfs), 0) + h * LANES
        well = owner_row[...] * well_dev + well_row[...]
        well_ref[h] = turned(eye, hot(slot == well))
        place = iota((well_dev, LANES), 0) + flags[4] * well_dev
        place = (place == iota((well_dev, LANES), 1) + h * LANES).astype(F32)
        for v in range(WELL_UNK + 1):
            value = rhs_well[...] if v == 0 else inv_well[v - 1]
            value = jnp.dot(
                value, place, precision=lax.Precision.HIGHEST, preferred_element_type=F32
            )
            at = base + unk
            at += h * WELL_UNK if v == 0 else unk + (h * WELL_UNK + v - 1) * WELL_UNK
            m1_ref[at : at + WELL_UNK, :] = value
    copies[0].wait()
    for u in range(WELL_UNK):
        expanded(eye, wcoef, u, own_half, wc_ref)
    copies[1].wait()
    for u in range(WELL_UNK):
        expanded(eye, ccoef, u, own_half, cc_ref)
    copies[2].wait()

    def write(row, value):
        m1_ref[base + row : base + row + 1, :] = value

    well_partials(x_ref, pick_ref, well_ref, wc_ref, xs_ref, g_ref, write)
    copies[3].wait()
    for r in range(PHASES):
        for t in range(PHASES):
            row_ref[0, r, t] = jac_ref[1, r, t, 0].astype(F32)
            row_ref[1, r, t] = jac_ref[2, r, t, rows - 1].astype(F32)
            for i in range(rows):
                col_ref[0, r, t, i : i + 1, :] = jac_ref[3, r, t, i, 0:8].astype(F32)[0:1]
                edge = jac_ref[4, r, t, i, cols - 8 : cols].astype(F32)
                col_ref[1, r, t, i : i + 1, :] = edge[7:8]
    edge_messages(flags, x_ref, row_ref, col_ref, m1_ref, m2_ref, m3_ref, m4_ref)
    copies[4].wait()
    inv_ref[...] = 1.0 / inv_ref[...]
    copies[5].wait()


def add_kernel(base, kept_ref, own_ref, got_ref, out_ref):
    out_ref[0:base, :] = kept_ref[...]
    out_ref[base:, :] = own_ref[base:, :] + got_ref[base:, :]


def inner_kernel(widen, x_ref, jac_ref, rhs_ref, z_ref, *rest):
    rows, cols = jac_ref.shape[3], jac_ref.shape[4]
    lane, col = iota((cols, LANES), 1), iota((cols, LANES), 0)

    def row_body(i, carry):
        before = jnp.where(i == 0, rows - 1, i - 1)
        after = jnp.where(i == rows - 1, 0, i + 1)
        open_row = {1: (after > 0).astype(F32), 2: (before < rows - 1).astype(F32)}
        shut_cell = {
            3: col == 0, 4: col == cols - 1, 5: lane == 0, 6: lane == LANES - 1
        }

        def load(row):
            start = pl.multiple_of(row * cols, cols)
            return [x_ref[r, pl.ds(start, cols), :] for r in range(PHASES)]

        def coefficient(d, r, t, row):
            if not widen:
                return jac_ref[d, r, t, row]
            value = jac_ref[d, r, t, row].astype(F32)
            if d in open_row:
                value = value * open_row[d]
            if d in shut_cell:
                value = jnp.where(shut_cell[d], 0.0, value)
            rest[0][d, r, t, row] = value
            return value

        def term(d, t, row, values):
            return sum(coefficient(d, r, t, row) * values[r] for r in range(PHASES))

        here, values_before, values_after = load(i), load(before), load(after)
        start = pl.multiple_of(i * cols, cols)
        for t in range(PHASES):
            total = term(0, t, i, here)
            total = total + term(1, t, after, values_after)
            total = total + term(2, t, before, values_before)
            total = total + pltpu.roll(term(3, t, i, here), cols - 1, 0)
            total = total + pltpu.roll(term(4, t, i, here), 1, 0)
            total = total + pltpu.roll(term(5, t, i, here), LANES - 1, 1)
            total = total + pltpu.roll(term(6, t, i, here), 1, 1)
            z_ref[t, pl.ds(start, cols), :] = rhs_ref[t, pl.ds(start, cols), :] - total
        return carry

    lax.fori_loop(0, rows, row_body, 0)


def update_kernel(
    last, flags, z_ref, own, g1, g2, g3, g4, wconst, inv_ref, spread_ref, well_ref, cc_ref,
    *rest,
):
    if last:
        x_out, adj_ref, rs_ref, c_ref, x_ref, sems = rest
    else:
        (row_ref, col_ref, pick_ref, wc_ref, x_ref, m1_ref, m2_ref, m3_ref, m4_ref,
         rs_ref, c_ref, xs_ref, g_ref) = rest
    cells, perfs = spread_ref.shape[0], spread_ref.shape[1] // 2
    rows = (own.shape[0] - WELL_UNK * well_ref.shape[0]) // PHASES
    cols = cells // rows
    base = PHASES * rows
    width = well_ref.shape[0]
    unk = WELL_UNK * width
    terms = own[base : base + unk, :] + g2[base : base + unk, :]
    left = wconst[0:unk, :] - terms
    solved = []
    for h in range(width):
        value = 0.0
        for v in range(WELL_UNK):
            at = unk + (h * WELL_UNK + v) * WELL_UNK
            at_v = h * WELL_UNK + v
            value = value + wconst[at : at + WELL_UNK, :] * left[at_v : at_v + 1, :]
        solved.append(value)
    if last:
        well_dev = adj_ref.shape[1]
        mine = 0.0
        for h in range(width):
            place = iota((LANES, well_dev), 1) + flags[4] * well_dev
            place = (place == iota((LANES, well_dev), 0) + h * LANES).astype(F32)
            mine = mine + jnp.dot(
                solved[h], place, precision=lax.Precision.HIGHEST, preferred_element_type=F32
            )
        adj_ref[...] = mine
    chunk = 64
    for start in range(0, perfs, chunk):
        part = slice(start, start + chunk)
        value = [0.0] * PHASES
        for u in range(WELL_UNK):
            chosen = sum(well_ref[h, part, :] * solved[h][u : u + 1, :] for h in range(width))
            factor = jnp.sum(chosen, axis=1, keepdims=True)
            for r in range(PHASES):
                value[r] = value[r] + cc_ref[u, r, part].astype(F32) * factor
        for r in range(PHASES):
            high, low = split_2(value[r])
            rs_ref[start : start + chunk, r * LANES : (r + 1) * LANES] = high
            rs_ref[perfs + start : perfs + start + chunk, r * LANES : (r + 1) * LANES] = low
    c_ref[...] = jnp.dot(spread_ref[...], rs_ref[...], preferred_element_type=F32)
    gx_odd, gy_odd = flags[0] == 1, flags[1] == 1
    gx_open, gy_open = flags[2].astype(F32), flags[3].astype(F32)
    for t in range(PHASES):
        x_ref[t] = (z_ref[t] - c_ref[:, t * LANES : (t + 1) * LANES]) * inv_ref[t]
    copies = []
    for t in range(PHASES):
        near, far = g3[t * cols : (t + 1) * cols, :], g4[t * cols : (t + 1) * cols, :] * gx_open
        first, final = slice(0, cols), slice((rows - 1) * cols, rows * cols)
        x_ref[t, first, :] = x_ref[t, first, :] - inv_ref[t, first, :] * jnp.where(gx_odd, near, far)
        x_ref[t, final, :] = x_ref[t, final, :] - inv_ref[t, final, :] * jnp.where(gx_odd, far, near)
        near, far = g1[t * rows : (t + 1) * rows, :], g2[t * rows : (t + 1) * rows, :] * gy_open
        first, final = pl.ds(0, rows, stride=cols), pl.ds(cols - 1, rows, stride=cols)
        x_ref[t, first, :] = x_ref[t, first, :] - inv_ref[t, first, :] * jnp.where(gy_odd, near, far)
        x_ref[t, final, :] = x_ref[t, final, :] - inv_ref[t, final, :] * jnp.where(gy_odd, far, near)
        if last:
            copies.append(pltpu.make_async_copy(x_ref.at[t], x_out.at[t], sems.at[t]))
            copies[t].start()
    for copy in copies:
        copy.wait()
    if not last:
        edge_messages(flags, x_ref, row_ref, col_ref, m1_ref, m2_ref, m3_ref, m4_ref)

        def write(row, value):
            m1_ref[base + row : base + row + 1, :] = value

        well_partials(x_ref, pick_ref, well_ref, wc_ref, xs_ref, g_ref, write)


def gx_swap(gx, gy, parity):
    pairs = []
    for i in range(gx):
        k = i ^ 1 if parity == 0 else ((i + 1) ^ 1) - 1
        for j in range(gy):
            pairs.append((i * gy + j, k * gy + j if 0 <= k < gx else i * gy + (j ^ 1)))
    return pairs


def gy_swap(gy, parity):
    if parity == 0:
        return [(j, j ^ 1) for j in range(gy)]
    return [(j, (((j + 1) ^ 1) - 1) % gy) for j in range(gy)]


def in_hbm(value):
    return pltpu.with_memory_space_constraint(value, pltpu.MemorySpace.HBM)


def shape(*dims, dtype=F32):
    return jax.ShapeDtypeStruct(dims, dtype)


def body(
    adjoint_init, adjoint_rhs, jacobian, cell_diag, perf_owner, perf_well, perf_block,
    well_coupling, cell_coupling, well_rhs, well_inverse,
):
    gx, gy = lax.axis_size("gx"), lax.axis_size("gy")
    ix, iy = lax.axis_index("gx"), lax.axis_index("gy")
    phases, rows, cols, layers = adjoint_init.shape
    cells = rows * cols
    perfs = perf_well.shape[0]
    well_dev = well_rhs.shape[1]
    width = gy * well_dev // LANES
    unk = WELL_UNK * width
    base = PHASES * rows
    both = ("gx", "gy")
    flags = jnp.stack(
        [
            ix % 2,
            iy % 2,
            jnp.where(ix % 2 == 1, ix < gx - 1, ix > 0).astype(jnp.int32),
            jnp.where(iy % 2 == 1, iy < gy - 1, iy > 0).astype(jnp.int32),
            iy,
        ]
    ).astype(jnp.int32)
    x = adjoint_init.reshape(phases, cells, layers)
    rhs = adjoint_rhs.reshape(phases, cells, layers)
    diag = cell_diag.reshape(phases, cells, layers)
    full = base + unk
    grid = shape(phases, cells, layers)
    jac_shape = shape(*jacobian.shape, dtype=BF16)
    first = pl.pallas_call(
        first_kernel,
        out_shape=(
            grid,
            jac_shape,
            grid,
            grid,
            shape(2, PHASES, PHASES, cols, LANES),
            shape(2, PHASES, PHASES, rows, LANES),
            shape(perfs, 2 * cells, dtype=BF16),
            shape(cells, 2 * perfs, dtype=BF16),
            shape(width, perfs, LANES),
            shape(WELL_UNK, PHASES, perfs, LANES, dtype=BF16),
            shape(WELL_UNK, PHASES, perfs, LANES, dtype=BF16),
            shape(full + 5 * unk, LANES),
            shape(base, LANES),
            shape(PHASES * cols, LANES),
            shape(PHASES * cols, LANES),
        ),
        in_specs=[SM] + [HB] * 11,
        out_specs=(VM,) * 15,
        scratch_shapes=[
            pltpu.VMEM(well_coupling.shape, BF16),
            pltpu.VMEM(cell_coupling.shape, BF16),
            pltpu.VMEM((2 * cells, PHASES * LANES), BF16),
            pltpu.VMEM((perfs, PHASES * LANES), F32),
            pltpu.VMEM((1, perfs), jnp.int32),
            pltpu.VMEM((1, perfs), jnp.int32),
            pltpu.VMEM((1, perfs), jnp.int32),
            pltpu.VMEM(well_rhs.shape, F32),
            pltpu.VMEM(well_inverse.shape, F32),
            pltpu.SemaphoreType.DMA((6,)),
            pltpu.SemaphoreType.DMA((5,)),
        ],
        compiler_params=PARAMS,
        name="first",
    )
    (x, jac, rhs, inv, row_edges, col_edges, pick, spread, well_hot, wc, cc, m1, m2_halo, m3,
     m4) = first(
        flags,
        *[
            in_hbm(v)
            for v in (
                x, jacobian, rhs, diag, well_coupling, cell_coupling,
                perf_block.reshape(1, perfs), perf_well.reshape(1, perfs),
                perf_owner.reshape(1, perfs), well_rhs, well_inverse,
            )
        ],
    )

    def add(kept, own, got):
        return pl.pallas_call(
            functools.partial(add_kernel, base),
            out_shape=shape(*own.shape),
            in_specs=[VM] * 3,
            out_specs=VM,
            compiler_params=PARAMS,
            name="add",
        )(kept, own, got)

    def inner(x, jac, rhs, widen):
        wide = (shape(*jac.shape),) if widen else ()
        return pl.pallas_call(
            functools.partial(inner_kernel, widen),
            out_shape=(grid,) + wide,
            in_specs=[VM] * 3,
            out_specs=(VM,) * (1 + len(wide)),
            compiler_params=PARAMS,
            name="inner_widen" if widen else "inner",
        )(x, jac, rhs)

    work = [
        pltpu.VMEM((2 * perfs, PHASES * LANES), BF16),
        pltpu.VMEM((cells, PHASES * LANES), F32),
    ]
    for sweep in range(ITERS):
        last = sweep == ITERS - 1
        g1 = lax.ppermute(m1, "gy", gy_swap(gy, 0))
        g3 = lax.ppermute(m3, both, gx_swap(gx, gy, 0))
        g4 = lax.ppermute(m4, both, gx_swap(gx, gy, 1))
        own = add(m2_halo, m1, g1)
        g2 = lax.ppermute(own, "gy", gy_swap(gy, 1))
        hop = 4
        while hop < gy:
            own = jnp.concatenate([own[:base], own[base:] + g2[base:]], axis=0)
            far = lax.ppermute(own[base:], "gy", [(j, (j + hop) % gy) for j in range(gy)])
            g2 = jnp.concatenate([g2[:base], far], axis=0)
            hop *= 2
        if sweep == 0:
            wconst = own[full:] + g2[full:]
            own, g1, g2 = own[:full], g1[:full], g2[:full]
        if sweep == 0:
            z, jac = inner(x, jac, rhs, True)
        else:
            (z,) = inner(x, jac, rhs, False)
        operands = (flags, z, own, g1, g2, g3, g4, wconst, inv, spread, well_hot, cc)
        if last:
            x, adj = pl.pallas_call(
                functools.partial(update_kernel, True),
                out_shape=(grid, shape(*well_rhs.shape)),
                in_specs=[SM] + [VM] * 11,
                out_specs=(HB, VM),
                scratch_shapes=work
                + [
                    pltpu.VMEM((phases, cells, layers), F32),
                    pltpu.SemaphoreType.DMA((PHASES,)),
                ],
                compiler_params=PARAMS,
                name="update_last",
            )(*operands)
        else:
            x, m1, m2_halo, m3, m4 = pl.pallas_call(
                functools.partial(update_kernel, False),
                out_shape=(
                    shape(phases, cells, layers),
                    shape(full, LANES),
                    shape(base, LANES),
                    shape(PHASES * cols, LANES),
                    shape(PHASES * cols, LANES),
                ),
                in_specs=[SM] + [VM] * 15,
                out_specs=(VM,) * 5,
                scratch_shapes=work
                + [
                    pltpu.VMEM((2 * cells, PHASES * LANES), BF16),
                    pltpu.VMEM((perfs, PHASES * LANES), F32),
                ],
                compiler_params=PARAMS,
                name="update",
            )(*operands, row_edges, col_edges, pick, wc)
    return x.reshape(adjoint_init.shape), adj


def solution(mesh):
    in_specs = (
        P(None, "gx", "gy", None),
        P(None, "gx", "gy", None),
        P(None, None, None, "gx", "gy", None),
        P(None, "gx", "gy", None),
        P(("gx", "gy"), None),
        P(("gx", "gy")),
        P(("gx", "gy")),
        P(None, None, ("gx", "gy")),
        P(None, None, ("gx", "gy")),
        P(None, ("gx", "gy")),
        P(None, None, ("gx", "gy")),
    )
    out_specs = (P(None, "gx", "gy", None), P(None, ("gx", "gy")))
    return jax.shard_map(body, mesh=mesh, in_specs=in_specs, out_specs=out_specs, check_vma=False)
```

time: 90.1 us -> 79 us (0.88)
  local copies, waits for them, and re-layouts: 15.4 us -> 0.1 us
  Pallas kernels: 35.5 us -> 39.6 us
  waiting for transfers between devices: 5.59 us -> 9.08 us
  other arithmetic: 2.18 us -> 0.01 us
    unnamed x26 -> x0, local copies, waits for them, and re-layouts: 13.6 us -> none
    pallas_call x10, Pallas kernels: 21 us -> 24.9 us  [the longest x8 15.1 us: inner(): pl.pallas_call(functools.partial(inner_kernel, widen), out_shape=(grid,)...]
    ppermute x8, waiting for transfers between devices: 4.43 us -> 7.95 us  [body(): g2 = lax.ppermute(own, 'gy', gy_swap(gy, 1))]
    ppermute x8, starting transfers between devices: 6.46 us -> 5.39 us  [body(): g2 = lax.ppermute(own, 'gy', gy_swap(gy, 1))]
    reshape x2 -> x0, local copies, waits for them, and re-layouts: 0.95 us -> none  [the longest x1 0.81 us: body(): perf_block.reshape(perfs, 1)]
  transfers between devices with their start and end apart: 32 -> 32, of which waited for: 8 -> 9; matrix products, arithmetic and copies ran while one was open for 0% -> 0% of each run, Pallas kernels for 18% -> 19%
where the time goes in v1:
time: 79 us; the launch traced here: 78.9 us
  Pallas kernels  39.6 us (50%)
  starting transfers between devices  29 us (37%)
  waiting for transfers between devices  9.08 us (11%)
  between operations  1.06 us (1%)
    ppermute x8, starting transfers between devices, body(): g3 = lax.ppermute(m3, both, gx_swap(gx, gy, 0))  19.1 us
    pallas_call x8, Pallas kernels, inner(): pl.pallas_call(functools.partial(inner_kernel, widen), out_shape=(grid,)...  15.1 us
    pallas_call x7, Pallas kernels, body(): pl.pallas_call(functools.partial(update_kernel, False), out_shape=(shape(...  14.7 us
    ppermute x8, waiting for transfers between devices, body(): g2 = lax.ppermute(own, 'gy', gy_swap(gy, 1))  7.95 us
    pallas_call x1, Pallas kernels, body(): first(flags, *[in_hbm(v) for v in (x, jacobian, rhs, diag, well_coupling,...  7.02 us
    ppermute x8, starting transfers between devices, body(): g2 = lax.ppermute(own, 'gy', gy_swap(gy, 1))  5.39 us
    ppermute x8, starting transfers between devices, body(): g1 = lax.ppermute(m1, 'gy', gy_swap(gy, 0))  3.45 us
    pallas_call x1, Pallas kernels, body(): pl.pallas_call(functools.partial(update_kernel, True), out_shape=(grid, s...  2.81 us
  transfers between devices with their start and end apart: 32, of which 9 were waited for; matrix products, arithmetic and copies ran while one was open for 0% of the time, Pallas kernels for 19%

profile of v1, /device:TPU:0, one launch (start us, length us, event | category | flops | bytes accessed | tf_op | source)
XLA Modules:
  0.0 78.9 jit_solution(15724411102531721291)
XLA Ops:
  0.7 7.0 %first.1 = (f32[3,512,128]{2,1,0:T(8,128)S(1)}, bf16[7,3,3,16,32,128]{5,4,3,2,1,0:T(8,128)(2,1)S(1)}, f32[3,512,128]{2,1,0:T(8,128)S(1)}, f32[3,512,128]{2,1,0:T...) custom-call(s32[5]{0:T(128)S(1)} %stack.31.flags, ...), custom_call_target="tpu_custom_call" | custom-call | tf_op jit(solution)/shard_map/first/pallas_call | solution.py:387
  9.2 2.6 %collective-permute-start.1 = (f32[72,128]{1,0:T(8,128)S(1)}, f32[72,128]{1,0:T(8,128)S(1)}, u32[]{:S(2)}, u32[]{:S(2)}) collective-permute-start(f32[72,128]{1,0:T(8,128)S(1)} %add.24), channel_id=1, source_target_pairs={{0,3},{1,2},{2,1},{3,0},{4,7},{5,6},{6,5},{7,4},{8,11},{9,10},{10,... | collective-permute-start | bytes 110600 | tf_op jit(solution)/shard_map/ppermute | solution.py:430
  11.8 1.5 %collective-permute-start.2 = (f32[96,128]{1,0:T(8,128)S(1)}, f32[96,128]{1,0:T(8,128)S(1)}, u32[]{:S(2)}, u32[]{:S(2)}) collective-permute-start(f32[96,128]{1,0:T(8,128)S(1)} %get-tuple-element.62), channel_id=1, source_target_pairs={{0,4},{1,5},{2,6},{3,7},{4,0},{5,1},{6,2},{7,3},{8,12},{9,13},{10,... | collective-permute-start | bytes 147464 | tf_op jit(solution)/shard_map/ppermute | solution.py:427
  13.3 2.9 %inner_widen.1 = (f32[3,512,128]{2,1,0:T(8,128)S(1)}, f32[7,3,3,16,32,128]{5,4,3,2,1,0:T(8,128)S(1)}) custom-call(f32[3,512,128]{2,1,0:T(8,128)S(1)} %get-tuple-element.56.x_ref, bf16[7,3,3,16,32,128]{5,4,3,2,1,0:T(8,128)(2,1)S(1)} %get-tuple-element.57.jac_ref, f32[3,512,128]{2,1,0:T(8,128)S(1)} %get-tuple-element.58.rhs_ref), custom_call_target="tpu_custom_call" | custom-call | tf_op jit(solution)/shard_map/inner_widen/pallas_call | solution.py:411
  16.3 2.1 %update.7 = (f32[3,512,128]{2,1,0:T(8,128)S(1)}, f32[52,128]{1,0:T(8,128)S(1)}, f32[48,128]{1,0:T(8,128)S(1)}, f32[96,128]{1,0:T(8,128)S(1)}, f32[96,128]{1,0:T(8,128)S(1)}) custom-call(s32[5]{0:T(128)S(1)} %stack.31.flags, f32[3,512,128]{2,1,0:T(8,128)S(1)} %get-tuple-element.59.z_ref, f32[52,128]{1,0:T(8,128)S(1)} %slice.20.own, f32[52,128]{1,0:T(8,128)S(1)} %slice.21.g1, ...), custom_call_target="tpu_custom_call" | custom-call | tf_op jit(solution)/shard_map/update/pallas_call | solution.py:460
  18.9 2.6 %collective-permute-start.6 = (f32[96,128]{1,0:T(8,128)S(1)}, f32[96,128]{1,0:T(8,128)S(1)}, u32[]{:S(2)}, u32[]{:S(2)}) collective-permute-start(f32[96,128]{1,0:T(8,128)S(1)} %get-tuple-element.76), channel_id=1, source_target_pairs={{0,4},{1,5},{2,6},{3,7},{4,0},{5,1},{6,2},{7,3},{8,12},{9,13},{10,... | collective-permute-start | bytes 147464 | tf_op jit(solution)/shard_map/ppermute | solution.py:427
  22.2 1.8 %inner.7.z_ref = f32[3,512,128]{2,1,0:T(8,128)S(1)} custom-call(f32[3,512,128]{2,1,0:T(8,128)S(1)} %get-tuple-element.72.x_ref, f32[7,3,3,16,32,128]{5,4,3,2,1,0:T(8,128)S(1)} %get-tuple-element.73.jac_ref, f32[3,512,128]{2,1,0:T(8,128)S(1)} %get-tuple-element.58.rhs_ref), custom_call_target="tpu_custom_call" | custom-call | tf_op jit(solution)/shard_map/inner/pallas_call | solution.py:411
  25.0 2.1 %update.8 = (f32[3,512,128]{2,1,0:T(8,128)S(1)}, f32[52,128]{1,0:T(8,128)S(1)}, f32[48,128]{1,0:T(8,128)S(1)}, f32[96,128]{1,0:T(8,128)S(1)}, f32[96,128]{1,0:T(8,128)S(1)}) custom-call(s32[5]{0:T(128)S(1)} %stack.31.flags, f32[3,512,128]{2,1,0:T(8,128)S(1)} %inner.7.z_ref, f32[52,128]{1,0:T(8,128)S(1)} %add.25.own, ...), custom_call_target="tpu_custom_call" | custom-call | tf_op jit(solution)/shard_map/update/pallas_call | solution.py:460
  27.5 2.9 %collective-permute-start.10 = (f32[96,128]{1,0:T(8,128)S(1)}, f32[96,128]{1,0:T(8,128)S(1)}, u32[]{:S(2)}, u32[]{:S(2)}) collective-permute-start(f32[96,128]{1,0:T(8,128)S(1)} %get-tuple-element.81), channel_id=1, source_target_pairs={{0,4},{1,5},{2,6},{3,7},{4,0},{5,1},{6,2},{7,3},{8,12},{9,13},{10,... | collective-permute-start | bytes 147464 | tf_op jit(solution)/shard_map/ppermute | solution.py:427
  31.0 1.7 %inner.8.z_ref = f32[3,512,128]{2,1,0:T(8,128)S(1)} custom-call(f32[3,512,128]{2,1,0:T(8,128)S(1)} %get-tuple-element.78.x_ref, f32[7,3,3,16,32,128]{5,4,3,2,1,0:T(8,128)S(1)} %get-tuple-element.73.jac_ref, f32[3,512,128]{2,1,0:T(8,128)S(1)} %get-tuple-element.58.rhs_ref), custom_call_target="tpu_custom_call" | custom-call | tf_op jit(solution)/shard_map/inner/pallas_call | solution.py:411
  32.8 1.1 %collective-permute-done.9.g2 = f32[52,128]{1,0:T(8,128)S(1)} collective-permute-done((f32[52,128]{1,0:T(8,128)S(1)}, f32[52,128]{1,0:T(8,128)S(1)}, u32[]{:S(2)}, u32[]{:S(2)}) %collective-permute-start.9) | collective-permute-done | bytes 26656 | tf_op jit(solution)/shard_map/ppermute | solution.py:430
  33.9 2.1 %update.9 = (f32[3,512,128]{2,1,0:T(8,128)S(1)}, f32[52,128]{1,0:T(8,128)S(1)}, f32[48,128]{1,0:T(8,128)S(1)}, f32[96,128]{1,0:T(8,128)S(1)}, f32[96,128]{1,0:T(8,128)S(1)}) custom-call(s32[5]{0:T(128)S(1)} %stack.31.flags, f32[3,512,128]{2,1,0:T(8,128)S(1)} %inner.8.z_ref, f32[52,128]{1,0:T(8,128)S(1)} %add.26.own, ...), custom_call_target="tpu_custom_call" | custom-call | tf_op jit(solution)/shard_map/update/pallas_call | solution.py:460
  36.4 2.9 %collective-permute-start.14 = (f32[96,128]{1,0:T(8,128)S(1)}, f32[96,128]{1,0:T(8,128)S(1)}, u32[]{:S(2)}, u32[]{:S(2)}) collective-permute-start(f32[96,128]{1,0:T(8,128)S(1)} %get-tuple-element.86), channel_id=1, source_target_pairs={{0,4},{1,5},{2,6},{3,7},{4,0},{5,1},{6,2},{7,3},{8,12},{9,13},{10,... | collective-permute-start | bytes 147464 | tf_op jit(solution)/shard_map/ppermute | solution.py:427
  39.9 1.7 %inner.9.z_ref = f32[3,512,128]{2,1,0:T(8,128)S(1)} custom-call(f32[3,512,128]{2,1,0:T(8,128)S(1)} %get-tuple-element.83.x_ref, f32[7,3,3,16,32,128]{5,4,3,2,1,0:T(8,128)S(1)} %get-tuple-element.73.jac_ref, f32[3,512,128]{2,1,0:T(8,128)S(1)} %get-tuple-element.58.rhs_ref), custom_call_target="tpu_custom_call" | custom-call | tf_op jit(solution)/shard_map/inner/pallas_call | solution.py:411
  41.7 1.1 %collective-permute-done.13.g2 = f32[52,128]{1,0:T(8,128)S(1)} collective-permute-done((f32[52,128]{1,0:T(8,128)S(1)}, f32[52,128]{1,0:T(8,128)S(1)}, u32[]{:S(2)}, u32[]{:S(2)}) %collective-permute-start.13) | collective-permute-done | bytes 26656 | tf_op jit(solution)/shard_map/ppermute | solution.py:430
  42.8 2.1 %update.10 = (f32[3,512,128]{2,1,0:T(8,128)S(1)}, f32[52,128]{1,0:T(8,128)S(1)}, f32[48,128]{1,0:T(8,128)S(1)}, f32[96,128]{1,0:T(8,128)S(1)}, f32[96,128]{1,0:T(8,128)S(1)}) custom-call(s32[5]{0:T(128)S(1)} %stack.31.flags, f32[3,512,128]{2,1,0:T(8,128)S(1)} %inner.9.z_ref, f32[52,128]{1,0:T(8,128)S(1)} %add.27.own, ...), custom_call_target="tpu_custom_call" | custom-call | tf_op jit(solution)/shard_map/update/pallas_call | solution.py:460
  45.3 2.3 %collective-permute-start.18 = (f32[96,128]{1,0:T(8,128)S(1)}, f32[96,128]{1,0:T(8,128)S(1)}, u32[]{:S(2)}, u32[]{:S(2)}) collective-permute-start(f32[96,128]{1,0:T(8,128)S(1)} %get-tuple-element.91), channel_id=1, source_target_pairs={{0,4},{1,5},{2,6},{3,7},{4,0},{5,1},{6,2},{7,3},{8,12},{9,13},{10,... | collective-permute-start | bytes 147464 | tf_op jit(solution)/shard_map/ppermute | solution.py:427
  48.1 1.7 %inner.10.z_ref = f32[3,512,128]{2,1,0:T(8,128)S(1)} custom-call(f32[3,512,128]{2,1,0:T(8,128)S(1)} %get-tuple-element.88.x_ref, f32[7,3,3,16,32,128]{5,4,3,2,1,0:T(8,128)S(1)} %get-tuple-element.73.jac_ref, f32[3,512,128]{2,1,0:T(8,128)S(1)} %get-tuple-element.58.rhs_ref), custom_call_target="tpu_custom_call" | custom-call | tf_op jit(solution)/shard_map/inner/pallas_call | solution.py:411
  49.9 1.2 %collective-permute-done.17.g2 = f32[52,128]{1,0:T(8,128)S(1)} collective-permute-done((f32[52,128]{1,0:T(8,128)S(1)}, f32[52,128]{1,0:T(8,128)S(1)}, u32[]{:S(2)}, u32[]{:S(2)}) %collective-permute-start.17) | collective-permute-done | bytes 26656 | tf_op jit(solution)/shard_map/ppermute | solution.py:430
  51.1 2.1 %update.11 = (f32[3,512,128]{2,1,0:T(8,128)S(1)}, f32[52,128]{1,0:T(8,128)S(1)}, f32[48,128]{1,0:T(8,128)S(1)}, f32[96,128]{1,0:T(8,128)S(1)}, f32[96,128]{1,0:T(8,128)S(1)}) custom-call(s32[5]{0:T(128)S(1)} %stack.31.flags, f32[3,512,128]{2,1,0:T(8,128)S(1)} %inner.10.z_ref, f32[52,128]{1,0:T(8,128)S(1)} %add.28.own, ...), custom_call_target="tpu_custom_call" | custom-call | tf_op jit(solution)/shard_map/update/pallas_call | solution.py:460
  53.6 2.3 %collective-permute-start.22 = (f32[96,128]{1,0:T(8,128)S(1)}, f32[96,128]{1,0:T(8,128)S(1)}, u32[]{:S(2)}, u32[]{:S(2)}) collective-permute-start(f32[96,128]{1,0:T(8,128)S(1)} %get-tuple-element.96), channel_id=1, source_target_pairs={{0,4},{1,5},{2,6},{3,7},{4,0},{5,1},{6,2},{7,3},{8,12},{9,13},{10,... | collective-permute-start | bytes 147464 | tf_op jit(solution)/shard_map/ppermute | solution.py:427
  56.4 1.7 %inner.11.z_ref = f32[3,512,128]{2,1,0:T(8,128)S(1)} custom-call(f32[3,512,128]{2,1,0:T(8,128)S(1)} %get-tuple-element.93.x_ref, f32[7,3,3,16,32,128]{5,4,3,2,1,0:T(8,128)S(1)} %get-tuple-element.73.jac_ref, f32[3,512,128]{2,1,0:T(8,128)S(1)} %get-tuple-element.58.rhs_ref), custom_call_target="tpu_custom_call" | custom-call | tf_op jit(solution)/shard_map/inner/pallas_call | solution.py:411
  58.1 1.2 %collective-permute-done.21.g2 = f32[52,128]{1,0:T(8,128)S(1)} collective-permute-done((f32[52,128]{1,0:T(8,128)S(1)}, f32[52,128]{1,0:T(8,128)S(1)}, u32[]{:S(2)}, u32[]{:S(2)}) %collective-permute-start.21) | collective-permute-done | bytes 26656 | tf_op jit(solution)/shard_map/ppermute | solution.py:430
  59.3 2.1 %update.12 = (f32[3,512,128]{2,1,0:T(8,128)S(1)}, f32[52,128]{1,0:T(8,128)S(1)}, f32[48,128]{1,0:T(8,128)S(1)}, f32[96,128]{1,0:T(8,128)S(1)}, f32[96,128]{1,0:T(8,128)S(1)}) custom-call(s32[5]{0:T(128)S(1)} %stack.31.flags, f32[3,512,128]{2,1,0:T(8,128)S(1)} %inner.11.z_ref, f32[52,128]{1,0:T(8,128)S(1)} %add.29.own, ...), custom_call_target="tpu_custom_call" | custom-call | tf_op jit(solution)/shard_map/update/pallas_call | solution.py:460
  61.8 2.3 %collective-permute-start.26 = (f32[96,128]{1,0:T(8,128)S(1)}, f32[96,128]{1,0:T(8,128)S(1)}, u32[]{:S(2)}, u32[]{:S(2)}) collective-permute-start(f32[96,128]{1,0:T(8,128)S(1)} %get-tuple-element.101), channel_id=1, source_target_pairs={{0,4},{1,5},{2,6},{3,7},{4,0},{5,1},{6,2},{7,3},{8,12},{9,13},{10,... | collective-permute-start | bytes 147464 | tf_op jit(solution)/shard_map/ppermute | solution.py:427
  64.6 1.7 %inner.12.z_ref = f32[3,512,128]{2,1,0:T(8,128)S(1)} custom-call(f32[3,512,128]{2,1,0:T(8,128)S(1)} %get-tuple-element.98.x_ref, f32[7,3,3,16,32,128]{5,4,3,2,1,0:T(8,128)S(1)} %get-tuple-element.73.jac_ref, f32[3,512,128]{2,1,0:T(8,128)S(1)} %get-tuple-element.58.rhs_ref), custom_call_target="tpu_custom_call" | custom-call | tf_op jit(solution)/shard_map/inner/pallas_call | solution.py:411
  66.4 1.2 %collective-permute-done.25.g2 = f32[52,128]{1,0:T(8,128)S(1)} collective-permute-done((f32[52,128]{1,0:T(8,128)S(1)}, f32[52,128]{1,0:T(8,128)S(1)}, u32[]{:S(2)}, u32[]{:S(2)}) %collective-permute-start.25) | collective-permute-done | bytes 26656 | tf_op jit(solution)/shard_map/ppermute | solution.py:430
  67.6 2.1 %update.13 = (f32[3,512,128]{2,1,0:T(8,128)S(1)}, f32[52,128]{1,0:T(8,128)S(1)}, f32[48,128]{1,0:T(8,128)S(1)}, f32[96,128]{1,0:T(8,128)S(1)}, f32[96,128]{1,0:T(8,128)S(1)}) custom-call(s32[5]{0:T(128)S(1)} %stack.31.flags, f32[3,512,128]{2,1,0:T(8,128)S(1)} %inner.12.z_ref, f32[52,128]{1,0:T(8,128)S(1)} %add.30.own, ...), custom_call_target="tpu_custom_call" | custom-call | tf_op jit(solution)/shard_map/update/pallas_call | solution.py:460
  70.1 2.3 %collective-permute-start.30 = (f32[96,128]{1,0:T(8,128)S(1)}, f32[96,128]{1,0:T(8,128)S(1)}, u32[]{:S(2)}, u32[]{:S(2)}) collective-permute-start(f32[96,128]{1,0:T(8,128)S(1)} %get-tuple-element.106), channel_id=1, source_target_pairs={{0,4},{1,5},{2,6},{3,7},{4,0},{5,1},{6,2},{7,3},{8,12},{9,13},{10,... | collective-permute-start | bytes 147464 | tf_op jit(solution)/shard_map/ppermute | solution.py:427
  72.8 1.7 %inner.13.z_ref = f32[3,512,128]{2,1,0:T(8,128)S(1)} custom-call(f32[3,512,128]{2,1,0:T(8,128)S(1)} %get-tuple-element.103.x_ref, f32[7,3,3,16,32,128]{5,4,3,2,1,0:T(8,128)S(1)} %get-tuple-element.73.jac_ref, f32[3,512,128]{2,1,0:T(8,128)S(1)} %get-tuple-element.58.rhs_ref), custom_call_target="tpu_custom_call" | custom-call | tf_op jit(solution)/shard_map/inner/pallas_call | solution.py:411
  74.7 1.2 %collective-permute-done.29.g2 = f32[52,128]{1,0:T(8,128)S(1)} collective-permute-done((f32[52,128]{1,0:T(8,128)S(1)}, f32[52,128]{1,0:T(8,128)S(1)}, u32[]{:S(2)}, u32[]{:S(2)}) %collective-permute-start.29) | collective-permute-done | bytes 26656 | tf_op jit(solution)/shard_map/ppermute | solution.py:430
  75.9 2.8 %update_last.1 = (f32[3,512,128]{2,1,0:T(8,128)}, f32[4,32]{1,0:T(4,128)}) custom-call(s32[5]{0:T(128)S(1)} %stack.31.flags, f32[3,512,128]{2,1,0:T(8,128)S(1)} %inner.13.z_ref, f32[52,128]{1,0:T(8,128)S(1)} %add.31.own, f32[52,128]{1,0:T(8,128)S(1)} %collective-permute-done.28.got_ref.g1, f32[52,128]{1,0:T(8,128)S(1)} %collective-permute-done.29.g2, ...), custom_call_target="tpu_custom_call" | custom-call | tf_op jit(solution)/shard_map/update_last/pallas_call | solution.py:446
  (62 shorter events, 9.6 us)
Async XLA Ops:
  7.8 1.4 %collective-permute-start = (f32[72,128]{1,0:T(8,128)S(1)}, f32[72,128]{1,0:T(8,128)S(1)}, u32[]{:S(2)}, u32[]{:S(2)}) collective-permute-start(f32[72,128]{1,0:T(8,128)S(1)} %get-tuple-element.61.own_ref), channel_id=1, source_target_pairs={{0,1},{1,0},{2,3},{3,2},{4,5},{5,4},{6,7},{7,6},{8,9},{9,8},{10,11... | collective-permute-start | bytes 110600 | tf_op jit(solution)/shard_map/ppermute | solution.py:426
  9.2 7.1 %collective-permute-start.1 = (f32[72,128]{1,0:T(8,128)S(1)}, f32[72,128]{1,0:T(8,128)S(1)}, u32[]{:S(2)}, u32[]{:S(2)}) collective-permute-start(f32[72,128]{1,0:T(8,128)S(1)} %add.24), channel_id=1, source_target_pairs={{0,3},{1,2},{2,1},{3,0},{4,7},{5,6},{6,5},{7,4},{8,11},{9,10},{10,... | collective-permute-start | bytes 110600 | tf_op jit(solution)/shard_map/ppermute | solution.py:430
  11.8 4.5 %collective-permute-start.2 = (f32[96,128]{1,0:T(8,128)S(1)}, f32[96,128]{1,0:T(8,128)S(1)}, u32[]{:S(2)}, u32[]{:S(2)}) collective-permute-start(f32[96,128]{1,0:T(8,128)S(1)} %get-tuple-element.62), channel_id=1, source_target_pairs={{0,4},{1,5},{2,6},{3,7},{4,0},{5,1},{6,2},{7,3},{8,12},{9,13},{10,... | collective-permute-start | bytes 147464 | tf_op jit(solution)/shard_map/ppermute | solution.py:427
  13.3 3.0 %collective-permute-start.3 = (f32[96,128]{1,0:T(8,128)S(1)}, f32[96,128]{1,0:T(8,128)S(1)}, u32[]{:S(2)}, u32[]{:S(2)}) collective-permute-start(f32[96,128]{1,0:T(8,128)S(1)} %get-tuple-element.63), channel_id=1, source_target_pairs={{0,1},{1,0},{2,3},{3,2},{4,8},{5,9},{6,10},{7,11},{8,4},{9,5},{10,... | collective-permute-start | bytes 147464 | tf_op jit(solution)/shard_map/ppermute | solution.py:428
  18.4 3.3 %collective-permute-start.4 = (f32[52,128]{1,0:T(8,128)S(1)}, f32[52,128]{1,0:T(8,128)S(1)}, u32[]{:S(2)}, u32[]{:S(2)}) collective-permute-start(f32[52,128]{1,0:T(8,128)S(1)} %get-tuple-element.75.own_ref), channel_id=1, source_target_pairs={{0,1},{1,0},{2,3},{3,2},{4,5},{5,4},{6,7},{7,6},{8,9},{9,8},{10,11... | collective-permute-start | bytes 79880 | tf_op jit(solution)/shard_map/ppermute | solution.py:426
  18.9 5.0 %collective-permute-start.6 = (f32[96,128]{1,0:T(8,128)S(1)}, f32[96,128]{1,0:T(8,128)S(1)}, u32[]{:S(2)}, u32[]{:S(2)}) collective-permute-start(f32[96,128]{1,0:T(8,128)S(1)} %get-tuple-element.76), channel_id=1, source_target_pairs={{0,4},{1,5},{2,6},{3,7},{4,0},{5,1},{6,2},{7,3},{8,12},{9,13},{10,... | collective-permute-start | bytes 147464 | tf_op jit(solution)/shard_map/ppermute | solution.py:427
  21.5 2.4 %collective-permute-start.7 = (f32[96,128]{1,0:T(8,128)S(1)}, f32[96,128]{1,0:T(8,128)S(1)}, u32[]{:S(2)}, u32[]{:S(2)}) collective-permute-start(f32[96,128]{1,0:T(8,128)S(1)} %get-tuple-element.77), channel_id=1, source_target_pairs={{0,1},{1,0},{2,3},{3,2},{4,8},{5,9},{6,10},{7,11},{8,4},{9,5},{10,... | collective-permute-start | bytes 147464 | tf_op jit(solution)/shard_map/ppermute | solution.py:428
  21.7 3.3 %collective-permute-start.5 = (f32[52,128]{1,0:T(8,128)S(1)}, f32[52,128]{1,0:T(8,128)S(1)}, u32[]{:S(2)}, u32[]{:S(2)}) collective-permute-start(f32[52,128]{1,0:T(8,128)S(1)} %add.25.own), channel_id=1, source_target_pairs={{0,3},{1,2},{2,1},{3,0},{4,7},{5,6},{6,5},{7,4},{8,11},{9,10},{10,... | collective-permute-start | bytes 79880 | tf_op jit(solution)/shard_map/ppermute | solution.py:430
  27.1 3.4 %collective-permute-start.8 = (f32[52,128]{1,0:T(8,128)S(1)}, f32[52,128]{1,0:T(8,128)S(1)}, u32[]{:S(2)}, u32[]{:S(2)}) collective-permute-start(f32[52,128]{1,0:T(8,128)S(1)} %get-tuple-element.80.own_ref), channel_id=1, source_target_pairs={{0,1},{1,0},{2,3},{3,2},{4,5},{5,4},{6,7},{7,6},{8,9},{9,8},{10,11... | collective-permute-start | bytes 79880 | tf_op jit(solution)/shard_map/ppermute | solution.py:426
  27.5 5.3 %collective-permute-start.10 = (f32[96,128]{1,0:T(8,128)S(1)}, f32[96,128]{1,0:T(8,128)S(1)}, u32[]{:S(2)}, u32[]{:S(2)}) collective-permute-start(f32[96,128]{1,0:T(8,128)S(1)} %get-tuple-element.81), channel_id=1, source_target_pairs={{0,4},{1,5},{2,6},{3,7},{4,0},{5,1},{6,2},{7,3},{8,12},{9,13},{10,... | collective-permute-start | bytes 147464 | tf_op jit(solution)/shard_map/ppermute | solution.py:427
  30.4 2.4 %collective-permute-start.11 = (f32[96,128]{1,0:T(8,128)S(1)}, f32[96,128]{1,0:T(8,128)S(1)}, u32[]{:S(2)}, u32[]{:S(2)}) collective-permute-start(f32[96,128]{1,0:T(8,128)S(1)} %get-tuple-element.82), channel_id=1, source_target_pairs={{0,1},{1,0},{2,3},{3,2},{4,8},{5,9},{6,10},{7,11},{8,4},{9,5},{10,... | collective-permute-start | bytes 147464 | tf_op jit(solution)/shard_map/ppermute | solution.py:428
  30.5 3.3 %collective-permute-start.9 = (f32[52,128]{1,0:T(8,128)S(1)}, f32[52,128]{1,0:T(8,128)S(1)}, u32[]{:S(2)}, u32[]{:S(2)}) collective-permute-start(f32[52,128]{1,0:T(8,128)S(1)} %add.26.own), channel_id=1, source_target_pairs={{0,3},{1,2},{2,1},{3,0},{4,7},{5,6},{6,5},{7,4},{8,11},{9,10},{10,... | collective-permute-start | bytes 79880 | tf_op jit(solution)/shard_map/ppermute | solution.py:430
  36.0 3.5 %collective-permute-start.12 = (f32[52,128]{1,0:T(8,128)S(1)}, f32[52,128]{1,0:T(8,128)S(1)}, u32[]{:S(2)}, u32[]{:S(2)}) collective-permute-start(f32[52,128]{1,0:T(8,128)S(1)} %get-tuple-element.85.own_ref), channel_id=1, source_target_pairs={{0,1},{1,0},{2,3},{3,2},{4,5},{5,4},{6,7},{7,6},{8,9},{9,8},{10,11... | collective-permute-start | bytes 79880 | tf_op jit(solution)/shard_map/ppermute | solution.py:426
  36.4 5.3 %collective-permute-start.14 = (f32[96,128]{1,0:T(8,128)S(1)}, f32[96,128]{1,0:T(8,128)S(1)}, u32[]{:S(2)}, u32[]{:S(2)}) collective-permute-start(f32[96,128]{1,0:T(8,128)S(1)} %get-tuple-element.86), channel_id=1, source_target_pairs={{0,4},{1,5},{2,6},{3,7},{4,0},{5,1},{6,2},{7,3},{8,12},{9,13},{10,... | collective-permute-start | bytes 147464 | tf_op jit(solution)/shard_map/ppermute | solution.py:427
  39.3 2.3 %collective-permute-start.15 = (f32[96,128]{1,0:T(8,128)S(1)}, f32[96,128]{1,0:T(8,128)S(1)}, u32[]{:S(2)}, u32[]{:S(2)}) collective-permute-start(f32[96,128]{1,0:T(8,128)S(1)} %get-tuple-element.87), channel_id=1, source_target_pairs={{0,1},{1,0},{2,3},{3,2},{4,8},{5,9},{6,10},{7,11},{8,4},{9,5},{10,... | collective-permute-start | bytes 147464 | tf_op jit(solution)/shard_map/ppermute | solution.py:428
  39.5 3.3 %collective-permute-start.13 = (f32[52,128]{1,0:T(8,128)S(1)}, f32[52,128]{1,0:T(8,128)S(1)}, u32[]{:S(2)}, u32[]{:S(2)}) collective-permute-start(f32[52,128]{1,0:T(8,128)S(1)} %add.27.own), channel_id=1, source_target_pairs={{0,3},{1,2},{2,1},{3,0},{4,7},{5,6},{6,5},{7,4},{8,11},{9,10},{10,... | collective-permute-start | bytes 79880 | tf_op jit(solution)/shard_map/ppermute | solution.py:430
  44.9 2.8 %collective-permute-start.16 = (f32[52,128]{1,0:T(8,128)S(1)}, f32[52,128]{1,0:T(8,128)S(1)}, u32[]{:S(2)}, u32[]{:S(2)}) collective-permute-start(f32[52,128]{1,0:T(8,128)S(1)} %get-tuple-element.90.own_ref), channel_id=1, source_target_pairs={{0,1},{1,0},{2,3},{3,2},{4,5},{5,4},{6,7},{7,6},{8,9},{9,8},{10,11... | collective-permute-start | bytes 79880 | tf_op jit(solution)/shard_map/ppermute | solution.py:426
  45.3 4.6 %collective-permute-start.18 = (f32[96,128]{1,0:T(8,128)S(1)}, f32[96,128]{1,0:T(8,128)S(1)}, u32[]{:S(2)}, u32[]{:S(2)}) collective-permute-start(f32[96,128]{1,0:T(8,128)S(1)} %get-tuple-element.91), channel_id=1, source_target_pairs={{0,4},{1,5},{2,6},{3,7},{4,0},{5,1},{6,2},{7,3},{8,12},{9,13},{10,... | collective-permute-start | bytes 147464 | tf_op jit(solution)/shard_map/ppermute | solution.py:427
  47.6 2.3 %collective-permute-start.19 = (f32[96,128]{1,0:T(8,128)S(1)}, f32[96,128]{1,0:T(8,128)S(1)}, u32[]{:S(2)}, u32[]{:S(2)}) collective-permute-start(f32[96,128]{1,0:T(8,128)S(1)} %get-tuple-element.92), channel_id=1, source_target_pairs={{0,1},{1,0},{2,3},{3,2},{4,8},{5,9},{6,10},{7,11},{8,4},{9,5},{10,... | collective-permute-start | bytes 147464 | tf_op jit(solution)/shard_map/ppermute | solution.py:428
  47.7 3.3 %collective-permute-start.17 = (f32[52,128]{1,0:T(8,128)S(1)}, f32[52,128]{1,0:T(8,128)S(1)}, u32[]{:S(2)}, u32[]{:S(2)}) collective-permute-start(f32[52,128]{1,0:T(8,128)S(1)} %add.28.own), channel_id=1, source_target_pairs={{0,3},{1,2},{2,1},{3,0},{4,7},{5,6},{6,5},{7,4},{8,11},{9,10},{10,... | collective-permute-start | bytes 79880 | tf_op jit(solution)/shard_map/ppermute | solution.py:430
  53.2 2.8 %collective-permute-start.20 = (f32[52,128]{1,0:T(8,128)S(1)}, f32[52,128]{1,0:T(8,128)S(1)}, u32[]{:S(2)}, u32[]{:S(2)}) collective-permute-start(f32[52,128]{1,0:T(8,128)S(1)} %get-tuple-element.95.own_ref), channel_id=1, source_target_pairs={{0,1},{1,0},{2,3},{3,2},{4,5},{5,4},{6,7},{7,6},{8,9},{9,8},{10,11... | collective-permute-start | bytes 79880 | tf_op jit(solution)/shard_map/ppermute | solution.py:426
  53.6 4.6 %collective-permute-start.22 = (f32[96,128]{1,0:T(8,128)S(1)}, f32[96,128]{1,0:T(8,128)S(1)}, u32[]{:S(2)}, u32[]{:S(2)}) collective-permute-start(f32[96,128]{1,0:T(8,128)S(1)} %get-tuple-element.96), channel_id=1, source_target_pairs={{0,4},{1,5},{2,6},{3,7},{4,0},{5,1},{6,2},{7,3},{8,12},{9,13},{10,... | collective-permute-start | bytes 147464 | tf_op jit(solution)/shard_map/ppermute | solution.py:427
  55.8 2.3 %collective-permute-start.23 = (f32[96,128]{1,0:T(8,128)S(1)}, f32[96,128]{1,0:T(8,128)S(1)}, u32[]{:S(2)}, u32[]{:S(2)}) collective-permute-start(f32[96,128]{1,0:T(8,128)S(1)} %get-tuple-element.97), channel_id=1, source_target_pairs={{0,1},{1,0},{2,3},{3,2},{4,8},{5,9},{6,10},{7,11},{8,4},{9,5},{10,... | collective-permute-start | bytes 147464 | tf_op jit(solution)/shard_map/ppermute | solution.py:428
  56.0 3.3 %collective-permute-start.21 = (f32[52,128]{1,0:T(8,128)S(1)}, f32[52,128]{1,0:T(8,128)S(1)}, u32[]{:S(2)}, u32[]{:S(2)}) collective-permute-start(f32[52,128]{1,0:T(8,128)S(1)} %add.29.own), channel_id=1, source_target_pairs={{0,3},{1,2},{2,1},{3,0},{4,7},{5,6},{6,5},{7,4},{8,11},{9,10},{10,... | collective-permute-start | bytes 79880 | tf_op jit(solution)/shard_map/ppermute | solution.py:430
  61.4 2.8 %collective-permute-start.24 = (f32[52,128]{1,0:T(8,128)S(1)}, f32[52,128]{1,0:T(8,128)S(1)}, u32[]{:S(2)}, u32[]{:S(2)}) collective-permute-start(f32[52,128]{1,0:T(8,128)S(1)} %get-tuple-element.100.own_ref), channel_id=1, source_target_pairs={{0,1},{1,0},{2,3},{3,2},{4,5},{5,4},{6,7},{7,6},{8,9},{9,8},{10,11... | collective-permute-start | bytes 79880 | tf_op jit(solution)/shard_map/ppermute | solution.py:426
  61.8 4.6 %collective-permute-start.26 = (f32[96,128]{1,0:T(8,128)S(1)}, f32[96,128]{1,0:T(8,128)S(1)}, u32[]{:S(2)}, u32[]{:S(2)}) collective-permute-start(f32[96,128]{1,0:T(8,128)S(1)} %get-tuple-element.101), channel_id=1, source_target_pairs={{0,4},{1,5},{2,6},{3,7},{4,0},{5,1},{6,2},{7,3},{8,12},{9,13},{10,... | collective-permute-start | bytes 147464 | tf_op jit(solution)/shard_map/ppermute | solution.py:427
  64.1 2.3 %collective-permute-start.27 = (f32[96,128]{1,0:T(8,128)S(1)}, f32[96,128]{1,0:T(8,128)S(1)}, u32[]{:S(2)}, u32[]{:S(2)}) collective-permute-start(f32[96,128]{1,0:T(8,128)S(1)} %get-tuple-element.102), channel_id=1, source_target_pairs={{0,1},{1,0},{2,3},{3,2},{4,8},{5,9},{6,10},{7,11},{8,4},{9,5},{10,... | collective-permute-start | bytes 147464 | tf_op jit(solution)/shard_map/ppermute | solution.py:428
  64.2 3.4 %collective-permute-start.25 = (f32[52,128]{1,0:T(8,128)S(1)}, f32[52,128]{1,0:T(8,128)S(1)}, u32[]{:S(2)}, u32[]{:S(2)}) collective-permute-start(f32[52,128]{1,0:T(8,128)S(1)} %add.30.own), channel_id=1, source_target_pairs={{0,3},{1,2},{2,1},{3,0},{4,7},{5,6},{6,5},{7,4},{8,11},{9,10},{10,... | collective-permute-start | bytes 79880 | tf_op jit(solution)/shard_map/ppermute | solution.py:430
  69.7 2.9 %collective-permute-start.28 = (f32[52,128]{1,0:T(8,128)S(1)}, f32[52,128]{1,0:T(8,128)S(1)}, u32[]{:S(2)}, u32[]{:S(2)}) collective-permute-start(f32[52,128]{1,0:T(8,128)S(1)} %get-tuple-element.105.own_ref), channel_id=1, source_target_pairs={{0,1},{1,0},{2,3},{3,2},{4,5},{5,4},{6,7},{7,6},{8,9},{9,8},{10,11... | collective-permute-start | bytes 79880 | tf_op jit(solution)/shard_map/ppermute | solution.py:426
  70.1 4.6 %collective-permute-start.30 = (f32[96,128]{1,0:T(8,128)S(1)}, f32[96,128]{1,0:T(8,128)S(1)}, u32[]{:S(2)}, u32[]{:S(2)}) collective-permute-start(f32[96,128]{1,0:T(8,128)S(1)} %get-tuple-element.106), channel_id=1, source_target_pairs={{0,4},{1,5},{2,6},{3,7},{4,0},{5,1},{6,2},{7,3},{8,12},{9,13},{10,... | collective-permute-start | bytes 147464 | tf_op jit(solution)/shard_map/ppermute | solution.py:427
  72.4 2.3 %collective-permute-start.31 = (f32[96,128]{1,0:T(8,128)S(1)}, f32[96,128]{1,0:T(8,128)S(1)}, u32[]{:S(2)}, u32[]{:S(2)}) collective-permute-start(f32[96,128]{1,0:T(8,128)S(1)} %get-tuple-element.107), channel_id=1, source_target_pairs={{0,1},{1,0},{2,3},{3,2},{4,8},{5,9},{6,10},{7,11},{8,4},{9,5},{10,... | collective-permute-start | bytes 147464 | tf_op jit(solution)/shard_map/ppermute | solution.py:428
  72.6 3.3 %collective-permute-start.29 = (f32[52,128]{1,0:T(8,128)S(1)}, f32[52,128]{1,0:T(8,128)S(1)}, u32[]{:S(2)}, u32[]{:S(2)}) collective-permute-start(f32[52,128]{1,0:T(8,128)S(1)} %add.31.own), channel_id=1, source_target_pairs={{0,3},{1,2},{2,1},{3,0},{4,7},{5,6},{6,5},{7,4},{8,11},{9,10},{10,... | collective-permute-start | bytes 79880 | tf_op jit(solution)/shard_map/ppermute | solution.py:430

commit v2 on v1

--- a/solution.py
+++ b/solution.py
@@ -43,20 +43,22 @@
         m2_ref[t * rows : (t + 1) * rows, :] = jnp.where(gy_odd, right, left)
 
 
-def well_partials(x_ref, pick_ref, well_ref, wc_ref, xs_ref, g_ref, write):
-    cells = x_ref.shape[1]
+def picked_rows(r, x_ref, pick_ref, xs_ref, g_ref):
+    high, low = split_2(x_ref[r])
+    xs_ref[r, :, 0:LANES] = high
+    xs_ref[r, :, LANES : 2 * LANES] = low
+    both = jnp.dot(pick_ref[...], xs_ref[r], preferred_element_type=F32)
+    g_ref[r] = both[:, 0:LANES] + both[:, LANES:]
+
+
+def well_partials(pick_ref, well_ref, wc_ref, g_ref, write):
     perfs = pick_ref.shape[0]
-    for r in range(PHASES):
-        high, low = split_2(x_ref[r])
-        xs_ref[0:cells, r * LANES : (r + 1) * LANES] = high
-        xs_ref[cells : 2 * cells, r * LANES : (r + 1) * LANES] = low
-    g_ref[...] = jnp.dot(pick_ref[...], xs_ref[...], preferred_element_type=F32)
     width = well_ref.shape[0]
     chunk = 64
     totals = [[jnp.zeros((8, LANES), F32) for _ in range(width)] for _ in range(WELL_UNK)]
     for start in range(0, perfs, chunk):
         rows = slice(start, start + chunk)
-        picked = [g_ref[rows, r * LANES : (r + 1) * LANES] for r in range(PHASES)]
+        picked = [g_ref[r, rows, :] for r in range(PHASES)]
         for u in range(WELL_UNK):
             lane_terms = sum(wc_ref[u, r, rows].astype(F32) * picked[r] for r in range(PHASES))
             term = jnp.sum(lane_terms, axis=1, keepdims=True)
@@ -92,8 +94,10 @@
     block_in, well_in, owner_in, rhs_well_in, inv_well_in,
     x_ref, jac_ref, rhs_ref, inv_ref, row_ref, col_ref, pick_ref, spread_ref, well_ref, wc_ref,
     cc_ref, m1_ref, m2_ref, m3_ref, m4_ref, wcoef, ccoef, xs_ref, g_ref,
-    block_row, well_row, owner_row, rhs_well, inv_well, sems, small_sems,
+    block_row, well_row, owner_row, rhs_well, inv_well, row_raw, col_raw, held, sems, small_sems,
 ):
+    rows, cols = jac_in.shape[3], jac_in.shape[4]
+    early = rows // 4 + 2
     pairs = [
         (block_in, block_row), (well_in, well_row), (owner_in, owner_row),
         (rhs_well_in, rhs_well), (inv_well_in, inv_well),
@@ -103,12 +107,17 @@
         copy.start()
     pairs = [
         (wcoef_in, wcoef), (ccoef_in, ccoef), (x_in, x_ref),
-        (jac_in, jac_ref), (diag_in, inv_ref), (rhs_in, rhs_ref),
+        (jac_in.at[1, :, :, 0], row_raw.at[0]),
+        (jac_in.at[2, :, :, rows - 1], row_raw.at[1]),
+        (jac_in.at[3, :, :, :, 0:8], col_raw.at[0]),
+        (jac_in.at[4, :, :, :, cols - 8 : cols], col_raw.at[1]),
+        (diag_in, inv_ref),
+        (jac_in.at[:, :, :, rows - 1], jac_ref.at[:, :, :, rows - 1]),
+        (jac_in.at[:, :, :, 0:early], jac_ref.at[:, :, :, 0:early]), (rhs_in, rhs_ref),
     ]
     copies = [pltpu.make_async_copy(a, b, sems.at[i]) for i, (a, b) in enumerate(pairs)]
     for copy in copies:
         copy.start()
-    rows, cols = jac_ref.shape[3], jac_ref.shape[4]
     cells = rows * cols
     perfs = block_row.shape[1]
     width = well_ref.shape[0]
@@ -119,26 +128,26 @@
         copy.wait()
     block = block_row[...]
     spread = hot(iota((cells, perfs), 0) == block // 2)
-    spread_ref[:, 0:perfs] = spread
-    spread_ref[:, perfs : 2 * perfs] = spread
+    spread_ref[...] = spread
     pick = turned(eye, spread).astype(BF16)
-    pick_ref[:, 0:cells] = pick
-    pick_ref[:, cells : 2 * cells] = pick
+    pick_ref[...] = pick
     own_half = turned(eye, hot(iota((LANES, perfs), 0) // BLOCK == block % 2)) > 0.5
     for h in range(width):
         slot = iota((LANES, perfs), 0) + h * LANES
         well = owner_row[...] * well_dev + well_row[...]
         well_ref[h] = turned(eye, hot(slot == well))
-        place = iota((well_dev, LANES), 0) + flags[4] * well_dev
-        place = (place == iota((well_dev, LANES), 1) + h * LANES).astype(F32)
-        for v in range(WELL_UNK + 1):
-            value = rhs_well[...] if v == 0 else inv_well[v - 1]
-            value = jnp.dot(
-                value, place, precision=lax.Precision.HIGHEST, preferred_element_type=F32
-            )
-            at = base + unk
-            at += h * WELL_UNK if v == 0 else unk + (h * WELL_UNK + v - 1) * WELL_UNK
-            m1_ref[at : at + WELL_UNK, :] = value
+    held[...] = jnp.zeros_like(held)
+    held[0:WELL_UNK, 0:well_dev] = rhs_well[...]
+    for v in range(WELL_UNK):
+        held[(v + 1) * WELL_UNK : (v + 2) * WELL_UNK, 0:well_dev] = inv_well[v]
+    own_lane = flags[4] * well_dev
+    placed = pltpu.roll(held[...], own_lane % LANES, 1)
+    for h in range(width):
+        value = jnp.where(own_lane // LANES == h, placed, 0.0)
+        at = base + unk + h * WELL_UNK
+        m1_ref[at : at + WELL_UNK, :] = value[0:WELL_UNK]
+        at = base + 2 * unk + h * WELL_UNK * WELL_UNK
+        m1_ref[at : at + WELL_UNK * WELL_UNK, :] = value[WELL_UNK : 5 * WELL_UNK]
     copies[0].wait()
     for u in range(WELL_UNK):
         expanded(eye, wcoef, u, own_half, wc_ref)
@@ -150,20 +159,22 @@
     def write(row, value):
         m1_ref[base + row : base + row + 1, :] = value
 
-    well_partials(x_ref, pick_ref, well_ref, wc_ref, xs_ref, g_ref, write)
-    copies[3].wait()
+    for r in range(PHASES):
+        picked_rows(r, x_ref, pick_ref, xs_ref, g_ref)
+    well_partials(pick_ref, well_ref, wc_ref, g_ref, write)
+    for copy in copies[3:7]:
+        copy.wait()
+    row_ref[...] = row_raw[...].astype(F32)
     for r in range(PHASES):
         for t in range(PHASES):
-            row_ref[0, r, t] = jac_ref[1, r, t, 0].astype(F32)
-            row_ref[1, r, t] = jac_ref[2, r, t, rows - 1].astype(F32)
             for i in range(rows):
-                col_ref[0, r, t, i : i + 1, :] = jac_ref[3, r, t, i, 0:8].astype(F32)[0:1]
-                edge = jac_ref[4, r, t, i, cols - 8 : cols].astype(F32)
-                col_ref[1, r, t, i : i + 1, :] = edge[7:8]
+                col_ref[0, r, t, i : i + 1, :] = col_raw[0, r, t, i].astype(F32)[0:1]
+                col_ref[1, r, t, i : i + 1, :] = col_raw[1, r, t, i].astype(F32)[7:8]
     edge_messages(flags, x_ref, row_ref, col_ref, m1_ref, m2_ref, m3_ref, m4_ref)
-    copies[4].wait()
+    copies[7].wait()
     inv_ref[...] = 1.0 / inv_ref[...]
-    copies[5].wait()
+    for copy in copies[8:]:
+        copy.wait()
 
 
 def add_kernel(base, kept_ref, own_ref, got_ref, out_ref):
@@ -171,11 +182,27 @@
     out_ref[base:, :] = own_ref[base:, :] + got_ref[base:, :]
 
 
-def inner_kernel(widen, x_ref, jac_ref, rhs_ref, z_ref, *rest):
-    rows, cols = jac_ref.shape[3], jac_ref.shape[4]
+def inner_kernel(widen, x_ref, jac_in, rhs_ref, *rest):
+    rows, cols = jac_in.shape[3], jac_in.shape[4]
+    early = rows // 4 + 2
+    z_ref = rest[1] if widen else rest[0]
+    if widen:
+        wide_ref, jac_ref, sems = rest[2:]
+
+        def fetch(row):
+            return pltpu.make_async_copy(
+                jac_in.at[:, :, :, row], jac_ref.at[:, :, :, row], sems.at[row]
+            )
+
+        for row in range(early, rows - 1):
+            fetch(row).start()
+    else:
+        jac_ref = jac_in
     lane, col = iota((cols, LANES), 1), iota((cols, LANES), 0)
 
     def row_body(i, carry):
+        if widen:
+            pl.when((i + 1 >= early) & (i < rows - 2))(lambda: fetch(i + 1).wait())
         before = jnp.where(i == 0, rows - 1, i - 1)
         after = jnp.where(i == rows - 1, 0, i + 1)
         open_row = {1: (after > 0).astype(F32), 2: (before < rows - 1).astype(F32)}
@@ -195,7 +222,7 @@
                 value = value * open_row[d]
             if d in shut_cell:
                 value = jnp.where(shut_cell[d], 0.0, value)
-            rest[0][d, r, t, row] = value
+            wide_ref[d, r, t, row] = value
             return value
 
         def term(d, t, row, values):
@@ -214,7 +241,7 @@
             z_ref[t, pl.ds(start, cols), :] = rhs_ref[t, pl.ds(start, cols), :] - total
         return carry
 
-    lax.fori_loop(0, rows, row_body, 0)
+    lax.fori_loop(0, rows, row_body, 0, unroll=1 if widen else 2)
 
 
 def update_kernel(
@@ -222,11 +249,11 @@
     *rest,
 ):
     if last:
-        x_out, adj_ref, rs_ref, c_ref, x_ref, sems = rest
+        x_out, adj_ref, rs_ref, x_ref, sems = rest
     else:
         (row_ref, col_ref, pick_ref, wc_ref, x_ref, m1_ref, m2_ref, m3_ref, m4_ref,
-         rs_ref, c_ref, xs_ref, g_ref) = rest
-    cells, perfs = spread_ref.shape[0], spread_ref.shape[1] // 2
+         rs_ref, xs_ref, g_ref) = rest
+    cells, perfs = spread_ref.shape
     rows = (own.shape[0] - WELL_UNK * well_ref.shape[0]) // PHASES
     cols = cells // rows
     base = PHASES * rows
@@ -242,16 +269,6 @@
             at_v = h * WELL_UNK + v
             value = value + wconst[at : at + WELL_UNK, :] * left[at_v : at_v + 1, :]
         solved.append(value)
-    if last:
-        well_dev = adj_ref.shape[1]
-        mine = 0.0
-        for h in range(width):
-            place = iota((LANES, well_dev), 1) + flags[4] * well_dev
-            place = (place == iota((LANES, well_dev), 0) + h * LANES).astype(F32)
-            mine = mine + jnp.dot(
-                solved[h], place, precision=lax.Precision.HIGHEST, preferred_element_type=F32
-            )
-        adj_ref[...] = mine
     chunk = 64
     for start in range(0, perfs, chunk):
         part = slice(start, start + chunk)
@@ -263,15 +280,14 @@
                 value[r] = value[r] + cc_ref[u, r, part].astype(F32) * factor
         for r in range(PHASES):
             high, low = split_2(value[r])
-            rs_ref[start : start + chunk, r * LANES : (r + 1) * LANES] = high
-            rs_ref[perfs + start : perfs + start + chunk, r * LANES : (r + 1) * LANES] = low
-    c_ref[...] = jnp.dot(spread_ref[...], rs_ref[...], preferred_element_type=F32)
+            rs_ref[r, part, 0:LANES] = high
+            rs_ref[r, part, LANES : 2 * LANES] = low
     gx_odd, gy_odd = flags[0] == 1, flags[1] == 1
     gx_open, gy_open = flags[2].astype(F32), flags[3].astype(F32)
-    for t in range(PHASES):
-        x_ref[t] = (z_ref[t] - c_ref[:, t * LANES : (t + 1) * LANES]) * inv_ref[t]
     copies = []
     for t in range(PHASES):
+        both = jnp.dot(spread_ref[...], rs_ref[t], preferred_element_type=F32)
+        x_ref[t] = (z_ref[t] - both[:, 0:LANES] - both[:, LANES:]) * inv_ref[t]
         near, far = g3[t * cols : (t + 1) * cols, :], g4[t * cols : (t + 1) * cols, :] * gx_open
         first, final = slice(0, cols), slice((rows - 1) * cols, rows * cols)
         x_ref[t, first, :] = x_ref[t, first, :] - inv_ref[t, first, :] * jnp.where(gx_odd, near, far)
@@ -283,6 +299,18 @@
         if last:
             copies.append(pltpu.make_async_copy(x_ref.at[t], x_out.at[t], sems.at[t]))
             copies[t].start()
+        else:
+            picked_rows(t, x_ref, pick_ref, xs_ref, g_ref)
+    if last:
+        well_dev = adj_ref.shape[1]
+        mine = 0.0
+        for h in range(width):
+            place = iota((LANES, well_dev), 1) + flags[4] * well_dev
+            place = (place == iota((LANES, well_dev), 0) + h * LANES).astype(F32)
+            mine = mine + jnp.dot(
+                solved[h], place, precision=lax.Precision.HIGHEST, preferred_element_type=F32
+            )
+        adj_ref[...] = mine
     for copy in copies:
         copy.wait()
     if not last:
@@ -291,7 +319,7 @@
         def write(row, value):
             m1_ref[base + row : base + row + 1, :] = value
 
-        well_partials(x_ref, pick_ref, well_ref, wc_ref, xs_ref, g_ref, write)
+        well_partials(pick_ref, well_ref, wc_ref, g_ref, write)
 
 
 def gx_swap(gx, gy, parity):
@@ -345,18 +373,17 @@
     diag = cell_diag.reshape(phases, cells, layers)
     full = base + unk
     grid = shape(phases, cells, layers)
-    jac_shape = shape(*jacobian.shape, dtype=BF16)
     first = pl.pallas_call(
         first_kernel,
         out_shape=(
             grid,
-            jac_shape,
+            shape(*jacobian.shape, dtype=BF16),
             grid,
             grid,
             shape(2, PHASES, PHASES, cols, LANES),
             shape(2, PHASES, PHASES, rows, LANES),
-            shape(perfs, 2 * cells, dtype=BF16),
-            shape(cells, 2 * perfs, dtype=BF16),
+            shape(perfs, cells, dtype=BF16),
+            shape(cells, perfs, dtype=BF16),
             shape(width, perfs, LANES),
             shape(WELL_UNK, PHASES, perfs, LANES, dtype=BF16),
             shape(WELL_UNK, PHASES, perfs, LANES, dtype=BF16),
@@ -370,20 +397,23 @@
         scratch_shapes=[
             pltpu.VMEM(well_coupling.shape, BF16),
             pltpu.VMEM(cell_coupling.shape, BF16),
-            pltpu.VMEM((2 * cells, PHASES * LANES), BF16),
-            pltpu.VMEM((perfs, PHASES * LANES), F32),
+            pltpu.VMEM((PHASES, cells, 2 * LANES), BF16),
+            pltpu.VMEM((PHASES, perfs, LANES), F32),
             pltpu.VMEM((1, perfs), jnp.int32),
             pltpu.VMEM((1, perfs), jnp.int32),
             pltpu.VMEM((1, perfs), jnp.int32),
             pltpu.VMEM(well_rhs.shape, F32),
             pltpu.VMEM(well_inverse.shape, F32),
-            pltpu.SemaphoreType.DMA((6,)),
+            pltpu.VMEM((2, PHASES, PHASES, cols, LANES), BF16),
+            pltpu.VMEM((2, PHASES, PHASES, rows, 8, LANES), BF16),
+            pltpu.VMEM((24, LANES), F32),
+            pltpu.SemaphoreType.DMA((11,)),
             pltpu.SemaphoreType.DMA((5,)),
         ],
         compiler_params=PARAMS,
         name="first",
     )
-    (x, jac, rhs, inv, row_edges, col_edges, pick, spread, well_hot, wc, cc, m1, m2_halo, m3,
+    (x, jac_part, rhs, inv, row_edges, col_edges, pick, spread, well_hot, wc, cc, m1, m2_halo, m3,
      m4) = first(
         flags,
         *[
@@ -406,20 +436,28 @@
             name="add",
         )(kept, own, got)
 
-    def inner(x, jac, rhs, widen):
-        wide = (shape(*jac.shape),) if widen else ()
+    def inner_first(x, jac, rhs, jac_part):
         return pl.pallas_call(
-            functools.partial(inner_kernel, widen),
-            out_shape=(grid,) + wide,
-            in_specs=[VM] * 3,
-            out_specs=(VM,) * (1 + len(wide)),
+            functools.partial(inner_kernel, True),
+            out_shape=(grid, shape(*jac.shape), shape(*jac.shape, dtype=BF16)),
+            in_specs=[VM, HB, VM, VM],
+            out_specs=(VM,) * 3,
+            scratch_shapes=[pltpu.SemaphoreType.DMA((rows,))],
+            input_output_aliases={3: 2},
             compiler_params=PARAMS,
-            name="inner_widen" if widen else "inner",
-        )(x, jac, rhs)
-
+            name="inner_widen",
+        )(x, in_hbm(jac), rhs, jac_part)[:2]
+
+    inner = pl.pallas_call(
+        functools.partial(inner_kernel, False),
+        out_shape=grid,
+        in_specs=[VM] * 3,
+        out_specs=VM,
+        compiler_params=PARAMS,
+        name="inner",
+    )
     work = [
-        pltpu.VMEM((2 * perfs, PHASES * LANES), BF16),
-        pltpu.VMEM((cells, PHASES * LANES), F32),
+        pltpu.VMEM((PHASES, perfs, 2 * LANES), BF16),
     ]
     for sweep in range(ITERS):
         last = sweep == ITERS - 1
@@ -438,9 +476,9 @@
             wconst = own[full:] + g2[full:]
             own, g1, g2 = own[:full], g1[:full], g2[:full]
         if sweep == 0:
-            z, jac = inner(x, jac, rhs, True)
+            z, jac = inner_first(x, jacobian, rhs, jac_part)
         else:
-            (z,) = inner(x, jac, rhs, False)
+            z = inner(x, jac, rhs)
         operands = (flags, z, own, g1, g2, g3, g4, wconst, inv, spread, well_hot, cc)
         if last:
             x, adj = pl.pallas_call(
@@ -470,8 +508,8 @@
                 out_specs=(VM,) * 5,
                 scratch_shapes=work
                 + [
-                    pltpu.VMEM((2 * cells, PHASES * LANES), BF16),
-                    pltpu.VMEM((perfs, PHASES * LANES), F32),
+                    pltpu.VMEM((PHASES, cells, 2 * LANES), BF16),
+                    pltpu.VMEM((PHASES, perfs, LANES), F32),
                 ],
                 compiler_params=PARAMS,
                 name="update",

time: 79 us -> 77.4 us (0.980)
  Pallas kernels: 39.6 us -> 36.2 us
  waiting for transfers between devices: 9.08 us -> 10.9 us
    ppermute x8, waiting for transfers between devices: 0.23 us -> 1.83 us  [body(): g3 = lax.ppermute(m3, both, gx_swap(gx, gy, 0))]
    pallas_call x8, Pallas kernels: 15.1 us -> 13.6 us  [the longest x7 10.4 us: body(): z = inner(x, jac, rhs)]
    pallas_call x1, Pallas kernels: 7.02 us -> 5.93 us  [body(): first(flags, *[in_hbm(v) for v in (x, jacobian, rhs, diag, well_coupling,...]
  transfers between devices with their start and end apart: 32 -> 32, of which waited for: 9 -> 15; matrix products, arithmetic and copies ran while one was open for 0% -> 0% of each run, Pallas kernels for 19% -> 18%
where the time goes in v2:
time: 77.4 us; the launch traced here: 77.3 us
  Pallas kernels  36.2 us (47%)
  starting transfers between devices  29.1 us (38%)
  waiting for transfers between devices  10.9 us (14%)
  between operations  0.98 us (1%)
    ppermute x8, starting transfers between devices, body(): g3 = lax.ppermute(m3, both, gx_swap(gx, gy, 0))  19.2 us
    pallas_call x7, Pallas kernels, body(): pl.pallas_call(functools.partial(update_kernel, False), out_shape=(shape(...  13.9 us
    pallas_call x7, Pallas kernels, body(): z = inner(x, jac, rhs)  10.4 us
    ppermute x8, waiting for transfers between devices, body(): g2 = lax.ppermute(own, 'gy', gy_swap(gy, 1))  8.16 us
    pallas_call x1, Pallas kernels, body(): first(flags, *[in_hbm(v) for v in (x, jacobian, rhs, diag, well_coupling,...  5.93 us
    ppermute x8, starting transfers between devices, body(): g2 = lax.ppermute(own, 'gy', gy_swap(gy, 1))  5.47 us
    ppermute x8, starting transfers between devices, body(): g1 = lax.ppermute(m1, 'gy', gy_swap(gy, 0))  3.47 us
    pallas_call x1, Pallas kernels, inner_first(): pl.pallas_call(functools.partial(inner_kernel, True), out_shape=(grid, sh...  3.17 us
  transfers between devices with their start and end apart: 32, of which 15 were waited for; matrix products, arithmetic and copies ran while one was open for 0% of the time, Pallas kernels for 18%

profile of v2, /device:TPU:0, one launch (start us, length us, event | category | flops | bytes accessed | tf_op | source)
XLA Modules:
  0.0 77.3 jit_solution(13901168035010137433)
XLA Ops:
  0.7 5.9 %first.1 = (f32[3,512,128]{2,1,0:T(8,128)S(1)}, bf16[7,3,3,16,32,128]{5,4,3,2,1,0:T(8,128)(2,1)S(1)}, f32[3,512,128]{2,1,0:T(8,128)S(1)}, f32[3,512,128]{2,1,0:T...) custom-call(s32[5]{0:T(128)S(1)} %stack.31.flags, ...), custom_call_target="tpu_custom_call" | custom-call | tf_op jit(solution)/shard_map/first/pallas_call | solution.py:417
  8.1 2.6 %collective-permute-start.1 = (f32[72,128]{1,0:T(8,128)S(1)}, f32[72,128]{1,0:T(8,128)S(1)}, u32[]{:S(2)}, u32[]{:S(2)}) collective-permute-start(f32[72,128]{1,0:T(8,128)S(1)} %add.24), channel_id=1, source_target_pairs={{0,3},{1,2},{2,1},{3,0},{4,7},{5,6},{6,5},{7,4},{8,11},{9,10},{10,... | collective-permute-start | bytes 110600 | tf_op jit(solution)/shard_map/ppermute | solution.py:468
  10.7 1.5 %collective-permute-start.2 = (f32[96,128]{1,0:T(8,128)S(1)}, f32[96,128]{1,0:T(8,128)S(1)}, u32[]{:S(2)}, u32[]{:S(2)}) collective-permute-start(f32[96,128]{1,0:T(8,128)S(1)} %get-tuple-element.62), channel_id=1, source_target_pairs={{0,4},{1,5},{2,6},{3,7},{4,0},{5,1},{6,2},{7,3},{8,12},{9,13},{10,... | collective-permute-start | bytes 147464 | tf_op jit(solution)/shard_map/ppermute | solution.py:465
  12.3 3.2 %inner_widen.1 = (f32[3,512,128]{2,1,0:T(8,128)S(1)}, f32[7,3,3,16,32,128]{5,4,3,2,1,0:T(8,128)S(1)}, bf16[7,3,3,16,32,128]{5,4,3,2,1,0:T(8,128)(2,1)S(1)}) custom-call(f32[3,512,128]{2,1,0:T(8,128)S(1)} %get-tuple-element.56.x_ref, bf16[7,3,3,16,32,128]{5,4,3,2,1,0:T(8,128)(2,1)} %jac_in.3, ...), custom_call_target="tpu_custom_call", output_to_operand_aliasing={{2}: (3, {})} | custom-call | tf_op jit(solution)/shard_map/inner_widen/pallas_call | solution.py:440
  15.5 2.0 %update.7 = (f32[3,512,128]{2,1,0:T(8,128)S(1)}, f32[52,128]{1,0:T(8,128)S(1)}, f32[48,128]{1,0:T(8,128)S(1)}, f32[96,128]{1,0:T(8,128)S(1)}, f32[96,128]{1,0:T(8,128)S(1)}) custom-call(s32[5]{0:T(128)S(1)} %stack.31.flags, f32[3,512,128]{2,1,0:T(8,128)S(1)} %get-tuple-element.59.z_ref, f32[52,128]{1,0:T(8,128)S(1)} %slice.20.own, f32[52,128]{1,0:T(8,128)S(1)} %slice.21.g1, ...), custom_call_target="tpu_custom_call" | custom-call | tf_op jit(solution)/shard_map/update/pallas_call | solution.py:498
  18.0 2.6 %collective-permute-start.6 = (f32[96,128]{1,0:T(8,128)S(1)}, f32[96,128]{1,0:T(8,128)S(1)}, u32[]{:S(2)}, u32[]{:S(2)}) collective-permute-start(f32[96,128]{1,0:T(8,128)S(1)} %get-tuple-element.76), channel_id=1, source_target_pairs={{0,4},{1,5},{2,6},{3,7},{4,0},{5,1},{6,2},{7,3},{8,12},{9,13},{10,... | collective-permute-start | bytes 147464 | tf_op jit(solution)/shard_map/ppermute | solution.py:465
  21.3 1.5 %inner.7.z_ref = f32[3,512,128]{2,1,0:T(8,128)S(1)} custom-call(f32[3,512,128]{2,1,0:T(8,128)S(1)} %get-tuple-element.72.x_ref, f32[7,3,3,16,32,128]{5,4,3,2,1,0:T(8,128)S(1)} %get-tuple-element.73.jac_in, f32[3,512,128]{2,1,0:T(8,128)S(1)} %get-tuple-element.57.rhs_ref), custom_call_target="tpu_custom_call" | custom-call | tf_op jit(solution)/shard_map/inner/pallas_call | solution.py:481
  24.1 2.0 %update.8 = (f32[3,512,128]{2,1,0:T(8,128)S(1)}, f32[52,128]{1,0:T(8,128)S(1)}, f32[48,128]{1,0:T(8,128)S(1)}, f32[96,128]{1,0:T(8,128)S(1)}, f32[96,128]{1,0:T(8,128)S(1)}) custom-call(s32[5]{0:T(128)S(1)} %stack.31.flags, f32[3,512,128]{2,1,0:T(8,128)S(1)} %inner.7.z_ref, f32[52,128]{1,0:T(8,128)S(1)} %add.25.own, ...), custom_call_target="tpu_custom_call" | custom-call | tf_op jit(solution)/shard_map/update/pallas_call | solution.py:498
  26.5 2.9 %collective-permute-start.10 = (f32[96,128]{1,0:T(8,128)S(1)}, f32[96,128]{1,0:T(8,128)S(1)}, u32[]{:S(2)}, u32[]{:S(2)}) collective-permute-start(f32[96,128]{1,0:T(8,128)S(1)} %get-tuple-element.81), channel_id=1, source_target_pairs={{0,4},{1,5},{2,6},{3,7},{4,0},{5,1},{6,2},{7,3},{8,12},{9,13},{10,... | collective-permute-start | bytes 147464 | tf_op jit(solution)/shard_map/ppermute | solution.py:465
  30.0 1.5 %inner.8.z_ref = f32[3,512,128]{2,1,0:T(8,128)S(1)} custom-call(f32[3,512,128]{2,1,0:T(8,128)S(1)} %get-tuple-element.78.x_ref, f32[7,3,3,16,32,128]{5,4,3,2,1,0:T(8,128)S(1)} %get-tuple-element.73.jac_in, f32[3,512,128]{2,1,0:T(8,128)S(1)} %get-tuple-element.57.rhs_ref), custom_call_target="tpu_custom_call" | custom-call | tf_op jit(solution)/shard_map/inner/pallas_call | solution.py:481
  31.7 1.2 %collective-permute-done.9.g2 = f32[52,128]{1,0:T(8,128)S(1)} collective-permute-done((f32[52,128]{1,0:T(8,128)S(1)}, f32[52,128]{1,0:T(8,128)S(1)}, u32[]{:S(2)}, u32[]{:S(2)}) %collective-permute-start.9) | collective-permute-done | bytes 26656 | tf_op jit(solution)/shard_map/ppermute | solution.py:468
  32.9 2.0 %update.9 = (f32[3,512,128]{2,1,0:T(8,128)S(1)}, f32[52,128]{1,0:T(8,128)S(1)}, f32[48,128]{1,0:T(8,128)S(1)}, f32[96,128]{1,0:T(8,128)S(1)}, f32[96,128]{1,0:T(8,128)S(1)}) custom-call(s32[5]{0:T(128)S(1)} %stack.31.flags, f32[3,512,128]{2,1,0:T(8,128)S(1)} %inner.8.z_ref, f32[52,128]{1,0:T(8,128)S(1)} %add.26.own, ...), custom_call_target="tpu_custom_call" | custom-call | tf_op jit(solution)/shard_map/update/pallas_call | solution.py:498
  35.3 2.9 %collective-permute-start.14 = (f32[96,128]{1,0:T(8,128)S(1)}, f32[96,128]{1,0:T(8,128)S(1)}, u32[]{:S(2)}, u32[]{:S(2)}) collective-permute-start(f32[96,128]{1,0:T(8,128)S(1)} %get-tuple-element.86), channel_id=1, source_target_pairs={{0,4},{1,5},{2,6},{3,7},{4,0},{5,1},{6,2},{7,3},{8,12},{9,13},{10,... | collective-permute-start | bytes 147464 | tf_op jit(solution)/shard_map/ppermute | solution.py:465
  38.7 1.5 %inner.9.z_ref = f32[3,512,128]{2,1,0:T(8,128)S(1)} custom-call(f32[3,512,128]{2,1,0:T(8,128)S(1)} %get-tuple-element.83.x_ref, f32[7,3,3,16,32,128]{5,4,3,2,1,0:T(8,128)S(1)} %get-tuple-element.73.jac_in, f32[3,512,128]{2,1,0:T(8,128)S(1)} %get-tuple-element.57.rhs_ref), custom_call_target="tpu_custom_call" | custom-call | tf_op jit(solution)/shard_map/inner/pallas_call | solution.py:481
  40.5 1.2 %collective-permute-done.13.g2 = f32[52,128]{1,0:T(8,128)S(1)} collective-permute-done((f32[52,128]{1,0:T(8,128)S(1)}, f32[52,128]{1,0:T(8,128)S(1)}, u32[]{:S(2)}, u32[]{:S(2)}) %collective-permute-start.13) | collective-permute-done | bytes 26656 | tf_op jit(solution)/shard_map/ppermute | solution.py:468
  41.7 2.0 %update.10 = (f32[3,512,128]{2,1,0:T(8,128)S(1)}, f32[52,128]{1,0:T(8,128)S(1)}, f32[48,128]{1,0:T(8,128)S(1)}, f32[96,128]{1,0:T(8,128)S(1)}, f32[96,128]{1,0:T(8,128)S(1)}) custom-call(s32[5]{0:T(128)S(1)} %stack.31.flags, f32[3,512,128]{2,1,0:T(8,128)S(1)} %inner.9.z_ref, f32[52,128]{1,0:T(8,128)S(1)} %add.27.own, ...), custom_call_target="tpu_custom_call" | custom-call | tf_op jit(solution)/shard_map/update/pallas_call | solution.py:498
  44.1 2.0 %collective-permute-start.18 = (f32[96,128]{1,0:T(8,128)S(1)}, f32[96,128]{1,0:T(8,128)S(1)}, u32[]{:S(2)}, u32[]{:S(2)}) collective-permute-start(f32[96,128]{1,0:T(8,128)S(1)} %get-tuple-element.91), channel_id=1, source_target_pairs={{0,4},{1,5},{2,6},{3,7},{4,0},{5,1},{6,2},{7,3},{8,12},{9,13},{10,... | collective-permute-start | bytes 147464 | tf_op jit(solution)/shard_map/ppermute | solution.py:465
  46.7 1.5 %inner.10.z_ref = f32[3,512,128]{2,1,0:T(8,128)S(1)} custom-call(f32[3,512,128]{2,1,0:T(8,128)S(1)} %get-tuple-element.88.x_ref, f32[7,3,3,16,32,128]{5,4,3,2,1,0:T(8,128)S(1)} %get-tuple-element.73.jac_in, f32[3,512,128]{2,1,0:T(8,128)S(1)} %get-tuple-element.57.rhs_ref), custom_call_target="tpu_custom_call" | custom-call | tf_op jit(solution)/shard_map/inner/pallas_call | solution.py:481
  48.4 1.2 %collective-permute-done.17.g2 = f32[52,128]{1,0:T(8,128)S(1)} collective-permute-done((f32[52,128]{1,0:T(8,128)S(1)}, f32[52,128]{1,0:T(8,128)S(1)}, u32[]{:S(2)}, u32[]{:S(2)}) %collective-permute-start.17) | collective-permute-done | bytes 26656 | tf_op jit(solution)/shard_map/ppermute | solution.py:468
  49.5 2.0 %update.11 = (f32[3,512,128]{2,1,0:T(8,128)S(1)}, f32[52,128]{1,0:T(8,128)S(1)}, f32[48,128]{1,0:T(8,128)S(1)}, f32[96,128]{1,0:T(8,128)S(1)}, f32[96,128]{1,0:T(8,128)S(1)}) custom-call(s32[5]{0:T(128)S(1)} %stack.31.flags, f32[3,512,128]{2,1,0:T(8,128)S(1)} %inner.10.z_ref, f32[52,128]{1,0:T(8,128)S(1)} %add.28.own, ...), custom_call_target="tpu_custom_call" | custom-call | tf_op jit(solution)/shard_map/update/pallas_call | solution.py:498
  51.9 2.6 %collective-permute-start.22 = (f32[96,128]{1,0:T(8,128)S(1)}, f32[96,128]{1,0:T(8,128)S(1)}, u32[]{:S(2)}, u32[]{:S(2)}) collective-permute-start(f32[96,128]{1,0:T(8,128)S(1)} %get-tuple-element.96), channel_id=1, source_target_pairs={{0,4},{1,5},{2,6},{3,7},{4,0},{5,1},{6,2},{7,3},{8,12},{9,13},{10,... | collective-permute-start | bytes 147464 | tf_op jit(solution)/shard_map/ppermute | solution.py:465
  55.1 1.5 %inner.11.z_ref = f32[3,512,128]{2,1,0:T(8,128)S(1)} custom-call(f32[3,512,128]{2,1,0:T(8,128)S(1)} %get-tuple-element.93.x_ref, f32[7,3,3,16,32,128]{5,4,3,2,1,0:T(8,128)S(1)} %get-tuple-element.73.jac_in, f32[3,512,128]{2,1,0:T(8,128)S(1)} %get-tuple-element.57.rhs_ref), custom_call_target="tpu_custom_call" | custom-call | tf_op jit(solution)/shard_map/inner/pallas_call | solution.py:481
  56.8 1.2 %collective-permute-done.21.g2 = f32[52,128]{1,0:T(8,128)S(1)} collective-permute-done((f32[52,128]{1,0:T(8,128)S(1)}, f32[52,128]{1,0:T(8,128)S(1)}, u32[]{:S(2)}, u32[]{:S(2)}) %collective-permute-start.21) | collective-permute-done | bytes 26656 | tf_op jit(solution)/shard_map/ppermute | solution.py:468
  58.0 2.0 %update.12 = (f32[3,512,128]{2,1,0:T(8,128)S(1)}, f32[52,128]{1,0:T(8,128)S(1)}, f32[48,128]{1,0:T(8,128)S(1)}, f32[96,128]{1,0:T(8,128)S(1)}, f32[96,128]{1,0:T(8,128)S(1)}) custom-call(s32[5]{0:T(128)S(1)} %stack.31.flags, f32[3,512,128]{2,1,0:T(8,128)S(1)} %inner.11.z_ref, f32[52,128]{1,0:T(8,128)S(1)} %add.29.own, ...), custom_call_target="tpu_custom_call" | custom-call | tf_op jit(solution)/shard_map/update/pallas_call | solution.py:498
  60.4 2.0 %collective-permute-start.26 = (f32[96,128]{1,0:T(8,128)S(1)}, f32[96,128]{1,0:T(8,128)S(1)}, u32[]{:S(2)}, u32[]{:S(2)}) collective-permute-start(f32[96,128]{1,0:T(8,128)S(1)} %get-tuple-element.101), channel_id=1, source_target_pairs={{0,4},{1,5},{2,6},{3,7},{4,0},{5,1},{6,2},{7,3},{8,12},{9,13},{10,... | collective-permute-start | bytes 147464 | tf_op jit(solution)/shard_map/ppermute | solution.py:465
  63.0 1.5 %inner.12.z_ref = f32[3,512,128]{2,1,0:T(8,128)S(1)} custom-call(f32[3,512,128]{2,1,0:T(8,128)S(1)} %get-tuple-element.98.x_ref, f32[7,3,3,16,32,128]{5,4,3,2,1,0:T(8,128)S(1)} %get-tuple-element.73.jac_in, f32[3,512,128]{2,1,0:T(8,128)S(1)} %get-tuple-element.57.rhs_ref), custom_call_target="tpu_custom_call" | custom-call | tf_op jit(solution)/shard_map/inner/pallas_call | solution.py:481
  64.7 1.2 %collective-permute-done.25.g2 = f32[52,128]{1,0:T(8,128)S(1)} collective-permute-done((f32[52,128]{1,0:T(8,128)S(1)}, f32[52,128]{1,0:T(8,128)S(1)}, u32[]{:S(2)}, u32[]{:S(2)}) %collective-permute-start.25) | collective-permute-done | bytes 26656 | tf_op jit(solution)/shard_map/ppermute | solution.py:468
  65.8 2.0 %update.13 = (f32[3,512,128]{2,1,0:T(8,128)S(1)}, f32[52,128]{1,0:T(8,128)S(1)}, f32[48,128]{1,0:T(8,128)S(1)}, f32[96,128]{1,0:T(8,128)S(1)}, f32[96,128]{1,0:T(8,128)S(1)}) custom-call(s32[5]{0:T(128)S(1)} %stack.31.flags, f32[3,512,128]{2,1,0:T(8,128)S(1)} %inner.12.z_ref, f32[52,128]{1,0:T(8,128)S(1)} %add.30.own, ...), custom_call_target="tpu_custom_call" | custom-call | tf_op jit(solution)/shard_map/update/pallas_call | solution.py:498
  68.3 2.7 %collective-permute-start.30 = (f32[96,128]{1,0:T(8,128)S(1)}, f32[96,128]{1,0:T(8,128)S(1)}, u32[]{:S(2)}, u32[]{:S(2)}) collective-permute-start(f32[96,128]{1,0:T(8,128)S(1)} %get-tuple-element.106), channel_id=1, source_target_pairs={{0,4},{1,5},{2,6},{3,7},{4,0},{5,1},{6,2},{7,3},{8,12},{9,13},{10,... | collective-permute-start | bytes 147464 | tf_op jit(solution)/shard_map/ppermute | solution.py:465
  71.3 1.5 %inner.13.z_ref = f32[3,512,128]{2,1,0:T(8,128)S(1)} custom-call(f32[3,512,128]{2,1,0:T(8,128)S(1)} %get-tuple-element.103.x_ref, f32[7,3,3,16,32,128]{5,4,3,2,1,0:T(8,128)S(1)} %get-tuple-element.73.jac_in, f32[3,512,128]{2,1,0:T(8,128)S(1)} %get-tuple-element.57.rhs_ref), custom_call_target="tpu_custom_call" | custom-call | tf_op jit(solution)/shard_map/inner/pallas_call | solution.py:481
  73.3 1.2 %collective-permute-done.29.g2 = f32[52,128]{1,0:T(8,128)S(1)} collective-permute-done((f32[52,128]{1,0:T(8,128)S(1)}, f32[52,128]{1,0:T(8,128)S(1)}, u32[]{:S(2)}, u32[]{:S(2)}) %collective-permute-start.29) | collective-permute-done | bytes 26656 | tf_op jit(solution)/shard_map/ppermute | solution.py:468
  74.4 2.7 %update_last.1 = (f32[3,512,128]{2,1,0:T(8,128)}, f32[4,32]{1,0:T(4,128)}) custom-call(s32[5]{0:T(128)S(1)} %stack.31.flags, f32[3,512,128]{2,1,0:T(8,128)S(1)} %inner.13.z_ref, f32[52,128]{1,0:T(8,128)S(1)} %add.31.own, f32[52,128]{1,0:T(8,128)S(1)} %collective-permute-done.28.got_ref.g1, f32[52,128]{1,0:T(8,128)S(1)} %collective-permute-done.29.g2, ...), custom_call_target="tpu_custom_call" | custom-call | tf_op jit(solution)/shard_map/update_last/pallas_call | solution.py:484
  (62 shorter events, 11.3 us)
Async XLA Ops:
  6.7 1.4 %collective-permute-start = (f32[72,128]{1,0:T(8,128)S(1)}, f32[72,128]{1,0:T(8,128)S(1)}, u32[]{:S(2)}, u32[]{:S(2)}) collective-permute-start(f32[72,128]{1,0:T(8,128)S(1)} %get-tuple-element.61.own_ref), channel_id=1, source_target_pairs={{0,1},{1,0},{2,3},{3,2},{4,5},{5,4},{6,7},{7,6},{8,9},{9,8},{10,11... | collective-permute-start | bytes 110600 | tf_op jit(solution)/shard_map/ppermute | solution.py:464
  8.1 7.4 %collective-permute-start.1 = (f32[72,128]{1,0:T(8,128)S(1)}, f32[72,128]{1,0:T(8,128)S(1)}, u32[]{:S(2)}, u32[]{:S(2)}) collective-permute-start(f32[72,128]{1,0:T(8,128)S(1)} %add.24), channel_id=1, source_target_pairs={{0,3},{1,2},{2,1},{3,0},{4,7},{5,6},{6,5},{7,4},{8,11},{9,10},{10,... | collective-permute-start | bytes 110600 | tf_op jit(solution)/shard_map/ppermute | solution.py:468
  10.7 4.8 %collective-permute-start.2 = (f32[96,128]{1,0:T(8,128)S(1)}, f32[96,128]{1,0:T(8,128)S(1)}, u32[]{:S(2)}, u32[]{:S(2)}) collective-permute-start(f32[96,128]{1,0:T(8,128)S(1)} %get-tuple-element.62), channel_id=1, source_target_pairs={{0,4},{1,5},{2,6},{3,7},{4,0},{5,1},{6,2},{7,3},{8,12},{9,13},{10,... | collective-permute-start | bytes 147464 | tf_op jit(solution)/shard_map/ppermute | solution.py:465
  12.2 3.3 %collective-permute-start.3 = (f32[96,128]{1,0:T(8,128)S(1)}, f32[96,128]{1,0:T(8,128)S(1)}, u32[]{:S(2)}, u32[]{:S(2)}) collective-permute-start(f32[96,128]{1,0:T(8,128)S(1)} %get-tuple-element.63), channel_id=1, source_target_pairs={{0,1},{1,0},{2,3},{3,2},{4,8},{5,9},{6,10},{7,11},{8,4},{9,5},{10,... | collective-permute-start | bytes 147464 | tf_op jit(solution)/shard_map/ppermute | solution.py:466
  17.5 3.3 %collective-permute-start.4 = (f32[52,128]{1,0:T(8,128)S(1)}, f32[52,128]{1,0:T(8,128)S(1)}, u32[]{:S(2)}, u32[]{:S(2)}) collective-permute-start(f32[52,128]{1,0:T(8,128)S(1)} %get-tuple-element.75.own_ref), channel_id=1, source_target_pairs={{0,1},{1,0},{2,3},{3,2},{4,5},{5,4},{6,7},{7,6},{8,9},{9,8},{10,11... | collective-permute-start | bytes 79880 | tf_op jit(solution)/shard_map/ppermute | solution.py:464
  18.0 4.9 %collective-permute-start.6 = (f32[96,128]{1,0:T(8,128)S(1)}, f32[96,128]{1,0:T(8,128)S(1)}, u32[]{:S(2)}, u32[]{:S(2)}) collective-permute-start(f32[96,128]{1,0:T(8,128)S(1)} %get-tuple-element.76), channel_id=1, source_target_pairs={{0,4},{1,5},{2,6},{3,7},{4,0},{5,1},{6,2},{7,3},{8,12},{9,13},{10,... | collective-permute-start | bytes 147464 | tf_op jit(solution)/shard_map/ppermute | solution.py:465
  20.6 2.3 %collective-permute-start.7 = (f32[96,128]{1,0:T(8,128)S(1)}, f32[96,128]{1,0:T(8,128)S(1)}, u32[]{:S(2)}, u32[]{:S(2)}) collective-permute-start(f32[96,128]{1,0:T(8,128)S(1)} %get-tuple-element.77), channel_id=1, source_target_pairs={{0,1},{1,0},{2,3},{3,2},{4,8},{5,9},{6,10},{7,11},{8,4},{9,5},{10,... | collective-permute-start | bytes 147464 | tf_op jit(solution)/shard_map/ppermute | solution.py:466
  20.8 3.3 %collective-permute-start.5 = (f32[52,128]{1,0:T(8,128)S(1)}, f32[52,128]{1,0:T(8,128)S(1)}, u32[]{:S(2)}, u32[]{:S(2)}) collective-permute-start(f32[52,128]{1,0:T(8,128)S(1)} %add.25.own), channel_id=1, source_target_pairs={{0,3},{1,2},{2,1},{3,0},{4,7},{5,6},{6,5},{7,4},{8,11},{9,10},{10,... | collective-permute-start | bytes 79880 | tf_op jit(solution)/shard_map/ppermute | solution.py:468
  26.1 3.4 %collective-permute-start.8 = (f32[52,128]{1,0:T(8,128)S(1)}, f32[52,128]{1,0:T(8,128)S(1)}, u32[]{:S(2)}, u32[]{:S(2)}) collective-permute-start(f32[52,128]{1,0:T(8,128)S(1)} %get-tuple-element.80.own_ref), channel_id=1, source_target_pairs={{0,1},{1,0},{2,3},{3,2},{4,5},{5,4},{6,7},{7,6},{8,9},{9,8},{10,11... | collective-permute-start | bytes 79880 | tf_op jit(solution)/shard_map/ppermute | solution.py:464
  26.5 5.2 %collective-permute-start.10 = (f32[96,128]{1,0:T(8,128)S(1)}, f32[96,128]{1,0:T(8,128)S(1)}, u32[]{:S(2)}, u32[]{:S(2)}) collective-permute-start(f32[96,128]{1,0:T(8,128)S(1)} %get-tuple-element.81), channel_id=1, source_target_pairs={{0,4},{1,5},{2,6},{3,7},{4,0},{5,1},{6,2},{7,3},{8,12},{9,13},{10,... | collective-permute-start | bytes 147464 | tf_op jit(solution)/shard_map/ppermute | solution.py:465
  29.4 2.3 %collective-permute-start.11 = (f32[96,128]{1,0:T(8,128)S(1)}, f32[96,128]{1,0:T(8,128)S(1)}, u32[]{:S(2)}, u32[]{:S(2)}) collective-permute-start(f32[96,128]{1,0:T(8,128)S(1)} %get-tuple-element.82), channel_id=1, source_target_pairs={{0,1},{1,0},{2,3},{3,2},{4,8},{5,9},{6,10},{7,11},{8,4},{9,5},{10,... | collective-permute-start | bytes 147464 | tf_op jit(solution)/shard_map/ppermute | solution.py:466
  29.5 3.4 %collective-permute-start.9 = (f32[52,128]{1,0:T(8,128)S(1)}, f32[52,128]{1,0:T(8,128)S(1)}, u32[]{:S(2)}, u32[]{:S(2)}) collective-permute-start(f32[52,128]{1,0:T(8,128)S(1)} %add.26.own), channel_id=1, source_target_pairs={{0,3},{1,2},{2,1},{3,0},{4,7},{5,6},{6,5},{7,4},{8,11},{9,10},{10,... | collective-permute-start | bytes 79880 | tf_op jit(solution)/shard_map/ppermute | solution.py:468
  34.9 3.5 %collective-permute-start.12 = (f32[52,128]{1,0:T(8,128)S(1)}, f32[52,128]{1,0:T(8,128)S(1)}, u32[]{:S(2)}, u32[]{:S(2)}) collective-permute-start(f32[52,128]{1,0:T(8,128)S(1)} %get-tuple-element.85.own_ref), channel_id=1, source_target_pairs={{0,1},{1,0},{2,3},{3,2},{4,5},{5,4},{6,7},{7,6},{8,9},{9,8},{10,11... | collective-permute-start | bytes 79880 | tf_op jit(solution)/shard_map/ppermute | solution.py:464
  35.3 5.2 %collective-permute-start.14 = (f32[96,128]{1,0:T(8,128)S(1)}, f32[96,128]{1,0:T(8,128)S(1)}, u32[]{:S(2)}, u32[]{:S(2)}) collective-permute-start(f32[96,128]{1,0:T(8,128)S(1)} %get-tuple-element.86), channel_id=1, source_target_pairs={{0,4},{1,5},{2,6},{3,7},{4,0},{5,1},{6,2},{7,3},{8,12},{9,13},{10,... | collective-permute-start | bytes 147464 | tf_op jit(solution)/shard_map/ppermute | solution.py:465
  38.2 2.3 %collective-permute-start.15 = (f32[96,128]{1,0:T(8,128)S(1)}, f32[96,128]{1,0:T(8,128)S(1)}, u32[]{:S(2)}, u32[]{:S(2)}) collective-permute-start(f32[96,128]{1,0:T(8,128)S(1)} %get-tuple-element.87), channel_id=1, source_target_pairs={{0,1},{1,0},{2,3},{3,2},{4,8},{5,9},{6,10},{7,11},{8,4},{9,5},{10,... | collective-permute-start | bytes 147464 | tf_op jit(solution)/shard_map/ppermute | solution.py:466
  38.4 3.3 %collective-permute-start.13 = (f32[52,128]{1,0:T(8,128)S(1)}, f32[52,128]{1,0:T(8,128)S(1)}, u32[]{:S(2)}, u32[]{:S(2)}) collective-permute-start(f32[52,128]{1,0:T(8,128)S(1)} %add.27.own), channel_id=1, source_target_pairs={{0,3},{1,2},{2,1},{3,0},{4,7},{5,6},{6,5},{7,4},{8,11},{9,10},{10,... | collective-permute-start | bytes 79880 | tf_op jit(solution)/shard_map/ppermute | solution.py:468
  43.7 2.5 %collective-permute-start.16 = (f32[52,128]{1,0:T(8,128)S(1)}, f32[52,128]{1,0:T(8,128)S(1)}, u32[]{:S(2)}, u32[]{:S(2)}) collective-permute-start(f32[52,128]{1,0:T(8,128)S(1)} %get-tuple-element.90.own_ref), channel_id=1, source_target_pairs={{0,1},{1,0},{2,3},{3,2},{4,5},{5,4},{6,7},{7,6},{8,9},{9,8},{10,11... | collective-permute-start | bytes 79880 | tf_op jit(solution)/shard_map/ppermute | solution.py:464
  44.1 4.3 %collective-permute-start.18 = (f32[96,128]{1,0:T(8,128)S(1)}, f32[96,128]{1,0:T(8,128)S(1)}, u32[]{:S(2)}, u32[]{:S(2)}) collective-permute-start(f32[96,128]{1,0:T(8,128)S(1)} %get-tuple-element.91), channel_id=1, source_target_pairs={{0,4},{1,5},{2,6},{3,7},{4,0},{5,1},{6,2},{7,3},{8,12},{9,13},{10,... | collective-permute-start | bytes 147464 | tf_op jit(solution)/shard_map/ppermute | solution.py:465
  46.0 2.3 %collective-permute-start.19 = (f32[96,128]{1,0:T(8,128)S(1)}, f32[96,128]{1,0:T(8,128)S(1)}, u32[]{:S(2)}, u32[]{:S(2)}) collective-permute-start(f32[96,128]{1,0:T(8,128)S(1)} %get-tuple-element.92), channel_id=1, source_target_pairs={{0,1},{1,0},{2,3},{3,2},{4,8},{5,9},{6,10},{7,11},{8,4},{9,5},{10,... | collective-permute-start | bytes 147464 | tf_op jit(solution)/shard_map/ppermute | solution.py:466
  46.2 3.3 %collective-permute-start.17 = (f32[52,128]{1,0:T(8,128)S(1)}, f32[52,128]{1,0:T(8,128)S(1)}, u32[]{:S(2)}, u32[]{:S(2)}) collective-permute-start(f32[52,128]{1,0:T(8,128)S(1)} %add.28.own), channel_id=1, source_target_pairs={{0,3},{1,2},{2,1},{3,0},{4,7},{5,6},{6,5},{7,4},{8,11},{9,10},{10,... | collective-permute-start | bytes 79880 | tf_op jit(solution)/shard_map/ppermute | solution.py:468
  51.5 3.2 %collective-permute-start.20 = (f32[52,128]{1,0:T(8,128)S(1)}, f32[52,128]{1,0:T(8,128)S(1)}, u32[]{:S(2)}, u32[]{:S(2)}) collective-permute-start(f32[52,128]{1,0:T(8,128)S(1)} %get-tuple-element.95.own_ref), channel_id=1, source_target_pairs={{0,1},{1,0},{2,3},{3,2},{4,5},{5,4},{6,7},{7,6},{8,9},{9,8},{10,11... | collective-permute-start | bytes 79880 | tf_op jit(solution)/shard_map/ppermute | solution.py:464
  51.9 4.9 %collective-permute-start.22 = (f32[96,128]{1,0:T(8,128)S(1)}, f32[96,128]{1,0:T(8,128)S(1)}, u32[]{:S(2)}, u32[]{:S(2)}) collective-permute-start(f32[96,128]{1,0:T(8,128)S(1)} %get-tuple-element.96), channel_id=1, source_target_pairs={{0,4},{1,5},{2,6},{3,7},{4,0},{5,1},{6,2},{7,3},{8,12},{9,13},{10,... | collective-permute-start | bytes 147464 | tf_op jit(solution)/shard_map/ppermute | solution.py:465
  54.5 2.3 %collective-permute-start.23 = (f32[96,128]{1,0:T(8,128)S(1)}, f32[96,128]{1,0:T(8,128)S(1)}, u32[]{:S(2)}, u32[]{:S(2)}) collective-permute-start(f32[96,128]{1,0:T(8,128)S(1)} %get-tuple-element.97), channel_id=1, source_target_pairs={{0,1},{1,0},{2,3},{3,2},{4,8},{5,9},{6,10},{7,11},{8,4},{9,5},{10,... | collective-permute-start | bytes 147464 | tf_op jit(solution)/shard_map/ppermute | solution.py:466
  54.7 3.3 %collective-permute-start.21 = (f32[52,128]{1,0:T(8,128)S(1)}, f32[52,128]{1,0:T(8,128)S(1)}, u32[]{:S(2)}, u32[]{:S(2)}) collective-permute-start(f32[52,128]{1,0:T(8,128)S(1)} %add.29.own), channel_id=1, source_target_pairs={{0,3},{1,2},{2,1},{3,0},{4,7},{5,6},{6,5},{7,4},{8,11},{9,10},{10,... | collective-permute-start | bytes 79880 | tf_op jit(solution)/shard_map/ppermute | solution.py:468
  60.0 2.5 %collective-permute-start.24 = (f32[52,128]{1,0:T(8,128)S(1)}, f32[52,128]{1,0:T(8,128)S(1)}, u32[]{:S(2)}, u32[]{:S(2)}) collective-permute-start(f32[52,128]{1,0:T(8,128)S(1)} %get-tuple-element.100.own_ref), channel_id=1, source_target_pairs={{0,1},{1,0},{2,3},{3,2},{4,5},{5,4},{6,7},{7,6},{8,9},{9,8},{10,11... | collective-permute-start | bytes 79880 | tf_op jit(solution)/shard_map/ppermute | solution.py:464
  60.4 4.3 %collective-permute-start.26 = (f32[96,128]{1,0:T(8,128)S(1)}, f32[96,128]{1,0:T(8,128)S(1)}, u32[]{:S(2)}, u32[]{:S(2)}) collective-permute-start(f32[96,128]{1,0:T(8,128)S(1)} %get-tuple-element.101), channel_id=1, source_target_pairs={{0,4},{1,5},{2,6},{3,7},{4,0},{5,1},{6,2},{7,3},{8,12},{9,13},{10,... | collective-permute-start | bytes 147464 | tf_op jit(solution)/shard_map/ppermute | solution.py:465
  62.4 2.3 %collective-permute-start.27 = (f32[96,128]{1,0:T(8,128)S(1)}, f32[96,128]{1,0:T(8,128)S(1)}, u32[]{:S(2)}, u32[]{:S(2)}) collective-permute-start(f32[96,128]{1,0:T(8,128)S(1)} %get-tuple-element.102), channel_id=1, source_target_pairs={{0,1},{1,0},{2,3},{3,2},{4,8},{5,9},{6,10},{7,11},{8,4},{9,5},{10,... | collective-permute-start | bytes 147464 | tf_op jit(solution)/shard_map/ppermute | solution.py:466
  62.5 3.4 %collective-permute-start.25 = (f32[52,128]{1,0:T(8,128)S(1)}, f32[52,128]{1,0:T(8,128)S(1)}, u32[]{:S(2)}, u32[]{:S(2)}) collective-permute-start(f32[52,128]{1,0:T(8,128)S(1)} %add.30.own), channel_id=1, source_target_pairs={{0,3},{1,2},{2,1},{3,0},{4,7},{5,6},{6,5},{7,4},{8,11},{9,10},{10,... | collective-permute-start | bytes 79880 | tf_op jit(solution)/shard_map/ppermute | solution.py:468
  67.8 3.3 %collective-permute-start.28 = (f32[52,128]{1,0:T(8,128)S(1)}, f32[52,128]{1,0:T(8,128)S(1)}, u32[]{:S(2)}, u32[]{:S(2)}) collective-permute-start(f32[52,128]{1,0:T(8,128)S(1)} %get-tuple-element.105.own_ref), channel_id=1, source_target_pairs={{0,1},{1,0},{2,3},{3,2},{4,5},{5,4},{6,7},{7,6},{8,9},{9,8},{10,11... | collective-permute-start | bytes 79880 | tf_op jit(solution)/shard_map/ppermute | solution.py:464
  68.3 5.0 %collective-permute-start.30 = (f32[96,128]{1,0:T(8,128)S(1)}, f32[96,128]{1,0:T(8,128)S(1)}, u32[]{:S(2)}, u32[]{:S(2)}) collective-permute-start(f32[96,128]{1,0:T(8,128)S(1)} %get-tuple-element.106), channel_id=1, source_target_pairs={{0,4},{1,5},{2,6},{3,7},{4,0},{5,1},{6,2},{7,3},{8,12},{9,13},{10,... | collective-permute-start | bytes 147464 | tf_op jit(solution)/shard_map/ppermute | solution.py:465
  71.0 2.3 %collective-permute-start.31 = (f32[96,128]{1,0:T(8,128)S(1)}, f32[96,128]{1,0:T(8,128)S(1)}, u32[]{:S(2)}, u32[]{:S(2)}) collective-permute-start(f32[96,128]{1,0:T(8,128)S(1)} %get-tuple-element.107), channel_id=1, source_target_pairs={{0,1},{1,0},{2,3},{3,2},{4,8},{5,9},{6,10},{7,11},{8,4},{9,5},{10,... | collective-permute-start | bytes 147464 | tf_op jit(solution)/shard_map/ppermute | solution.py:466
  71.1 3.3 %collective-permute-start.29 = (f32[52,128]{1,0:T(8,128)S(1)}, f32[52,128]{1,0:T(8,128)S(1)}, u32[]{:S(2)}, u32[]{:S(2)}) collective-permute-start(f32[52,128]{1,0:T(8,128)S(1)} %add.31.own), channel_id=1, source_target_pairs={{0,3},{1,2},{2,1},{3,0},{4,7},{5,6},{6,5},{7,4},{8,11},{9,10},{10,... | collective-permute-start | bytes 79880 | tf_op jit(solution)/shard_map/ppermute | solution.py:468

commit v3 on v2

--- a/solution.py
+++ b/solution.py
@@ -90,10 +90,10 @@
 
 
 def first_kernel(
-    flags, x_in, jac_in, rhs_in, diag_in, wcoef_in, ccoef_in,
+    flags, x_in, jac_in, rhs_in, wcoef_in,
     block_in, well_in, owner_in, rhs_well_in, inv_well_in,
-    x_ref, jac_ref, rhs_ref, inv_ref, row_ref, col_ref, pick_ref, spread_ref, well_ref, wc_ref,
-    cc_ref, m1_ref, m2_ref, m3_ref, m4_ref, wcoef, ccoef, xs_ref, g_ref,
+    x_ref, jac_ref, rhs_ref, row_ref, col_ref, pick_ref, spread_ref, well_ref, wc_ref,
+    half_ref, m1_ref, m2_ref, m3_ref, m4_ref, wcoef, xs_ref, g_ref,
     block_row, well_row, owner_row, rhs_well, inv_well, row_raw, col_raw, held, sems, small_sems,
 ):
     rows, cols = jac_in.shape[3], jac_in.shape[4]
@@ -106,12 +106,11 @@
     for copy in small:
         copy.start()
     pairs = [
-        (wcoef_in, wcoef), (ccoef_in, ccoef), (x_in, x_ref),
+        (wcoef_in, wcoef), (x_in, x_ref),
         (jac_in.at[1, :, :, 0], row_raw.at[0]),
         (jac_in.at[2, :, :, rows - 1], row_raw.at[1]),
         (jac_in.at[3, :, :, :, 0:8], col_raw.at[0]),
         (jac_in.at[4, :, :, :, cols - 8 : cols], col_raw.at[1]),
-        (diag_in, inv_ref),
         (jac_in.at[:, :, :, rows - 1], jac_ref.at[:, :, :, rows - 1]),
         (jac_in.at[:, :, :, 0:early], jac_ref.at[:, :, :, 0:early]), (rhs_in, rhs_ref),
     ]
@@ -131,7 +130,8 @@
     spread_ref[...] = spread
     pick = turned(eye, spread).astype(BF16)
     pick_ref[...] = pick
-    own_half = turned(eye, hot(iota((LANES, perfs), 0) // BLOCK == block % 2)) > 0.5
+    half_ref[...] = turned(eye, hot(iota((LANES, perfs), 0) // BLOCK == block % 2))
+    own_half = half_ref[...] > 0.5
     for h in range(width):
         slot = iota((LANES, perfs), 0) + h * LANES
         well = owner_row[...] * well_dev + well_row[...]
@@ -152,9 +152,6 @@
     for u in range(WELL_UNK):
         expanded(eye, wcoef, u, own_half, wc_ref)
     copies[1].wait()
-    for u in range(WELL_UNK):
-        expanded(eye, ccoef, u, own_half, cc_ref)
-    copies[2].wait()
 
     def write(row, value):
         m1_ref[base + row : base + row + 1, :] = value
@@ -162,7 +159,7 @@
     for r in range(PHASES):
         picked_rows(r, x_ref, pick_ref, xs_ref, g_ref)
     well_partials(pick_ref, well_ref, wc_ref, g_ref, write)
-    for copy in copies[3:7]:
+    for copy in copies[2:6]:
         copy.wait()
     row_ref[...] = row_raw[...].astype(F32)
     for r in range(PHASES):
@@ -171,9 +168,7 @@
                 col_ref[0, r, t, i : i + 1, :] = col_raw[0, r, t, i].astype(F32)[0:1]
                 col_ref[1, r, t, i : i + 1, :] = col_raw[1, r, t, i].astype(F32)[7:8]
     edge_messages(flags, x_ref, row_ref, col_ref, m1_ref, m2_ref, m3_ref, m4_ref)
-    copies[7].wait()
-    inv_ref[...] = 1.0 / inv_ref[...]
-    for copy in copies[8:]:
+    for copy in copies[6:]:
         copy.wait()
 
 
@@ -185,9 +180,9 @@
 def inner_kernel(widen, x_ref, jac_in, rhs_ref, *rest):
     rows, cols = jac_in.shape[3], jac_in.shape[4]
     early = rows // 4 + 2
-    z_ref = rest[1] if widen else rest[0]
+    z_ref = rest[0]
     if widen:
-        wide_ref, jac_ref, sems = rest[2:]
+        ccoef_in, diag_in, half_ref, z_ref, wide_ref, jac_ref, cc_ref, inv_ref, ccoef, sems = rest[1:]
 
         def fetch(row):
             return pltpu.make_async_copy(
@@ -196,6 +191,12 @@
 
         for row in range(early, rows - 1):
             fetch(row).start()
+        extra = [
+            pltpu.make_async_copy(ccoef_in, ccoef, sems.at[0]),
+            pltpu.make_async_copy(diag_in, inv_ref, sems.at[1]),
+        ]
+        for copy in extra:
+            copy.start()
     else:
         jac_ref = jac_in
     lane, col = iota((cols, LANES), 1), iota((cols, LANES), 0)
@@ -242,6 +243,14 @@
         return carry
 
     lax.fori_loop(0, rows, row_body, 0, unroll=1 if widen else 2)
+    if widen:
+        perfs = half_ref.shape[0]
+        eye = hot(iota((perfs, perfs), 0) == iota((perfs, perfs), 1))
+        for copy in extra:
+            copy.wait()
+        for u in range(WELL_UNK):
+            expanded(eye, ccoef, u, half_ref[...] > 0.5, cc_ref)
+        inv_ref[...] = 1.0 / inv_ref[...]
 
 
 def update_kernel(
@@ -251,8 +260,7 @@
     if last:
         x_out, adj_ref, rs_ref, x_ref, sems = rest
     else:
-        (row_ref, col_ref, pick_ref, wc_ref, x_ref, m1_ref, m2_ref, m3_ref, m4_ref,
-         rs_ref, xs_ref, g_ref) = rest
+        (row_ref, col_ref, x_ref, m1_ref, m2_ref, m3_ref, m4_ref, rs_ref) = rest
     cells, perfs = spread_ref.shape
     rows = (own.shape[0] - WELL_UNK * well_ref.shape[0]) // PHASES
     cols = cells // rows
@@ -299,8 +307,6 @@
         if last:
             copies.append(pltpu.make_async_copy(x_ref.at[t], x_out.at[t], sems.at[t]))
             copies[t].start()
-        else:
-            picked_rows(t, x_ref, pick_ref, xs_ref, g_ref)
     if last:
         well_dev = adj_ref.shape[1]
         mine = 0.0
@@ -316,10 +322,20 @@
     if not last:
         edge_messages(flags, x_ref, row_ref, col_ref, m1_ref, m2_ref, m3_ref, m4_ref)
 
-        def write(row, value):
-            m1_ref[base + row : base + row + 1, :] = value
-
-        well_partials(pick_ref, well_ref, wc_ref, g_ref, write)
+
+def wells_kernel(
+    x_ref, pick_ref, well_ref, wc_ref, halo_ref, pass_ref, m1_ref, passed_ref, xs_ref, g_ref
+):
+    base = halo_ref.shape[0]
+    m1_ref[0:base, :] = halo_ref[...]
+    passed_ref[...] = pass_ref[...]
+    for t in range(PHASES):
+        picked_rows(t, x_ref, pick_ref, xs_ref, g_ref)
+
+    def write(row, value):
+        m1_ref[base + row : base + row + 1, :] = value
+
+    well_partials(pick_ref, well_ref, wc_ref, g_ref, write)
 
 
 def gx_swap(gx, gy, parity):
@@ -379,24 +395,22 @@
             grid,
             shape(*jacobian.shape, dtype=BF16),
             grid,
-            grid,
             shape(2, PHASES, PHASES, cols, LANES),
             shape(2, PHASES, PHASES, rows, LANES),
             shape(perfs, cells, dtype=BF16),
             shape(cells, perfs, dtype=BF16),
             shape(width, perfs, LANES),
             shape(WELL_UNK, PHASES, perfs, LANES, dtype=BF16),
-            shape(WELL_UNK, PHASES, perfs, LANES, dtype=BF16),
+            shape(perfs, LANES),
             shape(full + 5 * unk, LANES),
             shape(base, LANES),
             shape(PHASES * cols, LANES),
             shape(PHASES * cols, LANES),
         ),
-        in_specs=[SM] + [HB] * 11,
-        out_specs=(VM,) * 15,
+        in_specs=[SM] + [HB] * 9,
+        out_specs=(VM,) * 14,
         scratch_shapes=[
             pltpu.VMEM(well_coupling.shape, BF16),
-            pltpu.VMEM(cell_coupling.shape, BF16),
             pltpu.VMEM((PHASES, cells, 2 * LANES), BF16),
             pltpu.VMEM((PHASES, perfs, LANES), F32),
             pltpu.VMEM((1, perfs), jnp.int32),
@@ -407,19 +421,19 @@
             pltpu.VMEM((2, PHASES, PHASES, cols, LANES), BF16),
             pltpu.VMEM((2, PHASES, PHASES, rows, 8, LANES), BF16),
             pltpu.VMEM((24, LANES), F32),
-            pltpu.SemaphoreType.DMA((11,)),
+            pltpu.SemaphoreType.DMA((9,)),
             pltpu.SemaphoreType.DMA((5,)),
         ],
         compiler_params=PARAMS,
         name="first",
     )
-    (x, jac_part, rhs, inv, row_edges, col_edges, pick, spread, well_hot, wc, cc, m1, m2_halo, m3,
+    (x, jac_part, rhs, row_edges, col_edges, pick, spread, well_hot, wc, own_half, m1, m2_halo, m3,
      m4) = first(
         flags,
         *[
             in_hbm(v)
             for v in (
-                x, jacobian, rhs, diag, well_coupling, cell_coupling,
+                x, jacobian, rhs, well_coupling,
                 perf_block.reshape(1, perfs), perf_well.reshape(1, perfs),
                 perf_owner.reshape(1, perfs), well_rhs, well_inverse,
             )
@@ -436,17 +450,26 @@
             name="add",
         )(kept, own, got)
 
-    def inner_first(x, jac, rhs, jac_part):
+    def inner_first(x, jac, rhs, jac_part, own_half):
         return pl.pallas_call(
             functools.partial(inner_kernel, True),
-            out_shape=(grid, shape(*jac.shape), shape(*jac.shape, dtype=BF16)),
-            in_specs=[VM, HB, VM, VM],
-            out_specs=(VM,) * 3,
-            scratch_shapes=[pltpu.SemaphoreType.DMA((rows,))],
+            out_shape=(
+                grid,
+                shape(*jac.shape),
+                shape(*jac.shape, dtype=BF16),
+                shape(WELL_UNK, PHASES, perfs, LANES, dtype=BF16),
+                grid,
+            ),
+            in_specs=[VM, HB, VM, VM, HB, HB, VM],
+            out_specs=(VM,) * 5,
+            scratch_shapes=[
+                pltpu.VMEM(cell_coupling.shape, BF16),
+                pltpu.SemaphoreType.DMA((rows,)),
+            ],
             input_output_aliases={3: 2},
             compiler_params=PARAMS,
             name="inner_widen",
-        )(x, in_hbm(jac), rhs, jac_part)[:2]
+        )(x, in_hbm(jac), rhs, jac_part, in_hbm(cell_coupling), in_hbm(diag), own_half)
 
     inner = pl.pallas_call(
         functools.partial(inner_kernel, False),
@@ -476,7 +499,7 @@
             wconst = own[full:] + g2[full:]
             own, g1, g2 = own[:full], g1[:full], g2[:full]
         if sweep == 0:
-            z, jac = inner_first(x, jacobian, rhs, jac_part)
+            z, jac, _, cc, inv = inner_first(x, jacobian, rhs, jac_part, own_half)
         else:
             z = inner(x, jac, rhs)
         operands = (flags, z, own, g1, g2, g3, g4, wconst, inv, spread, well_hot, cc)
@@ -495,25 +518,33 @@
                 name="update_last",
             )(*operands)
         else:
-            x, m1, m2_halo, m3, m4 = pl.pallas_call(
+            x, m1_halo, m2_halo, m3, m4 = pl.pallas_call(
                 functools.partial(update_kernel, False),
                 out_shape=(
                     shape(phases, cells, layers),
-                    shape(full, LANES),
+                    shape(base, LANES),
                     shape(base, LANES),
                     shape(PHASES * cols, LANES),
                     shape(PHASES * cols, LANES),
                 ),
-                in_specs=[SM] + [VM] * 15,
+                in_specs=[SM] + [VM] * 13,
                 out_specs=(VM,) * 5,
-                scratch_shapes=work
-                + [
+                scratch_shapes=work,
+                compiler_params=PARAMS,
+                name="update",
+            )(*operands, row_edges, col_edges)
+            m1, m4 = pl.pallas_call(
+                wells_kernel,
+                out_shape=(shape(full, LANES), shape(*m4.shape)),
+                in_specs=[VM] * 6,
+                out_specs=(VM,) * 2,
+                scratch_shapes=[
                     pltpu.VMEM((PHASES, cells, 2 * LANES), BF16),
                     pltpu.VMEM((PHASES, perfs, LANES), F32),
                 ],
                 compiler_params=PARAMS,
-                name="update",
-            )(*operands, row_edges, col_edges, pick, wc)
+                name="wells",
+            )(x, pick, well_hot, wc, m1_halo, m4)
     return x.reshape(adjoint_init.shape), adj
 
 

time: 77.4 us -> 76.4 us (0.987)
  Pallas kernels: 36.2 us -> 35.2 us
    pallas_call x7, Pallas kernels: 13.9 us -> 9.1 us  [body(): pl.pallas_call(functools.partial(update_kernel, False), out_shape=(shape(...]
    pallas_call x1 -> x8, Pallas kernels: 5.93 us -> 9.21 us  [the longest x1 4.91 us: body(): first(flags, *[in_hbm(v) for v in (x, jacobian, rhs, well_coupling, perf_...]
  transfers between devices with their start and end apart: 32 -> 32, of which waited for: 15 -> 15; matrix products, arithmetic and copies ran while one was open for 0% -> 0% of each run, Pallas kernels for 18% -> 19%
where the time goes in v3:
time: 76.4 us; the launch traced here: 76.3 us
  Pallas kernels  35.2 us (46%)
  starting transfers between devices  29.5 us (39%)
  waiting for transfers between devices  10.5 us (14%)
  between operations  0.9 us (1%)
    ppermute x8, starting transfers between devices, body(): g3 = lax.ppermute(m3, both, gx_swap(gx, gy, 0))  19.2 us
    pallas_call x7, Pallas kernels, body(): z = inner(x, jac, rhs)  10.4 us
    pallas_call x7, Pallas kernels, body(): pl.pallas_call(functools.partial(update_kernel, False), out_shape=(shape(...  9.1 us
    ppermute x8, waiting for transfers between devices, body(): g2 = lax.ppermute(own, 'gy', gy_swap(gy, 1))  7.89 us
    ppermute x8, starting transfers between devices, body(): g2 = lax.ppermute(own, 'gy', gy_swap(gy, 1))  5.88 us
    pallas_call x1, Pallas kernels, body(): first(flags, *[in_hbm(v) for v in (x, jacobian, rhs, well_coupling, perf_...  4.91 us
    pallas_call x7, Pallas kernels, body(): pl.pallas_call(wells_kernel, out_shape=(shape(full, LANES), shape(*m4.sha...  4.3 us
    pallas_call x1, Pallas kernels, inner_first(): pl.pallas_call(functools.partial(inner_kernel, True), out_shape=(grid, sh...  3.82 us
  transfers between devices with their start and end apart: 32, of which 15 were waited for; matrix products, arithmetic and copies ran while one was open for 0% of the time, Pallas kernels for 19%

profile of v3, /device:TPU:0, one launch (start us, length us, event | category | flops | bytes accessed | tf_op | source)
XLA Modules:
  0.0 76.3 jit_solution(13383234294303361707)
XLA Ops:
  0.7 4.9 %first.1 = (f32[3,512,128]{2,1,0:T(8,128)S(1)}, bf16[7,3,3,16,32,128]{5,4,3,2,1,0:T(8,128)(2,1)S(1)}, f32[3,512,128]{2,1,0:T(8,128)S(1)}, f32[2,3,3,32,128]{4,3,...) custom-call(s32[5]{0:T(128)S(1)} %stack.31.flags, ...), custom_call_target="tpu_custom_call" | custom-call | tf_op jit(solution)/shard_map/first/pallas_call | solution.py:431
  7.1 2.6 %collective-permute-start.1 = (f32[72,128]{1,0:T(8,128)S(1)}, f32[72,128]{1,0:T(8,128)S(1)}, u32[]{:S(2)}, u32[]{:S(2)}) collective-permute-start(f32[72,128]{1,0:T(8,128)S(1)} %add.24), channel_id=1, source_target_pairs={{0,3},{1,2},{2,1},{3,0},{4,7},{5,6},{6,5},{7,4},{8,11},{9,10},{10,... | collective-permute-start | bytes 110600 | tf_op jit(solution)/shard_map/ppermute | solution.py:491
  9.7 1.5 %collective-permute-start.2 = (f32[96,128]{1,0:T(8,128)S(1)}, f32[96,128]{1,0:T(8,128)S(1)}, u32[]{:S(2)}, u32[]{:S(2)}) collective-permute-start(f32[96,128]{1,0:T(8,128)S(1)} %get-tuple-element.78), channel_id=1, source_target_pairs={{0,4},{1,5},{2,6},{3,7},{4,0},{5,1},{6,2},{7,3},{8,12},{9,13},{10,... | collective-permute-start | bytes 147464 | tf_op jit(solution)/shard_map/ppermute | solution.py:488
  11.2 3.8 %inner_widen.1 = (f32[3,512,128]{2,1,0:T(8,128)S(1)}, f32[7,3,3,16,32,128]{5,4,3,2,1,0:T(8,128)S(1)}, bf16[7,3,3,16,32,128]{5,4,3,2,1,0:T(8,128)(2,1)S(1)}, bf16...) custom-call(f32[3,512,128]{2,1,0:T(8,128)S(1)} %get-tuple-element.71.x_ref, ...), custom_call_target="tpu_custom_call", output_to_operand_aliasing={{2}: (3, {})} | custom-call | tf_op jit(solution)/shard_map/inner_widen/pallas_call | solution.py:454
  15.2 1.3 %update.7 = (f32[3,512,128]{2,1,0:T(8,128)S(1)}, f32[48,128]{1,0:T(8,128)S(1)}, f32[48,128]{1,0:T(8,128)S(1)}, f32[96,128]{1,0:T(8,128)S(1)}, f32[96,128]{1,0:T(8,128)S(1)}) custom-call(s32[5]{0:T(128)S(1)} %stack.31.flags, f32[3,512,128]{2,1,0:T(8,128)S(1)} %get-tuple-element.75.z_ref, f32[52,128]{1,0:T(8,128)S(1)} %slice.20.own, f32[52,128]{1,0:T(8,128)S(1)} %slice.21.g1, ...), custom_call_target="tpu_custom_call" | custom-call | tf_op jit(solution)/shard_map/update/pallas_call | solution.py:521
  17.6 2.6 %collective-permute-start.6 = (f32[96,128]{1,0:T(8,128)S(1)}, f32[96,128]{1,0:T(8,128)S(1)}, u32[]{:S(2)}, u32[]{:S(2)}) collective-permute-start(f32[96,128]{1,0:T(8,128)S(1)} %get-tuple-element.94), channel_id=1, source_target_pairs={{0,4},{1,5},{2,6},{3,7},{4,0},{5,1},{6,2},{7,3},{8,12},{9,13},{10,... | collective-permute-start | bytes 147464 | tf_op jit(solution)/shard_map/ppermute | solution.py:488
  20.8 1.5 %inner.7.z_ref = f32[3,512,128]{2,1,0:T(8,128)S(1)} custom-call(f32[3,512,128]{2,1,0:T(8,128)S(1)} %get-tuple-element.86.x_ref, f32[7,3,3,16,32,128]{5,4,3,2,1,0:T(8,128)S(1)} %get-tuple-element.87.jac_in, f32[3,512,128]{2,1,0:T(8,128)S(1)} %get-tuple-element.72.rhs_ref), custom_call_target="tpu_custom_call" | custom-call | tf_op jit(solution)/shard_map/inner/pallas_call | solution.py:504
  22.5 1.2 %collective-permute-done.5.g2 = f32[52,128]{1,0:T(8,128)S(1)} collective-permute-done((f32[52,128]{1,0:T(8,128)S(1)}, f32[52,128]{1,0:T(8,128)S(1)}, u32[]{:S(2)}, u32[]{:S(2)}) %collective-permute-start.5) | collective-permute-done | bytes 26656 | tf_op jit(solution)/shard_map/ppermute | solution.py:491
  23.7 1.3 %update.8 = (f32[3,512,128]{2,1,0:T(8,128)S(1)}, f32[48,128]{1,0:T(8,128)S(1)}, f32[48,128]{1,0:T(8,128)S(1)}, f32[96,128]{1,0:T(8,128)S(1)}, f32[96,128]{1,0:T(8,128)S(1)}) custom-call(s32[5]{0:T(128)S(1)} %stack.31.flags, f32[3,512,128]{2,1,0:T(8,128)S(1)} %inner.7.z_ref, f32[52,128]{1,0:T(8,128)S(1)} %add.25.own, ...), custom_call_target="tpu_custom_call" | custom-call | tf_op jit(solution)/shard_map/update/pallas_call | solution.py:521
  26.0 2.9 %collective-permute-start.10 = (f32[96,128]{1,0:T(8,128)S(1)}, f32[96,128]{1,0:T(8,128)S(1)}, u32[]{:S(2)}, u32[]{:S(2)}) collective-permute-start(f32[96,128]{1,0:T(8,128)S(1)} %get-tuple-element.101), channel_id=1, source_target_pairs={{0,4},{1,5},{2,6},{3,7},{4,0},{5,1},{6,2},{7,3},{8,12},{9,13},{10,... | collective-permute-start | bytes 147464 | tf_op jit(solution)/shard_map/ppermute | solution.py:488
  29.6 1.5 %inner.8.z_ref = f32[3,512,128]{2,1,0:T(8,128)S(1)} custom-call(f32[3,512,128]{2,1,0:T(8,128)S(1)} %get-tuple-element.96.x_ref, f32[7,3,3,16,32,128]{5,4,3,2,1,0:T(8,128)S(1)} %get-tuple-element.87.jac_in, f32[3,512,128]{2,1,0:T(8,128)S(1)} %get-tuple-element.72.rhs_ref), custom_call_target="tpu_custom_call" | custom-call | tf_op jit(solution)/shard_map/inner/pallas_call | solution.py:504
  31.2 1.2 %collective-permute-done.9.g2 = f32[52,128]{1,0:T(8,128)S(1)} collective-permute-done((f32[52,128]{1,0:T(8,128)S(1)}, f32[52,128]{1,0:T(8,128)S(1)}, u32[]{:S(2)}, u32[]{:S(2)}) %collective-permute-start.9) | collective-permute-done | bytes 26656 | tf_op jit(solution)/shard_map/ppermute | solution.py:491
  32.4 1.3 %update.9 = (f32[3,512,128]{2,1,0:T(8,128)S(1)}, f32[48,128]{1,0:T(8,128)S(1)}, f32[48,128]{1,0:T(8,128)S(1)}, f32[96,128]{1,0:T(8,128)S(1)}, f32[96,128]{1,0:T(8,128)S(1)}) custom-call(s32[5]{0:T(128)S(1)} %stack.31.flags, f32[3,512,128]{2,1,0:T(8,128)S(1)} %inner.8.z_ref, f32[52,128]{1,0:T(8,128)S(1)} %add.26.own, ...), custom_call_target="tpu_custom_call" | custom-call | tf_op jit(solution)/shard_map/update/pallas_call | solution.py:521
  34.7 2.9 %collective-permute-start.14 = (f32[96,128]{1,0:T(8,128)S(1)}, f32[96,128]{1,0:T(8,128)S(1)}, u32[]{:S(2)}, u32[]{:S(2)}) collective-permute-start(f32[96,128]{1,0:T(8,128)S(1)} %get-tuple-element.108), channel_id=1, source_target_pairs={{0,4},{1,5},{2,6},{3,7},{4,0},{5,1},{6,2},{7,3},{8,12},{9,13},{10,... | collective-permute-start | bytes 147464 | tf_op jit(solution)/shard_map/ppermute | solution.py:488
  38.2 1.5 %inner.9.z_ref = f32[3,512,128]{2,1,0:T(8,128)S(1)} custom-call(f32[3,512,128]{2,1,0:T(8,128)S(1)} %get-tuple-element.103.x_ref, f32[7,3,3,16,32,128]{5,4,3,2,1,0:T(8,128)S(1)} %get-tuple-element.87.jac_in, f32[3,512,128]{2,1,0:T(8,128)S(1)} %get-tuple-element.72.rhs_ref), custom_call_target="tpu_custom_call" | custom-call | tf_op jit(solution)/shard_map/inner/pallas_call | solution.py:504
  40.0 1.2 %collective-permute-done.13.g2 = f32[52,128]{1,0:T(8,128)S(1)} collective-permute-done((f32[52,128]{1,0:T(8,128)S(1)}, f32[52,128]{1,0:T(8,128)S(1)}, u32[]{:S(2)}, u32[]{:S(2)}) %collective-permute-start.13) | collective-permute-done | bytes 26656 | tf_op jit(solution)/shard_map/ppermute | solution.py:491
  41.1 1.3 %update.10 = (f32[3,512,128]{2,1,0:T(8,128)S(1)}, f32[48,128]{1,0:T(8,128)S(1)}, f32[48,128]{1,0:T(8,128)S(1)}, f32[96,128]{1,0:T(8,128)S(1)}, f32[96,128]{1,0:T(8,128)S(1)}) custom-call(s32[5]{0:T(128)S(1)} %stack.31.flags, f32[3,512,128]{2,1,0:T(8,128)S(1)} %inner.9.z_ref, f32[52,128]{1,0:T(8,128)S(1)} %add.27.own, ...), custom_call_target="tpu_custom_call" | custom-call | tf_op jit(solution)/shard_map/update/pallas_call | solution.py:521
  43.5 1.6 %collective-permute-start.18 = (f32[96,128]{1,0:T(8,128)S(1)}, f32[96,128]{1,0:T(8,128)S(1)}, u32[]{:S(2)}, u32[]{:S(2)}) collective-permute-start(f32[96,128]{1,0:T(8,128)S(1)} %get-tuple-element.115), channel_id=1, source_target_pairs={{0,4},{1,5},{2,6},{3,7},{4,0},{5,1},{6,2},{7,3},{8,12},{9,13},{10,... | collective-permute-start | bytes 147464 | tf_op jit(solution)/shard_map/ppermute | solution.py:488
  45.7 1.5 %inner.10.z_ref = f32[3,512,128]{2,1,0:T(8,128)S(1)} custom-call(f32[3,512,128]{2,1,0:T(8,128)S(1)} %get-tuple-element.110.x_ref, f32[7,3,3,16,32,128]{5,4,3,2,1,0:T(8,128)S(1)} %get-tuple-element.87.jac_in, f32[3,512,128]{2,1,0:T(8,128)S(1)} %get-tuple-element.72.rhs_ref), custom_call_target="tpu_custom_call" | custom-call | tf_op jit(solution)/shard_map/inner/pallas_call | solution.py:504
  48.5 1.3 %update.11 = (f32[3,512,128]{2,1,0:T(8,128)S(1)}, f32[48,128]{1,0:T(8,128)S(1)}, f32[48,128]{1,0:T(8,128)S(1)}, f32[96,128]{1,0:T(8,128)S(1)}, f32[96,128]{1,0:T(8,128)S(1)}) custom-call(s32[5]{0:T(128)S(1)} %stack.31.flags, f32[3,512,128]{2,1,0:T(8,128)S(1)} %inner.10.z_ref, f32[52,128]{1,0:T(8,128)S(1)} %add.28.own, ...), custom_call_target="tpu_custom_call" | custom-call | tf_op jit(solution)/shard_map/update/pallas_call | solution.py:521
  50.9 3.0 %collective-permute-start.22 = (f32[96,128]{1,0:T(8,128)S(1)}, f32[96,128]{1,0:T(8,128)S(1)}, u32[]{:S(2)}, u32[]{:S(2)}) collective-permute-start(f32[96,128]{1,0:T(8,128)S(1)} %get-tuple-element.122), channel_id=1, source_target_pairs={{0,4},{1,5},{2,6},{3,7},{4,0},{5,1},{6,2},{7,3},{8,12},{9,13},{10,... | collective-permute-start | bytes 147464 | tf_op jit(solution)/shard_map/ppermute | solution.py:488
  54.5 1.5 %inner.11.z_ref = f32[3,512,128]{2,1,0:T(8,128)S(1)} custom-call(f32[3,512,128]{2,1,0:T(8,128)S(1)} %get-tuple-element.117.x_ref, f32[7,3,3,16,32,128]{5,4,3,2,1,0:T(8,128)S(1)} %get-tuple-element.87.jac_in, f32[3,512,128]{2,1,0:T(8,128)S(1)} %get-tuple-element.72.rhs_ref), custom_call_target="tpu_custom_call" | custom-call | tf_op jit(solution)/shard_map/inner/pallas_call | solution.py:504
  56.1 1.2 %collective-permute-done.21.g2 = f32[52,128]{1,0:T(8,128)S(1)} collective-permute-done((f32[52,128]{1,0:T(8,128)S(1)}, f32[52,128]{1,0:T(8,128)S(1)}, u32[]{:S(2)}, u32[]{:S(2)}) %collective-permute-start.21) | collective-permute-done | bytes 26656 | tf_op jit(solution)/shard_map/ppermute | solution.py:491
  57.3 1.3 %update.12 = (f32[3,512,128]{2,1,0:T(8,128)S(1)}, f32[48,128]{1,0:T(8,128)S(1)}, f32[48,128]{1,0:T(8,128)S(1)}, f32[96,128]{1,0:T(8,128)S(1)}, f32[96,128]{1,0:T(8,128)S(1)}) custom-call(s32[5]{0:T(128)S(1)} %stack.31.flags, f32[3,512,128]{2,1,0:T(8,128)S(1)} %inner.11.z_ref, f32[52,128]{1,0:T(8,128)S(1)} %add.29.own, ...), custom_call_target="tpu_custom_call" | custom-call | tf_op jit(solution)/shard_map/update/pallas_call | solution.py:521
  59.7 1.7 %collective-permute-start.26 = (f32[96,128]{1,0:T(8,128)S(1)}, f32[96,128]{1,0:T(8,128)S(1)}, u32[]{:S(2)}, u32[]{:S(2)}) collective-permute-start(f32[96,128]{1,0:T(8,128)S(1)} %get-tuple-element.129), channel_id=1, source_target_pairs={{0,4},{1,5},{2,6},{3,7},{4,0},{5,1},{6,2},{7,3},{8,12},{9,13},{10,... | collective-permute-start | bytes 147464 | tf_op jit(solution)/shard_map/ppermute | solution.py:488
  62.0 1.5 %inner.12.z_ref = f32[3,512,128]{2,1,0:T(8,128)S(1)} custom-call(f32[3,512,128]{2,1,0:T(8,128)S(1)} %get-tuple-element.124.x_ref, f32[7,3,3,16,32,128]{5,4,3,2,1,0:T(8,128)S(1)} %get-tuple-element.87.jac_in, f32[3,512,128]{2,1,0:T(8,128)S(1)} %get-tuple-element.72.rhs_ref), custom_call_target="tpu_custom_call" | custom-call | tf_op jit(solution)/shard_map/inner/pallas_call | solution.py:504
  63.8 1.1 %collective-permute-done.25.g2 = f32[52,128]{1,0:T(8,128)S(1)} collective-permute-done((f32[52,128]{1,0:T(8,128)S(1)}, f32[52,128]{1,0:T(8,128)S(1)}, u32[]{:S(2)}, u32[]{:S(2)}) %collective-permute-start.25) | collective-permute-done | bytes 26656 | tf_op jit(solution)/shard_map/ppermute | solution.py:491
  64.9 1.3 %update.13 = (f32[3,512,128]{2,1,0:T(8,128)S(1)}, f32[48,128]{1,0:T(8,128)S(1)}, f32[48,128]{1,0:T(8,128)S(1)}, f32[96,128]{1,0:T(8,128)S(1)}, f32[96,128]{1,0:T(8,128)S(1)}) custom-call(s32[5]{0:T(128)S(1)} %stack.31.flags, f32[3,512,128]{2,1,0:T(8,128)S(1)} %inner.12.z_ref, f32[52,128]{1,0:T(8,128)S(1)} %add.30.own, ...), custom_call_target="tpu_custom_call" | custom-call | tf_op jit(solution)/shard_map/update/pallas_call | solution.py:521
  67.2 3.0 %collective-permute-start.30 = (f32[96,128]{1,0:T(8,128)S(1)}, f32[96,128]{1,0:T(8,128)S(1)}, u32[]{:S(2)}, u32[]{:S(2)}) collective-permute-start(f32[96,128]{1,0:T(8,128)S(1)} %get-tuple-element.136), channel_id=1, source_target_pairs={{0,4},{1,5},{2,6},{3,7},{4,0},{5,1},{6,2},{7,3},{8,12},{9,13},{10,... | collective-permute-start | bytes 147464 | tf_op jit(solution)/shard_map/ppermute | solution.py:488
  70.6 1.5 %inner.13.z_ref = f32[3,512,128]{2,1,0:T(8,128)S(1)} custom-call(f32[3,512,128]{2,1,0:T(8,128)S(1)} %get-tuple-element.131.x_ref, f32[7,3,3,16,32,128]{5,4,3,2,1,0:T(8,128)S(1)} %get-tuple-element.87.jac_in, f32[3,512,128]{2,1,0:T(8,128)S(1)} %get-tuple-element.72.rhs_ref), custom_call_target="tpu_custom_call" | custom-call | tf_op jit(solution)/shard_map/inner/pallas_call | solution.py:504
  72.5 1.2 %collective-permute-done.29.g2 = f32[52,128]{1,0:T(8,128)S(1)} collective-permute-done((f32[52,128]{1,0:T(8,128)S(1)}, f32[52,128]{1,0:T(8,128)S(1)}, u32[]{:S(2)}, u32[]{:S(2)}) %collective-permute-start.29) | collective-permute-done | bytes 26656 | tf_op jit(solution)/shard_map/ppermute | solution.py:491
  73.6 2.6 %update_last.1 = (f32[3,512,128]{2,1,0:T(8,128)}, f32[4,32]{1,0:T(4,128)}) custom-call(s32[5]{0:T(128)S(1)} %stack.31.flags, f32[3,512,128]{2,1,0:T(8,128)S(1)} %inner.13.z_ref, f32[52,128]{1,0:T(8,128)S(1)} %add.31.own, f32[52,128]{1,0:T(8,128)S(1)} %collective-permute-done.28.got_ref.g1, f32[52,128]{1,0:T(8,128)S(1)} %collective-permute-done.29.g2, ...), custom_call_target="tpu_custom_call" | custom-call | tf_op jit(solution)/shard_map/update_last/pallas_call | solution.py:507
  (69 shorter events, 15.7 us)
Async XLA Ops:
  5.7 1.4 %collective-permute-start = (f32[72,128]{1,0:T(8,128)S(1)}, f32[72,128]{1,0:T(8,128)S(1)}, u32[]{:S(2)}, u32[]{:S(2)}) collective-permute-start(f32[72,128]{1,0:T(8,128)S(1)} %get-tuple-element.77.own_ref), channel_id=1, source_target_pairs={{0,1},{1,0},{2,3},{3,2},{4,5},{5,4},{6,7},{7,6},{8,9},{9,8},{10,11... | collective-permute-start | bytes 110600 | tf_op jit(solution)/shard_map/ppermute | solution.py:487
  7.1 8.0 %collective-permute-start.1 = (f32[72,128]{1,0:T(8,128)S(1)}, f32[72,128]{1,0:T(8,128)S(1)}, u32[]{:S(2)}, u32[]{:S(2)}) collective-permute-start(f32[72,128]{1,0:T(8,128)S(1)} %add.24), channel_id=1, source_target_pairs={{0,3},{1,2},{2,1},{3,0},{4,7},{5,6},{6,5},{7,4},{8,11},{9,10},{10,... | collective-permute-start | bytes 110600 | tf_op jit(solution)/shard_map/ppermute | solution.py:491
  9.7 5.4 %collective-permute-start.2 = (f32[96,128]{1,0:T(8,128)S(1)}, f32[96,128]{1,0:T(8,128)S(1)}, u32[]{:S(2)}, u32[]{:S(2)}) collective-permute-start(f32[96,128]{1,0:T(8,128)S(1)} %get-tuple-element.78), channel_id=1, source_target_pairs={{0,4},{1,5},{2,6},{3,7},{4,0},{5,1},{6,2},{7,3},{8,12},{9,13},{10,... | collective-permute-start | bytes 147464 | tf_op jit(solution)/shard_map/ppermute | solution.py:488
  11.2 4.0 %collective-permute-start.3 = (f32[96,128]{1,0:T(8,128)S(1)}, f32[96,128]{1,0:T(8,128)S(1)}, u32[]{:S(2)}, u32[]{:S(2)}) collective-permute-start(f32[96,128]{1,0:T(8,128)S(1)} %get-tuple-element.79), channel_id=1, source_target_pairs={{0,1},{1,0},{2,3},{3,2},{4,8},{5,9},{6,10},{7,11},{8,4},{9,5},{10,... | collective-permute-start | bytes 147464 | tf_op jit(solution)/shard_map/ppermute | solution.py:489
  17.1 3.3 %collective-permute-start.4 = (f32[52,128]{1,0:T(8,128)S(1)}, f32[52,128]{1,0:T(8,128)S(1)}, u32[]{:S(2)}, u32[]{:S(2)}) collective-permute-start(f32[52,128]{1,0:T(8,128)S(1)} %get-tuple-element.93.own_ref), channel_id=1, source_target_pairs={{0,1},{1,0},{2,3},{3,2},{4,5},{5,4},{6,7},{7,6},{8,9},{9,8},{10,11... | collective-permute-start | bytes 79880 | tf_op jit(solution)/shard_map/ppermute | solution.py:487
  17.6 4.9 %collective-permute-start.6 = (f32[96,128]{1,0:T(8,128)S(1)}, f32[96,128]{1,0:T(8,128)S(1)}, u32[]{:S(2)}, u32[]{:S(2)}) collective-permute-start(f32[96,128]{1,0:T(8,128)S(1)} %get-tuple-element.94), channel_id=1, source_target_pairs={{0,4},{1,5},{2,6},{3,7},{4,0},{5,1},{6,2},{7,3},{8,12},{9,13},{10,... | collective-permute-start | bytes 147464 | tf_op jit(solution)/shard_map/ppermute | solution.py:488
  20.2 2.3 %collective-permute-start.7 = (f32[96,128]{1,0:T(8,128)S(1)}, f32[96,128]{1,0:T(8,128)S(1)}, u32[]{:S(2)}, u32[]{:S(2)}) collective-permute-start(f32[96,128]{1,0:T(8,128)S(1)} %get-tuple-element.95), channel_id=1, source_target_pairs={{0,1},{1,0},{2,3},{3,2},{4,8},{5,9},{6,10},{7,11},{8,4},{9,5},{10,... | collective-permute-start | bytes 147464 | tf_op jit(solution)/shard_map/ppermute | solution.py:489
  20.4 3.3 %collective-permute-start.5 = (f32[52,128]{1,0:T(8,128)S(1)}, f32[52,128]{1,0:T(8,128)S(1)}, u32[]{:S(2)}, u32[]{:S(2)}) collective-permute-start(f32[52,128]{1,0:T(8,128)S(1)} %add.25.own), channel_id=1, source_target_pairs={{0,3},{1,2},{2,1},{3,0},{4,7},{5,6},{6,5},{7,4},{8,11},{9,10},{10,... | collective-permute-start | bytes 79880 | tf_op jit(solution)/shard_map/ppermute | solution.py:491
  25.6 3.4 %collective-permute-start.8 = (f32[52,128]{1,0:T(8,128)S(1)}, f32[52,128]{1,0:T(8,128)S(1)}, u32[]{:S(2)}, u32[]{:S(2)}) collective-permute-start(f32[52,128]{1,0:T(8,128)S(1)} %get-tuple-element.100.own_ref), channel_id=1, source_target_pairs={{0,1},{1,0},{2,3},{3,2},{4,5},{5,4},{6,7},{7,6},{8,9},{9,8},{10,11... | collective-permute-start | bytes 79880 | tf_op jit(solution)/shard_map/ppermute | solution.py:487
  26.0 5.2 %collective-permute-start.10 = (f32[96,128]{1,0:T(8,128)S(1)}, f32[96,128]{1,0:T(8,128)S(1)}, u32[]{:S(2)}, u32[]{:S(2)}) collective-permute-start(f32[96,128]{1,0:T(8,128)S(1)} %get-tuple-element.101), channel_id=1, source_target_pairs={{0,4},{1,5},{2,6},{3,7},{4,0},{5,1},{6,2},{7,3},{8,12},{9,13},{10,... | collective-permute-start | bytes 147464 | tf_op jit(solution)/shard_map/ppermute | solution.py:488
  28.9 2.3 %collective-permute-start.11 = (f32[96,128]{1,0:T(8,128)S(1)}, f32[96,128]{1,0:T(8,128)S(1)}, u32[]{:S(2)}, u32[]{:S(2)}) collective-permute-start(f32[96,128]{1,0:T(8,128)S(1)} %get-tuple-element.102), channel_id=1, source_target_pairs={{0,1},{1,0},{2,3},{3,2},{4,8},{5,9},{6,10},{7,11},{8,4},{9,5},{10,... | collective-permute-start | bytes 147464 | tf_op jit(solution)/shard_map/ppermute | solution.py:489
  29.0 3.4 %collective-permute-start.9 = (f32[52,128]{1,0:T(8,128)S(1)}, f32[52,128]{1,0:T(8,128)S(1)}, u32[]{:S(2)}, u32[]{:S(2)}) collective-permute-start(f32[52,128]{1,0:T(8,128)S(1)} %add.26.own), channel_id=1, source_target_pairs={{0,3},{1,2},{2,1},{3,0},{4,7},{5,6},{6,5},{7,4},{8,11},{9,10},{10,... | collective-permute-start | bytes 79880 | tf_op jit(solution)/shard_map/ppermute | solution.py:491
  34.3 3.5 %collective-permute-start.12 = (f32[52,128]{1,0:T(8,128)S(1)}, f32[52,128]{1,0:T(8,128)S(1)}, u32[]{:S(2)}, u32[]{:S(2)}) collective-permute-start(f32[52,128]{1,0:T(8,128)S(1)} %get-tuple-element.107.own_ref), channel_id=1, source_target_pairs={{0,1},{1,0},{2,3},{3,2},{4,5},{5,4},{6,7},{7,6},{8,9},{9,8},{10,11... | collective-permute-start | bytes 79880 | tf_op jit(solution)/shard_map/ppermute | solution.py:487
  34.7 5.2 %collective-permute-start.14 = (f32[96,128]{1,0:T(8,128)S(1)}, f32[96,128]{1,0:T(8,128)S(1)}, u32[]{:S(2)}, u32[]{:S(2)}) collective-permute-start(f32[96,128]{1,0:T(8,128)S(1)} %get-tuple-element.108), channel_id=1, source_target_pairs={{0,4},{1,5},{2,6},{3,7},{4,0},{5,1},{6,2},{7,3},{8,12},{9,13},{10,... | collective-permute-start | bytes 147464 | tf_op jit(solution)/shard_map/ppermute | solution.py:488
  37.7 2.3 %collective-permute-start.15 = (f32[96,128]{1,0:T(8,128)S(1)}, f32[96,128]{1,0:T(8,128)S(1)}, u32[]{:S(2)}, u32[]{:S(2)}) collective-permute-start(f32[96,128]{1,0:T(8,128)S(1)} %get-tuple-element.109), channel_id=1, source_target_pairs={{0,1},{1,0},{2,3},{3,2},{4,8},{5,9},{6,10},{7,11},{8,4},{9,5},{10,... | collective-permute-start | bytes 147464 | tf_op jit(solution)/shard_map/ppermute | solution.py:489
  37.8 3.3 %collective-permute-start.13 = (f32[52,128]{1,0:T(8,128)S(1)}, f32[52,128]{1,0:T(8,128)S(1)}, u32[]{:S(2)}, u32[]{:S(2)}) collective-permute-start(f32[52,128]{1,0:T(8,128)S(1)} %add.27.own), channel_id=1, source_target_pairs={{0,3},{1,2},{2,1},{3,0},{4,7},{5,6},{6,5},{7,4},{8,11},{9,10},{10,... | collective-permute-start | bytes 79880 | tf_op jit(solution)/shard_map/ppermute | solution.py:491
  43.1 2.2 %collective-permute-start.16 = (f32[52,128]{1,0:T(8,128)S(1)}, f32[52,128]{1,0:T(8,128)S(1)}, u32[]{:S(2)}, u32[]{:S(2)}) collective-permute-start(f32[52,128]{1,0:T(8,128)S(1)} %get-tuple-element.114.own_ref), channel_id=1, source_target_pairs={{0,1},{1,0},{2,3},{3,2},{4,5},{5,4},{6,7},{7,6},{8,9},{9,8},{10,11... | collective-permute-start | bytes 79880 | tf_op jit(solution)/shard_map/ppermute | solution.py:487
  43.5 4.1 %collective-permute-start.18 = (f32[96,128]{1,0:T(8,128)S(1)}, f32[96,128]{1,0:T(8,128)S(1)}, u32[]{:S(2)}, u32[]{:S(2)}) collective-permute-start(f32[96,128]{1,0:T(8,128)S(1)} %get-tuple-element.115), channel_id=1, source_target_pairs={{0,4},{1,5},{2,6},{3,7},{4,0},{5,1},{6,2},{7,3},{8,12},{9,13},{10,... | collective-permute-start | bytes 147464 | tf_op jit(solution)/shard_map/ppermute | solution.py:488
  45.1 2.5 %collective-permute-start.19 = (f32[96,128]{1,0:T(8,128)S(1)}, f32[96,128]{1,0:T(8,128)S(1)}, u32[]{:S(2)}, u32[]{:S(2)}) collective-permute-start(f32[96,128]{1,0:T(8,128)S(1)} %get-tuple-element.116), channel_id=1, source_target_pairs={{0,1},{1,0},{2,3},{3,2},{4,8},{5,9},{6,10},{7,11},{8,4},{9,5},{10,... | collective-permute-start | bytes 147464 | tf_op jit(solution)/shard_map/ppermute | solution.py:489
  45.2 3.3 %collective-permute-start.17 = (f32[52,128]{1,0:T(8,128)S(1)}, f32[52,128]{1,0:T(8,128)S(1)}, u32[]{:S(2)}, u32[]{:S(2)}) collective-permute-start(f32[52,128]{1,0:T(8,128)S(1)} %add.28.own), channel_id=1, source_target_pairs={{0,3},{1,2},{2,1},{3,0},{4,7},{5,6},{6,5},{7,4},{8,11},{9,10},{10,... | collective-permute-start | bytes 79880 | tf_op jit(solution)/shard_map/ppermute | solution.py:491
  50.5 3.5 %collective-permute-start.20 = (f32[52,128]{1,0:T(8,128)S(1)}, f32[52,128]{1,0:T(8,128)S(1)}, u32[]{:S(2)}, u32[]{:S(2)}) collective-permute-start(f32[52,128]{1,0:T(8,128)S(1)} %get-tuple-element.121.own_ref), channel_id=1, source_target_pairs={{0,1},{1,0},{2,3},{3,2},{4,5},{5,4},{6,7},{7,6},{8,9},{9,8},{10,11... | collective-permute-start | bytes 79880 | tf_op jit(solution)/shard_map/ppermute | solution.py:487
  50.9 5.3 %collective-permute-start.22 = (f32[96,128]{1,0:T(8,128)S(1)}, f32[96,128]{1,0:T(8,128)S(1)}, u32[]{:S(2)}, u32[]{:S(2)}) collective-permute-start(f32[96,128]{1,0:T(8,128)S(1)} %get-tuple-element.122), channel_id=1, source_target_pairs={{0,4},{1,5},{2,6},{3,7},{4,0},{5,1},{6,2},{7,3},{8,12},{9,13},{10,... | collective-permute-start | bytes 147464 | tf_op jit(solution)/shard_map/ppermute | solution.py:488
  53.9 2.3 %collective-permute-start.23 = (f32[96,128]{1,0:T(8,128)S(1)}, f32[96,128]{1,0:T(8,128)S(1)}, u32[]{:S(2)}, u32[]{:S(2)}) collective-permute-start(f32[96,128]{1,0:T(8,128)S(1)} %get-tuple-element.123), channel_id=1, source_target_pairs={{0,1},{1,0},{2,3},{3,2},{4,8},{5,9},{6,10},{7,11},{8,4},{9,5},{10,... | collective-permute-start | bytes 147464 | tf_op jit(solution)/shard_map/ppermute | solution.py:489
  54.0 3.4 %collective-permute-start.21 = (f32[52,128]{1,0:T(8,128)S(1)}, f32[52,128]{1,0:T(8,128)S(1)}, u32[]{:S(2)}, u32[]{:S(2)}) collective-permute-start(f32[52,128]{1,0:T(8,128)S(1)} %add.29.own), channel_id=1, source_target_pairs={{0,3},{1,2},{2,1},{3,0},{4,7},{5,6},{6,5},{7,4},{8,11},{9,10},{10,... | collective-permute-start | bytes 79880 | tf_op jit(solution)/shard_map/ppermute | solution.py:491
  59.3 2.3 %collective-permute-start.24 = (f32[52,128]{1,0:T(8,128)S(1)}, f32[52,128]{1,0:T(8,128)S(1)}, u32[]{:S(2)}, u32[]{:S(2)}) collective-permute-start(f32[52,128]{1,0:T(8,128)S(1)} %get-tuple-element.128.own_ref), channel_id=1, source_target_pairs={{0,1},{1,0},{2,3},{3,2},{4,5},{5,4},{6,7},{7,6},{8,9},{9,8},{10,11... | collective-permute-start | bytes 79880 | tf_op jit(solution)/shard_map/ppermute | solution.py:487
  59.7 4.1 %collective-permute-start.26 = (f32[96,128]{1,0:T(8,128)S(1)}, f32[96,128]{1,0:T(8,128)S(1)}, u32[]{:S(2)}, u32[]{:S(2)}) collective-permute-start(f32[96,128]{1,0:T(8,128)S(1)} %get-tuple-element.129), channel_id=1, source_target_pairs={{0,4},{1,5},{2,6},{3,7},{4,0},{5,1},{6,2},{7,3},{8,12},{9,13},{10,... | collective-permute-start | bytes 147464 | tf_op jit(solution)/shard_map/ppermute | solution.py:488
  61.4 2.4 %collective-permute-start.27 = (f32[96,128]{1,0:T(8,128)S(1)}, f32[96,128]{1,0:T(8,128)S(1)}, u32[]{:S(2)}, u32[]{:S(2)}) collective-permute-start(f32[96,128]{1,0:T(8,128)S(1)} %get-tuple-element.130), channel_id=1, source_target_pairs={{0,1},{1,0},{2,3},{3,2},{4,8},{5,9},{6,10},{7,11},{8,4},{9,5},{10,... | collective-permute-start | bytes 147464 | tf_op jit(solution)/shard_map/ppermute | solution.py:489
  61.5 3.3 %collective-permute-start.25 = (f32[52,128]{1,0:T(8,128)S(1)}, f32[52,128]{1,0:T(8,128)S(1)}, u32[]{:S(2)}, u32[]{:S(2)}) collective-permute-start(f32[52,128]{1,0:T(8,128)S(1)} %add.30.own), channel_id=1, source_target_pairs={{0,3},{1,2},{2,1},{3,0},{4,7},{5,6},{6,5},{7,4},{8,11},{9,10},{10,... | collective-permute-start | bytes 79880 | tf_op jit(solution)/shard_map/ppermute | solution.py:491
  66.8 3.5 %collective-permute-start.28 = (f32[52,128]{1,0:T(8,128)S(1)}, f32[52,128]{1,0:T(8,128)S(1)}, u32[]{:S(2)}, u32[]{:S(2)}) collective-permute-start(f32[52,128]{1,0:T(8,128)S(1)} %get-tuple-element.135.own_ref), channel_id=1, source_target_pairs={{0,1},{1,0},{2,3},{3,2},{4,5},{5,4},{6,7},{7,6},{8,9},{9,8},{10,11... | collective-permute-start | bytes 79880 | tf_op jit(solution)/shard_map/ppermute | solution.py:487
  67.2 5.3 %collective-permute-start.30 = (f32[96,128]{1,0:T(8,128)S(1)}, f32[96,128]{1,0:T(8,128)S(1)}, u32[]{:S(2)}, u32[]{:S(2)}) collective-permute-start(f32[96,128]{1,0:T(8,128)S(1)} %get-tuple-element.136), channel_id=1, source_target_pairs={{0,4},{1,5},{2,6},{3,7},{4,0},{5,1},{6,2},{7,3},{8,12},{9,13},{10,... | collective-permute-start | bytes 147464 | tf_op jit(solution)/shard_map/ppermute | solution.py:488
  70.1 2.3 %collective-permute-start.31 = (f32[96,128]{1,0:T(8,128)S(1)}, f32[96,128]{1,0:T(8,128)S(1)}, u32[]{:S(2)}, u32[]{:S(2)}) collective-permute-start(f32[96,128]{1,0:T(8,128)S(1)} %get-tuple-element.137), channel_id=1, source_target_pairs={{0,1},{1,0},{2,3},{3,2},{4,8},{5,9},{6,10},{7,11},{8,4},{9,5},{10,... | collective-permute-start | bytes 147464 | tf_op jit(solution)/shard_map/ppermute | solution.py:489
  70.3 3.3 %collective-permute-start.29 = (f32[52,128]{1,0:T(8,128)S(1)}, f32[52,128]{1,0:T(8,128)S(1)}, u32[]{:S(2)}, u32[]{:S(2)}) collective-permute-start(f32[52,128]{1,0:T(8,128)S(1)} %add.31.own), channel_id=1, source_target_pairs={{0,3},{1,2},{2,1},{3,0},{4,7},{5,6},{6,5},{7,4},{8,11},{9,10},{10,... | collective-permute-start | bytes 79880 | tf_op jit(solution)/shard_map/ppermute | solution.py:491

commit v4 on v3

--- a/solution.py
+++ b/solution.py
@@ -97,7 +97,7 @@
     block_row, well_row, owner_row, rhs_well, inv_well, row_raw, col_raw, held, sems, small_sems,
 ):
     rows, cols = jac_in.shape[3], jac_in.shape[4]
-    early = rows // 4 + 2
+    early = rows // 4 + 3
     pairs = [
         (block_in, block_row), (well_in, well_row), (owner_in, owner_row),
         (rhs_well_in, rhs_well), (inv_well_in, inv_well),
@@ -148,10 +148,10 @@
         m1_ref[at : at + WELL_UNK, :] = value[0:WELL_UNK]
         at = base + 2 * unk + h * WELL_UNK * WELL_UNK
         m1_ref[at : at + WELL_UNK * WELL_UNK, :] = value[WELL_UNK : 5 * WELL_UNK]
-    copies[0].wait()
+    for copy in copies[0:6]:
+        copy.wait()
     for u in range(WELL_UNK):
         expanded(eye, wcoef, u, own_half, wc_ref)
-    copies[1].wait()
 
     def write(row, value):
         m1_ref[base + row : base + row + 1, :] = value
@@ -159,8 +159,6 @@
     for r in range(PHASES):
         picked_rows(r, x_ref, pick_ref, xs_ref, g_ref)
     well_partials(pick_ref, well_ref, wc_ref, g_ref, write)
-    for copy in copies[2:6]:
-        copy.wait()
     row_ref[...] = row_raw[...].astype(F32)
     for r in range(PHASES):
         for t in range(PHASES):
@@ -179,7 +177,7 @@
 
 def inner_kernel(widen, x_ref, jac_in, rhs_ref, *rest):
     rows, cols = jac_in.shape[3], jac_in.shape[4]
-    early = rows // 4 + 2
+    early = rows // 4 + 3
     z_ref = rest[0]
     if widen:
         ccoef_in, diag_in, half_ref, z_ref, wide_ref, jac_ref, cc_ref, inv_ref, ccoef, sems = rest[1:]

time: 76.4 us -> 76.2 us (level)
  no operation moved by 1% of the time
where the time goes in v4:
time: 76.2 us; the launch traced here: 76 us
  Pallas kernels  35 us (46%)
  starting transfers between devices  29.6 us (39%)
  waiting for transfers between devices  10.4 us (14%)
  between operations  0.9 us (1%)
    ppermute x8, starting transfers between devices, body(): g3 = lax.ppermute(m3, both, gx_swap(gx, gy, 0))  19.1 us
    pallas_call x7, Pallas kernels, body(): z = inner(x, jac, rhs)  10.4 us
    pallas_call x7, Pallas kernels, body(): pl.pallas_call(functools.partial(update_kernel, False), out_shape=(shape(...  9.1 us
    ppermute x8, waiting for transfers between devices, body(): g2 = lax.ppermute(own, 'gy', gy_swap(gy, 1))  8.02 us
    ppermute x8, starting transfers between devices, body(): g2 = lax.ppermute(own, 'gy', gy_swap(gy, 1))  6.05 us
    pallas_call x1, Pallas kernels, body(): first(flags, *[in_hbm(v) for v in (x, jacobian, rhs, well_coupling, perf_...  4.83 us
    pallas_call x7, Pallas kernels, body(): pl.pallas_call(wells_kernel, out_shape=(shape(full, LANES), shape(*m4.sha...  4.3 us
    pallas_call x1, Pallas kernels, inner_first(): pl.pallas_call(functools.partial(inner_kernel, True), out_shape=(grid, sh...  3.7 us
  transfers between devices with their start and end apart: 32, of which 15 were waited for; matrix products, arithmetic and copies ran while one was open for 0% of the time, Pallas kernels for 19%

profile of v4, /device:TPU:0, one launch (start us, length us, event | category | flops | bytes accessed | tf_op | source)
XLA Modules:
  0.0 76.0 jit_solution(5081510426906220728)
XLA Ops:
  0.7 4.8 %first.1 = (f32[3,512,128]{2,1,0:T(8,128)S(1)}, bf16[7,3,3,16,32,128]{5,4,3,2,1,0:T(8,128)(2,1)S(1)}, f32[3,512,128]{2,1,0:T(8,128)S(1)}, f32[2,3,3,32,128]{4,3,...) custom-call(s32[5]{0:T(128)S(1)} %stack.31.flags, ...), custom_call_target="tpu_custom_call" | custom-call | tf_op jit(solution)/shard_map/first/pallas_call | solution.py:429
  7.0 2.6 %collective-permute-start.1 = (f32[72,128]{1,0:T(8,128)S(1)}, f32[72,128]{1,0:T(8,128)S(1)}, u32[]{:S(2)}, u32[]{:S(2)}) collective-permute-start(f32[72,128]{1,0:T(8,128)S(1)} %add.24), channel_id=1, source_target_pairs={{0,3},{1,2},{2,1},{3,0},{4,7},{5,6},{6,5},{7,4},{8,11},{9,10},{10,... | collective-permute-start | bytes 110600 | tf_op jit(solution)/shard_map/ppermute | solution.py:489
  9.6 1.5 %collective-permute-start.2 = (f32[96,128]{1,0:T(8,128)S(1)}, f32[96,128]{1,0:T(8,128)S(1)}, u32[]{:S(2)}, u32[]{:S(2)}) collective-permute-start(f32[96,128]{1,0:T(8,128)S(1)} %get-tuple-element.78), channel_id=1, source_target_pairs={{0,4},{1,5},{2,6},{3,7},{4,0},{5,1},{6,2},{7,3},{8,12},{9,13},{10,... | collective-permute-start | bytes 147464 | tf_op jit(solution)/shard_map/ppermute | solution.py:486
  11.2 3.7 %inner_widen.1 = (f32[3,512,128]{2,1,0:T(8,128)S(1)}, f32[7,3,3,16,32,128]{5,4,3,2,1,0:T(8,128)S(1)}, bf16[7,3,3,16,32,128]{5,4,3,2,1,0:T(8,128)(2,1)S(1)}, bf16...) custom-call(f32[3,512,128]{2,1,0:T(8,128)S(1)} %get-tuple-element.71.x_ref, ...), custom_call_target="tpu_custom_call", output_to_operand_aliasing={{2}: (3, {})} | custom-call | tf_op jit(solution)/shard_map/inner_widen/pallas_call | solution.py:452
  14.9 1.3 %update.7 = (f32[3,512,128]{2,1,0:T(8,128)S(1)}, f32[48,128]{1,0:T(8,128)S(1)}, f32[48,128]{1,0:T(8,128)S(1)}, f32[96,128]{1,0:T(8,128)S(1)}, f32[96,128]{1,0:T(8,128)S(1)}) custom-call(s32[5]{0:T(128)S(1)} %stack.31.flags, f32[3,512,128]{2,1,0:T(8,128)S(1)} %get-tuple-element.75.z_ref, f32[52,128]{1,0:T(8,128)S(1)} %slice.20.own, f32[52,128]{1,0:T(8,128)S(1)} %slice.21.g1, ...), custom_call_target="tpu_custom_call" | custom-call | tf_op jit(solution)/shard_map/update/pallas_call | solution.py:519
  17.4 2.6 %collective-permute-start.6 = (f32[96,128]{1,0:T(8,128)S(1)}, f32[96,128]{1,0:T(8,128)S(1)}, u32[]{:S(2)}, u32[]{:S(2)}) collective-permute-start(f32[96,128]{1,0:T(8,128)S(1)} %get-tuple-element.94), channel_id=1, source_target_pairs={{0,4},{1,5},{2,6},{3,7},{4,0},{5,1},{6,2},{7,3},{8,12},{9,13},{10,... | collective-permute-start | bytes 147464 | tf_op jit(solution)/shard_map/ppermute | solution.py:486
  20.6 1.5 %inner.7.z_ref = f32[3,512,128]{2,1,0:T(8,128)S(1)} custom-call(f32[3,512,128]{2,1,0:T(8,128)S(1)} %get-tuple-element.86.x_ref, f32[7,3,3,16,32,128]{5,4,3,2,1,0:T(8,128)S(1)} %get-tuple-element.87.jac_in, f32[3,512,128]{2,1,0:T(8,128)S(1)} %get-tuple-element.72.rhs_ref), custom_call_target="tpu_custom_call" | custom-call | tf_op jit(solution)/shard_map/inner/pallas_call | solution.py:502
  22.3 1.2 %collective-permute-done.5.g2 = f32[52,128]{1,0:T(8,128)S(1)} collective-permute-done((f32[52,128]{1,0:T(8,128)S(1)}, f32[52,128]{1,0:T(8,128)S(1)}, u32[]{:S(2)}, u32[]{:S(2)}) %collective-permute-start.5) | collective-permute-done | bytes 26656 | tf_op jit(solution)/shard_map/ppermute | solution.py:489
  23.5 1.3 %update.8 = (f32[3,512,128]{2,1,0:T(8,128)S(1)}, f32[48,128]{1,0:T(8,128)S(1)}, f32[48,128]{1,0:T(8,128)S(1)}, f32[96,128]{1,0:T(8,128)S(1)}, f32[96,128]{1,0:T(8,128)S(1)}) custom-call(s32[5]{0:T(128)S(1)} %stack.31.flags, f32[3,512,128]{2,1,0:T(8,128)S(1)} %inner.7.z_ref, f32[52,128]{1,0:T(8,128)S(1)} %add.25.own, ...), custom_call_target="tpu_custom_call" | custom-call | tf_op jit(solution)/shard_map/update/pallas_call | solution.py:519
  25.8 2.9 %collective-permute-start.10 = (f32[96,128]{1,0:T(8,128)S(1)}, f32[96,128]{1,0:T(8,128)S(1)}, u32[]{:S(2)}, u32[]{:S(2)}) collective-permute-start(f32[96,128]{1,0:T(8,128)S(1)} %get-tuple-element.101), channel_id=1, source_target_pairs={{0,4},{1,5},{2,6},{3,7},{4,0},{5,1},{6,2},{7,3},{8,12},{9,13},{10,... | collective-permute-start | bytes 147464 | tf_op jit(solution)/shard_map/ppermute | solution.py:486
  29.3 1.5 %inner.8.z_ref = f32[3,512,128]{2,1,0:T(8,128)S(1)} custom-call(f32[3,512,128]{2,1,0:T(8,128)S(1)} %get-tuple-element.96.x_ref, f32[7,3,3,16,32,128]{5,4,3,2,1,0:T(8,128)S(1)} %get-tuple-element.87.jac_in, f32[3,512,128]{2,1,0:T(8,128)S(1)} %get-tuple-element.72.rhs_ref), custom_call_target="tpu_custom_call" | custom-call | tf_op jit(solution)/shard_map/inner/pallas_call | solution.py:502
  31.0 1.2 %collective-permute-done.9.g2 = f32[52,128]{1,0:T(8,128)S(1)} collective-permute-done((f32[52,128]{1,0:T(8,128)S(1)}, f32[52,128]{1,0:T(8,128)S(1)}, u32[]{:S(2)}, u32[]{:S(2)}) %collective-permute-start.9) | collective-permute-done | bytes 26656 | tf_op jit(solution)/shard_map/ppermute | solution.py:489
  32.2 1.3 %update.9 = (f32[3,512,128]{2,1,0:T(8,128)S(1)}, f32[48,128]{1,0:T(8,128)S(1)}, f32[48,128]{1,0:T(8,128)S(1)}, f32[96,128]{1,0:T(8,128)S(1)}, f32[96,128]{1,0:T(8,128)S(1)}) custom-call(s32[5]{0:T(128)S(1)} %stack.31.flags, f32[3,512,128]{2,1,0:T(8,128)S(1)} %inner.8.z_ref, f32[52,128]{1,0:T(8,128)S(1)} %add.26.own, ...), custom_call_target="tpu_custom_call" | custom-call | tf_op jit(solution)/shard_map/update/pallas_call | solution.py:519
  34.5 2.9 %collective-permute-start.14 = (f32[96,128]{1,0:T(8,128)S(1)}, f32[96,128]{1,0:T(8,128)S(1)}, u32[]{:S(2)}, u32[]{:S(2)}) collective-permute-start(f32[96,128]{1,0:T(8,128)S(1)} %get-tuple-element.108), channel_id=1, source_target_pairs={{0,4},{1,5},{2,6},{3,7},{4,0},{5,1},{6,2},{7,3},{8,12},{9,13},{10,... | collective-permute-start | bytes 147464 | tf_op jit(solution)/shard_map/ppermute | solution.py:486
  38.1 1.5 %inner.9.z_ref = f32[3,512,128]{2,1,0:T(8,128)S(1)} custom-call(f32[3,512,128]{2,1,0:T(8,128)S(1)} %get-tuple-element.103.x_ref, f32[7,3,3,16,32,128]{5,4,3,2,1,0:T(8,128)S(1)} %get-tuple-element.87.jac_in, f32[3,512,128]{2,1,0:T(8,128)S(1)} %get-tuple-element.72.rhs_ref), custom_call_target="tpu_custom_call" | custom-call | tf_op jit(solution)/shard_map/inner/pallas_call | solution.py:502
  39.7 1.2 %collective-permute-done.13.g2 = f32[52,128]{1,0:T(8,128)S(1)} collective-permute-done((f32[52,128]{1,0:T(8,128)S(1)}, f32[52,128]{1,0:T(8,128)S(1)}, u32[]{:S(2)}, u32[]{:S(2)}) %collective-permute-start.13) | collective-permute-done | bytes 26656 | tf_op jit(solution)/shard_map/ppermute | solution.py:489
  40.9 1.3 %update.10 = (f32[3,512,128]{2,1,0:T(8,128)S(1)}, f32[48,128]{1,0:T(8,128)S(1)}, f32[48,128]{1,0:T(8,128)S(1)}, f32[96,128]{1,0:T(8,128)S(1)}, f32[96,128]{1,0:T(8,128)S(1)}) custom-call(s32[5]{0:T(128)S(1)} %stack.31.flags, f32[3,512,128]{2,1,0:T(8,128)S(1)} %inner.9.z_ref, f32[52,128]{1,0:T(8,128)S(1)} %add.27.own, ...), custom_call_target="tpu_custom_call" | custom-call | tf_op jit(solution)/shard_map/update/pallas_call | solution.py:519
  43.2 1.6 %collective-permute-start.18 = (f32[96,128]{1,0:T(8,128)S(1)}, f32[96,128]{1,0:T(8,128)S(1)}, u32[]{:S(2)}, u32[]{:S(2)}) collective-permute-start(f32[96,128]{1,0:T(8,128)S(1)} %get-tuple-element.115), channel_id=1, source_target_pairs={{0,4},{1,5},{2,6},{3,7},{4,0},{5,1},{6,2},{7,3},{8,12},{9,13},{10,... | collective-permute-start | bytes 147464 | tf_op jit(solution)/shard_map/ppermute | solution.py:486
  45.5 1.5 %inner.10.z_ref = f32[3,512,128]{2,1,0:T(8,128)S(1)} custom-call(f32[3,512,128]{2,1,0:T(8,128)S(1)} %get-tuple-element.110.x_ref, f32[7,3,3,16,32,128]{5,4,3,2,1,0:T(8,128)S(1)} %get-tuple-element.87.jac_in, f32[3,512,128]{2,1,0:T(8,128)S(1)} %get-tuple-element.72.rhs_ref), custom_call_target="tpu_custom_call" | custom-call | tf_op jit(solution)/shard_map/inner/pallas_call | solution.py:502
  48.3 1.3 %update.11 = (f32[3,512,128]{2,1,0:T(8,128)S(1)}, f32[48,128]{1,0:T(8,128)S(1)}, f32[48,128]{1,0:T(8,128)S(1)}, f32[96,128]{1,0:T(8,128)S(1)}, f32[96,128]{1,0:T(8,128)S(1)}) custom-call(s32[5]{0:T(128)S(1)} %stack.31.flags, f32[3,512,128]{2,1,0:T(8,128)S(1)} %inner.10.z_ref, f32[52,128]{1,0:T(8,128)S(1)} %add.28.own, ...), custom_call_target="tpu_custom_call" | custom-call | tf_op jit(solution)/shard_map/update/pallas_call | solution.py:519
  50.7 2.9 %collective-permute-start.22 = (f32[96,128]{1,0:T(8,128)S(1)}, f32[96,128]{1,0:T(8,128)S(1)}, u32[]{:S(2)}, u32[]{:S(2)}) collective-permute-start(f32[96,128]{1,0:T(8,128)S(1)} %get-tuple-element.122), channel_id=1, source_target_pairs={{0,4},{1,5},{2,6},{3,7},{4,0},{5,1},{6,2},{7,3},{8,12},{9,13},{10,... | collective-permute-start | bytes 147464 | tf_op jit(solution)/shard_map/ppermute | solution.py:486
  54.3 1.5 %inner.11.z_ref = f32[3,512,128]{2,1,0:T(8,128)S(1)} custom-call(f32[3,512,128]{2,1,0:T(8,128)S(1)} %get-tuple-element.117.x_ref, f32[7,3,3,16,32,128]{5,4,3,2,1,0:T(8,128)S(1)} %get-tuple-element.87.jac_in, f32[3,512,128]{2,1,0:T(8,128)S(1)} %get-tuple-element.72.rhs_ref), custom_call_target="tpu_custom_call" | custom-call | tf_op jit(solution)/shard_map/inner/pallas_call | solution.py:502
  55.9 1.2 %collective-permute-done.21.g2 = f32[52,128]{1,0:T(8,128)S(1)} collective-permute-done((f32[52,128]{1,0:T(8,128)S(1)}, f32[52,128]{1,0:T(8,128)S(1)}, u32[]{:S(2)}, u32[]{:S(2)}) %collective-permute-start.21) | collective-permute-done | bytes 26656 | tf_op jit(solution)/shard_map/ppermute | solution.py:489
  57.1 1.3 %update.12 = (f32[3,512,128]{2,1,0:T(8,128)S(1)}, f32[48,128]{1,0:T(8,128)S(1)}, f32[48,128]{1,0:T(8,128)S(1)}, f32[96,128]{1,0:T(8,128)S(1)}, f32[96,128]{1,0:T(8,128)S(1)}) custom-call(s32[5]{0:T(128)S(1)} %stack.31.flags, f32[3,512,128]{2,1,0:T(8,128)S(1)} %inner.11.z_ref, f32[52,128]{1,0:T(8,128)S(1)} %add.29.own, ...), custom_call_target="tpu_custom_call" | custom-call | tf_op jit(solution)/shard_map/update/pallas_call | solution.py:519
  59.4 1.8 %collective-permute-start.26 = (f32[96,128]{1,0:T(8,128)S(1)}, f32[96,128]{1,0:T(8,128)S(1)}, u32[]{:S(2)}, u32[]{:S(2)}) collective-permute-start(f32[96,128]{1,0:T(8,128)S(1)} %get-tuple-element.129), channel_id=1, source_target_pairs={{0,4},{1,5},{2,6},{3,7},{4,0},{5,1},{6,2},{7,3},{8,12},{9,13},{10,... | collective-permute-start | bytes 147464 | tf_op jit(solution)/shard_map/ppermute | solution.py:486
  61.7 1.5 %inner.12.z_ref = f32[3,512,128]{2,1,0:T(8,128)S(1)} custom-call(f32[3,512,128]{2,1,0:T(8,128)S(1)} %get-tuple-element.124.x_ref, f32[7,3,3,16,32,128]{5,4,3,2,1,0:T(8,128)S(1)} %get-tuple-element.87.jac_in, f32[3,512,128]{2,1,0:T(8,128)S(1)} %get-tuple-element.72.rhs_ref), custom_call_target="tpu_custom_call" | custom-call | tf_op jit(solution)/shard_map/inner/pallas_call | solution.py:502
  63.5 1.2 %collective-permute-done.25.g2 = f32[52,128]{1,0:T(8,128)S(1)} collective-permute-done((f32[52,128]{1,0:T(8,128)S(1)}, f32[52,128]{1,0:T(8,128)S(1)}, u32[]{:S(2)}, u32[]{:S(2)}) %collective-permute-start.25) | collective-permute-done | bytes 26656 | tf_op jit(solution)/shard_map/ppermute | solution.py:489
  64.7 1.3 %update.13 = (f32[3,512,128]{2,1,0:T(8,128)S(1)}, f32[48,128]{1,0:T(8,128)S(1)}, f32[48,128]{1,0:T(8,128)S(1)}, f32[96,128]{1,0:T(8,128)S(1)}, f32[96,128]{1,0:T(8,128)S(1)}) custom-call(s32[5]{0:T(128)S(1)} %stack.31.flags, f32[3,512,128]{2,1,0:T(8,128)S(1)} %inner.12.z_ref, f32[52,128]{1,0:T(8,128)S(1)} %add.30.own, ...), custom_call_target="tpu_custom_call" | custom-call | tf_op jit(solution)/shard_map/update/pallas_call | solution.py:519
  67.0 2.9 %collective-permute-start.30 = (f32[96,128]{1,0:T(8,128)S(1)}, f32[96,128]{1,0:T(8,128)S(1)}, u32[]{:S(2)}, u32[]{:S(2)}) collective-permute-start(f32[96,128]{1,0:T(8,128)S(1)} %get-tuple-element.136), channel_id=1, source_target_pairs={{0,4},{1,5},{2,6},{3,7},{4,0},{5,1},{6,2},{7,3},{8,12},{9,13},{10,... | collective-permute-start | bytes 147464 | tf_op jit(solution)/shard_map/ppermute | solution.py:486
  70.6 1.5 %inner.13.z_ref = f32[3,512,128]{2,1,0:T(8,128)S(1)} custom-call(f32[3,512,128]{2,1,0:T(8,128)S(1)} %get-tuple-element.131.x_ref, f32[7,3,3,16,32,128]{5,4,3,2,1,0:T(8,128)S(1)} %get-tuple-element.87.jac_in, f32[3,512,128]{2,1,0:T(8,128)S(1)} %get-tuple-element.72.rhs_ref), custom_call_target="tpu_custom_call" | custom-call | tf_op jit(solution)/shard_map/inner/pallas_call | solution.py:502
  72.2 1.2 %collective-permute-done.29.g2 = f32[52,128]{1,0:T(8,128)S(1)} collective-permute-done((f32[52,128]{1,0:T(8,128)S(1)}, f32[52,128]{1,0:T(8,128)S(1)}, u32[]{:S(2)}, u32[]{:S(2)}) %collective-permute-start.29) | collective-permute-done | bytes 26656 | tf_op jit(solution)/shard_map/ppermute | solution.py:489
  73.4 2.6 %update_last.1 = (f32[3,512,128]{2,1,0:T(8,128)}, f32[4,32]{1,0:T(4,128)}) custom-call(s32[5]{0:T(128)S(1)} %stack.31.flags, f32[3,512,128]{2,1,0:T(8,128)S(1)} %inner.13.z_ref, f32[52,128]{1,0:T(8,128)S(1)} %add.31.own, f32[52,128]{1,0:T(8,128)S(1)} %collective-permute-done.28.got_ref.g1, f32[52,128]{1,0:T(8,128)S(1)} %collective-permute-done.29.g2, ...), custom_call_target="tpu_custom_call" | custom-call | tf_op jit(solution)/shard_map/update_last/pallas_call | solution.py:505
  (69 shorter events, 15.6 us)
Async XLA Ops:
  5.6 1.4 %collective-permute-start = (f32[72,128]{1,0:T(8,128)S(1)}, f32[72,128]{1,0:T(8,128)S(1)}, u32[]{:S(2)}, u32[]{:S(2)}) collective-permute-start(f32[72,128]{1,0:T(8,128)S(1)} %get-tuple-element.77.own_ref), channel_id=1, source_target_pairs={{0,1},{1,0},{2,3},{3,2},{4,5},{5,4},{6,7},{7,6},{8,9},{9,8},{10,11... | collective-permute-start | bytes 110600 | tf_op jit(solution)/shard_map/ppermute | solution.py:485
  7.0 7.9 %collective-permute-start.1 = (f32[72,128]{1,0:T(8,128)S(1)}, f32[72,128]{1,0:T(8,128)S(1)}, u32[]{:S(2)}, u32[]{:S(2)}) collective-permute-start(f32[72,128]{1,0:T(8,128)S(1)} %add.24), channel_id=1, source_target_pairs={{0,3},{1,2},{2,1},{3,0},{4,7},{5,6},{6,5},{7,4},{8,11},{9,10},{10,... | collective-permute-start | bytes 110600 | tf_op jit(solution)/shard_map/ppermute | solution.py:489
  9.6 5.3 %collective-permute-start.2 = (f32[96,128]{1,0:T(8,128)S(1)}, f32[96,128]{1,0:T(8,128)S(1)}, u32[]{:S(2)}, u32[]{:S(2)}) collective-permute-start(f32[96,128]{1,0:T(8,128)S(1)} %get-tuple-element.78), channel_id=1, source_target_pairs={{0,4},{1,5},{2,6},{3,7},{4,0},{5,1},{6,2},{7,3},{8,12},{9,13},{10,... | collective-permute-start | bytes 147464 | tf_op jit(solution)/shard_map/ppermute | solution.py:486
  11.1 3.8 %collective-permute-start.3 = (f32[96,128]{1,0:T(8,128)S(1)}, f32[96,128]{1,0:T(8,128)S(1)}, u32[]{:S(2)}, u32[]{:S(2)}) collective-permute-start(f32[96,128]{1,0:T(8,128)S(1)} %get-tuple-element.79), channel_id=1, source_target_pairs={{0,1},{1,0},{2,3},{3,2},{4,8},{5,9},{6,10},{7,11},{8,4},{9,5},{10,... | collective-permute-start | bytes 147464 | tf_op jit(solution)/shard_map/ppermute | solution.py:487
  16.9 3.3 %collective-permute-start.4 = (f32[52,128]{1,0:T(8,128)S(1)}, f32[52,128]{1,0:T(8,128)S(1)}, u32[]{:S(2)}, u32[]{:S(2)}) collective-permute-start(f32[52,128]{1,0:T(8,128)S(1)} %get-tuple-element.93.own_ref), channel_id=1, source_target_pairs={{0,1},{1,0},{2,3},{3,2},{4,5},{5,4},{6,7},{7,6},{8,9},{9,8},{10,11... | collective-permute-start | bytes 79880 | tf_op jit(solution)/shard_map/ppermute | solution.py:485
  17.4 4.9 %collective-permute-start.6 = (f32[96,128]{1,0:T(8,128)S(1)}, f32[96,128]{1,0:T(8,128)S(1)}, u32[]{:S(2)}, u32[]{:S(2)}) collective-permute-start(f32[96,128]{1,0:T(8,128)S(1)} %get-tuple-element.94), channel_id=1, source_target_pairs={{0,4},{1,5},{2,6},{3,7},{4,0},{5,1},{6,2},{7,3},{8,12},{9,13},{10,... | collective-permute-start | bytes 147464 | tf_op jit(solution)/shard_map/ppermute | solution.py:486
  20.0 2.3 %collective-permute-start.7 = (f32[96,128]{1,0:T(8,128)S(1)}, f32[96,128]{1,0:T(8,128)S(1)}, u32[]{:S(2)}, u32[]{:S(2)}) collective-permute-start(f32[96,128]{1,0:T(8,128)S(1)} %get-tuple-element.95), channel_id=1, source_target_pairs={{0,1},{1,0},{2,3},{3,2},{4,8},{5,9},{6,10},{7,11},{8,4},{9,5},{10,... | collective-permute-start | bytes 147464 | tf_op jit(solution)/shard_map/ppermute | solution.py:487
  20.2 3.3 %collective-permute-start.5 = (f32[52,128]{1,0:T(8,128)S(1)}, f32[52,128]{1,0:T(8,128)S(1)}, u32[]{:S(2)}, u32[]{:S(2)}) collective-permute-start(f32[52,128]{1,0:T(8,128)S(1)} %add.25.own), channel_id=1, source_target_pairs={{0,3},{1,2},{2,1},{3,0},{4,7},{5,6},{6,5},{7,4},{8,11},{9,10},{10,... | collective-permute-start | bytes 79880 | tf_op jit(solution)/shard_map/ppermute | solution.py:489
  25.4 3.4 %collective-permute-start.8 = (f32[52,128]{1,0:T(8,128)S(1)}, f32[52,128]{1,0:T(8,128)S(1)}, u32[]{:S(2)}, u32[]{:S(2)}) collective-permute-start(f32[52,128]{1,0:T(8,128)S(1)} %get-tuple-element.100.own_ref), channel_id=1, source_target_pairs={{0,1},{1,0},{2,3},{3,2},{4,5},{5,4},{6,7},{7,6},{8,9},{9,8},{10,11... | collective-permute-start | bytes 79880 | tf_op jit(solution)/shard_map/ppermute | solution.py:485
  25.8 5.2 %collective-permute-start.10 = (f32[96,128]{1,0:T(8,128)S(1)}, f32[96,128]{1,0:T(8,128)S(1)}, u32[]{:S(2)}, u32[]{:S(2)}) collective-permute-start(f32[96,128]{1,0:T(8,128)S(1)} %get-tuple-element.101), channel_id=1, source_target_pairs={{0,4},{1,5},{2,6},{3,7},{4,0},{5,1},{6,2},{7,3},{8,12},{9,13},{10,... | collective-permute-start | bytes 147464 | tf_op jit(solution)/shard_map/ppermute | solution.py:486
  28.7 2.3 %collective-permute-start.11 = (f32[96,128]{1,0:T(8,128)S(1)}, f32[96,128]{1,0:T(8,128)S(1)}, u32[]{:S(2)}, u32[]{:S(2)}) collective-permute-start(f32[96,128]{1,0:T(8,128)S(1)} %get-tuple-element.102), channel_id=1, source_target_pairs={{0,1},{1,0},{2,3},{3,2},{4,8},{5,9},{6,10},{7,11},{8,4},{9,5},{10,... | collective-permute-start | bytes 147464 | tf_op jit(solution)/shard_map/ppermute | solution.py:487
  28.8 3.4 %collective-permute-start.9 = (f32[52,128]{1,0:T(8,128)S(1)}, f32[52,128]{1,0:T(8,128)S(1)}, u32[]{:S(2)}, u32[]{:S(2)}) collective-permute-start(f32[52,128]{1,0:T(8,128)S(1)} %add.26.own), channel_id=1, source_target_pairs={{0,3},{1,2},{2,1},{3,0},{4,7},{5,6},{6,5},{7,4},{8,11},{9,10},{10,... | collective-permute-start | bytes 79880 | tf_op jit(solution)/shard_map/ppermute | solution.py:489
  34.1 3.4 %collective-permute-start.12 = (f32[52,128]{1,0:T(8,128)S(1)}, f32[52,128]{1,0:T(8,128)S(1)}, u32[]{:S(2)}, u32[]{:S(2)}) collective-permute-start(f32[52,128]{1,0:T(8,128)S(1)} %get-tuple-element.107.own_ref), channel_id=1, source_target_pairs={{0,1},{1,0},{2,3},{3,2},{4,5},{5,4},{6,7},{7,6},{8,9},{9,8},{10,11... | collective-permute-start | bytes 79880 | tf_op jit(solution)/shard_map/ppermute | solution.py:485
  34.5 5.2 %collective-permute-start.14 = (f32[96,128]{1,0:T(8,128)S(1)}, f32[96,128]{1,0:T(8,128)S(1)}, u32[]{:S(2)}, u32[]{:S(2)}) collective-permute-start(f32[96,128]{1,0:T(8,128)S(1)} %get-tuple-element.108), channel_id=1, source_target_pairs={{0,4},{1,5},{2,6},{3,7},{4,0},{5,1},{6,2},{7,3},{8,12},{9,13},{10,... | collective-permute-start | bytes 147464 | tf_op jit(solution)/shard_map/ppermute | solution.py:486
  37.4 2.3 %collective-permute-start.15 = (f32[96,128]{1,0:T(8,128)S(1)}, f32[96,128]{1,0:T(8,128)S(1)}, u32[]{:S(2)}, u32[]{:S(2)}) collective-permute-start(f32[96,128]{1,0:T(8,128)S(1)} %get-tuple-element.109), channel_id=1, source_target_pairs={{0,1},{1,0},{2,3},{3,2},{4,8},{5,9},{6,10},{7,11},{8,4},{9,5},{10,... | collective-permute-start | bytes 147464 | tf_op jit(solution)/shard_map/ppermute | solution.py:487
  37.5 3.4 %collective-permute-start.13 = (f32[52,128]{1,0:T(8,128)S(1)}, f32[52,128]{1,0:T(8,128)S(1)}, u32[]{:S(2)}, u32[]{:S(2)}) collective-permute-start(f32[52,128]{1,0:T(8,128)S(1)} %add.27.own), channel_id=1, source_target_pairs={{0,3},{1,2},{2,1},{3,0},{4,7},{5,6},{6,5},{7,4},{8,11},{9,10},{10,... | collective-permute-start | bytes 79880 | tf_op jit(solution)/shard_map/ppermute | solution.py:489
  42.8 2.2 %collective-permute-start.16 = (f32[52,128]{1,0:T(8,128)S(1)}, f32[52,128]{1,0:T(8,128)S(1)}, u32[]{:S(2)}, u32[]{:S(2)}) collective-permute-start(f32[52,128]{1,0:T(8,128)S(1)} %get-tuple-element.114.own_ref), channel_id=1, source_target_pairs={{0,1},{1,0},{2,3},{3,2},{4,5},{5,4},{6,7},{7,6},{8,9},{9,8},{10,11... | collective-permute-start | bytes 79880 | tf_op jit(solution)/shard_map/ppermute | solution.py:485
  43.2 4.1 %collective-permute-start.18 = (f32[96,128]{1,0:T(8,128)S(1)}, f32[96,128]{1,0:T(8,128)S(1)}, u32[]{:S(2)}, u32[]{:S(2)}) collective-permute-start(f32[96,128]{1,0:T(8,128)S(1)} %get-tuple-element.115), channel_id=1, source_target_pairs={{0,4},{1,5},{2,6},{3,7},{4,0},{5,1},{6,2},{7,3},{8,12},{9,13},{10,... | collective-permute-start | bytes 147464 | tf_op jit(solution)/shard_map/ppermute | solution.py:486
  44.9 2.5 %collective-permute-start.19 = (f32[96,128]{1,0:T(8,128)S(1)}, f32[96,128]{1,0:T(8,128)S(1)}, u32[]{:S(2)}, u32[]{:S(2)}) collective-permute-start(f32[96,128]{1,0:T(8,128)S(1)} %get-tuple-element.116), channel_id=1, source_target_pairs={{0,1},{1,0},{2,3},{3,2},{4,8},{5,9},{6,10},{7,11},{8,4},{9,5},{10,... | collective-permute-start | bytes 147464 | tf_op jit(solution)/shard_map/ppermute | solution.py:487
  45.0 3.4 %collective-permute-start.17 = (f32[52,128]{1,0:T(8,128)S(1)}, f32[52,128]{1,0:T(8,128)S(1)}, u32[]{:S(2)}, u32[]{:S(2)}) collective-permute-start(f32[52,128]{1,0:T(8,128)S(1)} %add.28.own), channel_id=1, source_target_pairs={{0,3},{1,2},{2,1},{3,0},{4,7},{5,6},{6,5},{7,4},{8,11},{9,10},{10,... | collective-permute-start | bytes 79880 | tf_op jit(solution)/shard_map/ppermute | solution.py:489
  50.3 3.4 %collective-permute-start.20 = (f32[52,128]{1,0:T(8,128)S(1)}, f32[52,128]{1,0:T(8,128)S(1)}, u32[]{:S(2)}, u32[]{:S(2)}) collective-permute-start(f32[52,128]{1,0:T(8,128)S(1)} %get-tuple-element.121.own_ref), channel_id=1, source_target_pairs={{0,1},{1,0},{2,3},{3,2},{4,5},{5,4},{6,7},{7,6},{8,9},{9,8},{10,11... | collective-permute-start | bytes 79880 | tf_op jit(solution)/shard_map/ppermute | solution.py:485
  50.7 5.2 %collective-permute-start.22 = (f32[96,128]{1,0:T(8,128)S(1)}, f32[96,128]{1,0:T(8,128)S(1)}, u32[]{:S(2)}, u32[]{:S(2)}) collective-permute-start(f32[96,128]{1,0:T(8,128)S(1)} %get-tuple-element.122), channel_id=1, source_target_pairs={{0,4},{1,5},{2,6},{3,7},{4,0},{5,1},{6,2},{7,3},{8,12},{9,13},{10,... | collective-permute-start | bytes 147464 | tf_op jit(solution)/shard_map/ppermute | solution.py:486
  53.6 2.3 %collective-permute-start.23 = (f32[96,128]{1,0:T(8,128)S(1)}, f32[96,128]{1,0:T(8,128)S(1)}, u32[]{:S(2)}, u32[]{:S(2)}) collective-permute-start(f32[96,128]{1,0:T(8,128)S(1)} %get-tuple-element.123), channel_id=1, source_target_pairs={{0,1},{1,0},{2,3},{3,2},{4,8},{5,9},{6,10},{7,11},{8,4},{9,5},{10,... | collective-permute-start | bytes 147464 | tf_op jit(solution)/shard_map/ppermute | solution.py:487
  53.7 3.4 %collective-permute-start.21 = (f32[52,128]{1,0:T(8,128)S(1)}, f32[52,128]{1,0:T(8,128)S(1)}, u32[]{:S(2)}, u32[]{:S(2)}) collective-permute-start(f32[52,128]{1,0:T(8,128)S(1)} %add.29.own), channel_id=1, source_target_pairs={{0,3},{1,2},{2,1},{3,0},{4,7},{5,6},{6,5},{7,4},{8,11},{9,10},{10,... | collective-permute-start | bytes 79880 | tf_op jit(solution)/shard_map/ppermute | solution.py:489
  59.0 2.4 %collective-permute-start.24 = (f32[52,128]{1,0:T(8,128)S(1)}, f32[52,128]{1,0:T(8,128)S(1)}, u32[]{:S(2)}, u32[]{:S(2)}) collective-permute-start(f32[52,128]{1,0:T(8,128)S(1)} %get-tuple-element.128.own_ref), channel_id=1, source_target_pairs={{0,1},{1,0},{2,3},{3,2},{4,5},{5,4},{6,7},{7,6},{8,9},{9,8},{10,11... | collective-permute-start | bytes 79880 | tf_op jit(solution)/shard_map/ppermute | solution.py:485
  59.4 4.1 %collective-permute-start.26 = (f32[96,128]{1,0:T(8,128)S(1)}, f32[96,128]{1,0:T(8,128)S(1)}, u32[]{:S(2)}, u32[]{:S(2)}) collective-permute-start(f32[96,128]{1,0:T(8,128)S(1)} %get-tuple-element.129), channel_id=1, source_target_pairs={{0,4},{1,5},{2,6},{3,7},{4,0},{5,1},{6,2},{7,3},{8,12},{9,13},{10,... | collective-permute-start | bytes 147464 | tf_op jit(solution)/shard_map/ppermute | solution.py:486
  61.2 2.3 %collective-permute-start.27 = (f32[96,128]{1,0:T(8,128)S(1)}, f32[96,128]{1,0:T(8,128)S(1)}, u32[]{:S(2)}, u32[]{:S(2)}) collective-permute-start(f32[96,128]{1,0:T(8,128)S(1)} %get-tuple-element.130), channel_id=1, source_target_pairs={{0,1},{1,0},{2,3},{3,2},{4,8},{5,9},{6,10},{7,11},{8,4},{9,5},{10,... | collective-permute-start | bytes 147464 | tf_op jit(solution)/shard_map/ppermute | solution.py:487
  61.4 3.3 %collective-permute-start.25 = (f32[52,128]{1,0:T(8,128)S(1)}, f32[52,128]{1,0:T(8,128)S(1)}, u32[]{:S(2)}, u32[]{:S(2)}) collective-permute-start(f32[52,128]{1,0:T(8,128)S(1)} %add.30.own), channel_id=1, source_target_pairs={{0,3},{1,2},{2,1},{3,0},{4,7},{5,6},{6,5},{7,4},{8,11},{9,10},{10,... | collective-permute-start | bytes 79880 | tf_op jit(solution)/shard_map/ppermute | solution.py:489
  66.6 3.4 %collective-permute-start.28 = (f32[52,128]{1,0:T(8,128)S(1)}, f32[52,128]{1,0:T(8,128)S(1)}, u32[]{:S(2)}, u32[]{:S(2)}) collective-permute-start(f32[52,128]{1,0:T(8,128)S(1)} %get-tuple-element.135.own_ref), channel_id=1, source_target_pairs={{0,1},{1,0},{2,3},{3,2},{4,5},{5,4},{6,7},{7,6},{8,9},{9,8},{10,11... | collective-permute-start | bytes 79880 | tf_op jit(solution)/shard_map/ppermute | solution.py:485
  67.0 5.2 %collective-permute-start.30 = (f32[96,128]{1,0:T(8,128)S(1)}, f32[96,128]{1,0:T(8,128)S(1)}, u32[]{:S(2)}, u32[]{:S(2)}) collective-permute-start(f32[96,128]{1,0:T(8,128)S(1)} %get-tuple-element.136), channel_id=1, source_target_pairs={{0,4},{1,5},{2,6},{3,7},{4,0},{5,1},{6,2},{7,3},{8,12},{9,13},{10,... | collective-permute-start | bytes 147464 | tf_op jit(solution)/shard_map/ppermute | solution.py:486
  69.9 2.3 %collective-permute-start.31 = (f32[96,128]{1,0:T(8,128)S(1)}, f32[96,128]{1,0:T(8,128)S(1)}, u32[]{:S(2)}, u32[]{:S(2)}) collective-permute-start(f32[96,128]{1,0:T(8,128)S(1)} %get-tuple-element.137), channel_id=1, source_target_pairs={{0,1},{1,0},{2,3},{3,2},{4,8},{5,9},{6,10},{7,11},{8,4},{9,5},{10,... | collective-permute-start | bytes 147464 | tf_op jit(solution)/shard_map/ppermute | solution.py:487
  70.1 3.3 %collective-permute-start.29 = (f32[52,128]{1,0:T(8,128)S(1)}, f32[52,128]{1,0:T(8,128)S(1)}, u32[]{:S(2)}, u32[]{:S(2)}) collective-permute-start(f32[52,128]{1,0:T(8,128)S(1)} %add.31.own), channel_id=1, source_target_pairs={{0,3},{1,2},{2,1},{3,0},{4,7},{5,6},{6,5},{7,4},{8,11},{9,10},{10,... | collective-permute-start | bytes 79880 | tf_op jit(solution)/shard_map/ppermute | solution.py:489
